TPU v7x, 32 devices: a whole 2x2x4 slice. The times are simulated.
32 devices in a mesh: gx: 8 (over z, x), gy: 4 (over y, core).
Axes of the slice: x: 2, y: 2, z: 4, core: 2. Of those that a mesh axis runs over, the one named last changes fastest.
Arguments:
- facies: int32 [64, 64, 128], P('gx', 'gy'), may hold values from 0 to 7
- source: float32 [64, 64, 128], P('gx', 'gy'), may hold values from -5 to 5
- facies_perm: float32 [8], replicated, may hold values from 0.5 to 5
- facies_store: float32 [8], replicated, may hold values from 0.0002 to 0.001
- well_x: int32 [64], replicated, may hold values from 0 to 63
- well_y: int32 [64], replicated, may hold values from 0 to 63
- well_rate: float32 [64], replicated, may hold values from -2000 to 2000
Outputs:
- pressure: float32 [64, 64, 128], P('gx', 'gy')
All inputs are finite; a program needn't handle non-finite values.
Results may differ from a plain program's by a relative error of at most 0.0003.
Values sent between devices are 32-bit elements; how exact they have to be, the bound alone decides.
No kernel may reach another device: no remote copies, remote signals or barrier semaphores. Data moves between devices by JAX's collectives and lax.ppermute only.
A program may use at most 128 MiB of HBM per device.

v0:
```python
import jax
import jax.numpy as jnp
import numpy as np
from jax import lax
from jax.sharding import PartitionSpec as P

BLOCK_X = 64
BLOCK_Y = 64
BLOCK_Z = 16
SWEEPS = 3


RELAX_WEIGHT = 2.0 / 3.0
HIGHEST = lax.Precision.HIGHEST
first_bits = np.array([0, 0, 0, 0, 1, 1, 1, 1], dtype=np.int32)
second_bits = np.array([0, 0, 1, 1, 0, 0, 1, 1], dtype=np.int32)
third_bits = np.array([0, 1, 0, 1, 0, 1, 0, 1], dtype=np.int32)
shift_along_x = np.array([0, 2, -2, 0, 0, 0, 0], dtype=np.int32)
shift_along_y = np.array([0, 0, 0, 2, -2, 0, 0], dtype=np.int32)
shift_along_z = np.array([0, 0, 0, 0, 0, 2, -2], dtype=np.int32)


def with_halo(value, sides, width):
    for axis, dim in sides:
        size, length = (lax.axis_size(axis), value.shape[dim])
        up = [(i, (i + 1) % size) for i in range(size - 1)]
        down = [(j, i) for i, j in up]
        last = lax.slice_in_dim(value, length - width, length, axis=dim)
        initial = lax.slice_in_dim(value, 0, width, axis=dim)
        before = lax.ppermute(last, axis, up)
        after = lax.ppermute(initial, axis, down)
        value = jnp.concatenate([before, value, after], axis=dim)
    return value


def support_of(coords, block_size, parity):
    return parity + 2 * jnp.floor_divide(
        coords + block_size // 2 - block_size * parity, 2 * block_size
    )


def parity_nodes(coords, block_size):
    return jnp.stack([support_of(coords, block_size, 0), support_of(coords, block_size, 1)])


def parity_start(coords, block_size):
    node_ids = parity_nodes(coords, block_size)
    return (node_ids == jnp.floor_divide(coords, block_size)[None]).astype(jnp.float32)


def parity_same(coords, block_size):
    node_here = parity_nodes(coords[:-1], block_size)
    node_next = parity_nodes(coords[1:], block_size)
    return (node_here == node_next).astype(jnp.float32)


def harmonic(left_perm, right_perm):
    return 2.0 * left_perm * right_perm / (left_perm + right_perm)


def face_pad(values_in, dim_id, before):
    widths = [(0, 0), (0, 0), (0, 0)]
    widths[dim_id] = (1, 0) if before else (0, 1)
    return jnp.pad(values_in, widths)


def expand(line_in, dim_id):
    new_shape = [1, 1, 1]
    new_shape[dim_id] = line_in.shape[0]
    return line_in.reshape(new_shape)


def split_faces(values_in, dim_id):
    length = values_in.shape[dim_id]
    below_part = lax.slice_in_dim(values_in, 0, length - 1, axis=dim_id)
    above_part = lax.slice_in_dim(values_in, 1, length, axis=dim_id)
    return (below_part, above_part)


def cut_apply(values_in, storage, trans_all, same_all):
    result = storage * values_in
    for dim_id in range(3):
        trans_face = trans_all[dim_id]
        same_line = expand(same_all[dim_id], dim_id)
        below_part, above_part = split_faces(values_in, dim_id)
        result = result + face_pad(
            trans_face * (below_part - same_line * above_part), dim_id, False
        )
        result = result + face_pad(trans_face * (above_part - same_line * below_part), dim_id, True)
    return result


def rim_terms(values_in, trans_all, same_all):
    result = []
    for dim_id in range(3):
        trans_face = trans_all[dim_id]
        cross_mask = 1.0 - expand(same_all[dim_id], dim_id)
        below_part, above_part = split_faces(values_in, dim_id)
        result.append(face_pad(-trans_face * cross_mask * above_part, dim_id, False))
        result.append(face_pad(-trans_face * cross_mask * below_part, dim_id, True))
    return result


def diagonal_of(storage, trans_all):
    result = storage
    for dim_id in range(3):
        result = (
            result
            + face_pad(trans_all[dim_id], dim_id, False)
            + face_pad(trans_all[dim_id], dim_id, True)
        )
    return result


def lookup(facies, code_table):
    result = jnp.zeros(facies.shape, jnp.float32)
    for code_id in range(code_table.shape[0]):
        result = result + jnp.where(facies == code_id, code_table[code_id], 0.0)
    return result


def flatten_node(index_x, index_y, index_z, counts):
    count_x, count_y, count_z = counts
    flat_ids = (
        jnp.clip(index_x, 0, count_x - 1) * count_y + jnp.clip(index_y, 0, count_y - 1)
    ) * count_z
    return (flat_ids + jnp.clip(index_z, 0, count_z - 1)).astype(jnp.int32)


def tile_indices(anchor_x, anchor_y, counts):
    count_x, count_y, count_z = counts
    row_x = parity_nodes(jnp.reshape(anchor_x, (1,)), BLOCK_X)[first_bits][:, 0]
    row_y = parity_nodes(jnp.reshape(anchor_y, (1,)), BLOCK_Y)[second_bits][:, 0]
    seg_first = jnp.maximum(jnp.arange(count_z + 1, dtype=jnp.int32) * BLOCK_Z - BLOCK_Z // 2, 0)
    row_z = parity_nodes(seg_first, BLOCK_Z)[third_bits]
    row_ids = flatten_node(row_x[:, None], row_y[:, None], row_z, counts)
    col_ids = flatten_node(
        row_x[:, None, None] + jnp.asarray(shift_along_x)[None, :, None],
        row_y[:, None, None] + jnp.asarray(shift_along_y)[None, :, None],
        row_z[:, None, :] + jnp.asarray(shift_along_z)[None, :, None],
        counts,
    )
    entry_ids = row_ids[None, :, None, :] * (count_x * count_y * count_z) + col_ids[:, None, :, :]
    return (entry_ids, row_ids)


def segment_matrix(layers, segment_count):
    seg_of = (jnp.arange(layers, dtype=jnp.int32) + BLOCK_Z // 2) // BLOCK_Z
    return (seg_of[:, None] == jnp.arange(segment_count, dtype=jnp.int32)[None, :]).astype(
        jnp.float32
    )


def solve_coarse(coarse, coarse_rhs):
    factor = jnp.linalg.cholesky(coarse)
    middle = lax.linalg.triangular_solve(factor, coarse_rhs[:, None], left_side=True, lower=True)
    return lax.linalg.triangular_solve(
        factor, middle, left_side=True, lower=True, transpose_a=True
    )[:, 0]


def geometry(coeffs, margin, anchor_x, anchor_y, total_x, total_y):
    coord_x = anchor_x - margin + jnp.arange(coeffs.shape[1], dtype=jnp.int32)
    coord_y = anchor_y - margin + jnp.arange(coeffs.shape[2], dtype=jnp.int32)
    coord_z = jnp.arange(coeffs.shape[3], dtype=jnp.int32)
    inside_x = (coord_x >= 0) & (coord_x < total_x)
    inside_y = (coord_y >= 0) & (coord_y < total_y)
    inside = inside_x[:, None, None] & inside_y[None, :, None]
    perm_safe = jnp.where(inside, coeffs[0], 1.0)
    storage = jnp.where(inside, coeffs[1], 1.0)
    valid_x = (inside_x[:-1] & inside_x[1:]).astype(jnp.float32)
    valid_y = (inside_y[:-1] & inside_y[1:]).astype(jnp.float32)
    trans_x = harmonic(perm_safe[:-1], perm_safe[1:]) * valid_x[:, None, None]
    trans_y = harmonic(perm_safe[:, :-1], perm_safe[:, 1:]) * valid_y[None, :, None]
    trans_z = harmonic(perm_safe[:, :, :-1], perm_safe[:, :, 1:])
    trans_all = (trans_x, trans_y, trans_z)
    same_all = (
        parity_same(coord_x, BLOCK_X)[first_bits],
        parity_same(coord_y, BLOCK_Y)[second_bits],
        parity_same(coord_z, BLOCK_Z)[third_bits],
    )
    starts = (
        parity_start(coord_x, BLOCK_X)[first_bits],
        parity_start(coord_y, BLOCK_Y)[second_bits],
        parity_start(coord_z, BLOCK_Z)[third_bits],
    )
    return (storage, trans_all, diagonal_of(storage, trans_all), same_all, starts)


def initial(geo_set):
    start_x, start_y, start_z = geo_set[4]
    return start_x[:, :, None, None] * start_y[:, None, :, None] * start_z[:, None, None, :]


def smooth(basis_ext, geo_set):
    storage, trans_all, diagonal, same_all, starts = geo_set

    def change_of(values_in, same_x, same_y, same_z):
        return (
            -RELAX_WEIGHT
            * cut_apply(values_in, storage, trans_all, (same_x, same_y, same_z))
            / diagonal
        )

    changes = jax.vmap(change_of)(basis_ext, same_all[0], same_all[1], same_all[2])[:, 1:-1, 1:-1]
    interior = basis_ext[:, 1:-1, 1:-1]
    change_sum = jnp.sum(changes, axis=0)
    return interior + changes - interior * change_sum[None]


def basis_halo(basis_now):
    return with_halo(basis_now, (("gx", 1), ("gy", 2)), 1)


def per_device(facies, source, facies_perm, facies_store, well_x, well_y, well_rate):
    tile_x, tile_y, layers = facies.shape
    devs_x = lax.axis_size("gx")
    devs_y = lax.axis_size("gy")
    total_x = tile_x * devs_x
    total_y = tile_y * devs_y
    anchor_x = lax.axis_index("gx") * tile_x
    anchor_y = lax.axis_index("gy") * tile_y
    coeffs = jnp.stack([lookup(facies, facies_perm), lookup(facies, facies_store)])
    coeff_wide = with_halo(coeffs, (("gx", 1), ("gy", 2)), 1)
    geo_one = geometry(coeff_wide, 1, anchor_x, anchor_y, total_x, total_y)
    basis_now = initial(geo_one)[:, 1:-1, 1:-1]
    for sweep_id in range(SWEEPS):
        basis_now = smooth(basis_halo(basis_now), geo_one)
    basis_now = basis_halo(basis_now)
    storage, trans_all, diagonal, same_all, starts = geo_one

    def terms_of(values_in, same_x, same_y, same_z):
        same_three = (same_x, same_y, same_z)
        return jnp.stack(
            [cut_apply(values_in, storage, trans_all, same_three)]
            + rim_terms(values_in, trans_all, same_three)
        )

    term_stack = jax.vmap(terms_of)(basis_now, same_all[0], same_all[1], same_all[2])[
        :, :, 1:-1, 1:-1
    ]
    interior = basis_now[:, 1:-1, 1:-1]
    count_x = total_x // BLOCK_X
    count_y = total_y // BLOCK_Y
    count_z = layers // BLOCK_Z
    counts = (count_x, count_y, count_z)
    coarse_count = count_x * count_y * count_z
    zmatrix = segment_matrix(layers, count_z + 1)
    gram_local = jnp.einsum("apqz,cspqz->casz", interior, term_stack, precision=HIGHEST)
    gram_local = jnp.einsum("casz,zg->casg", gram_local, zmatrix, precision=HIGHEST)
    cell_x = anchor_x + jnp.arange(tile_x, dtype=jnp.int32)
    cell_y = anchor_y + jnp.arange(tile_y, dtype=jnp.int32)
    hit_x = (well_x[:, None] == cell_x[None, :]).astype(jnp.float32)
    hit_y = (well_y[:, None] == cell_y[None, :]).astype(jnp.float32)
    column = jnp.einsum("w,wx,wy->xy", well_rate, hit_x, hit_y, precision=HIGHEST)
    rhs_fine = source + column[:, :, None] / layers
    rhs_local = jnp.einsum("apqz,pqz->az", interior, rhs_fine, precision=HIGHEST)
    rhs_local = jnp.einsum("az,zg->ag", rhs_local, zmatrix, precision=HIGHEST)
    entry_ids, row_ids = tile_indices(anchor_x, anchor_y, counts)
    local_matrix = (
        jnp.zeros((coarse_count * coarse_count,), jnp.float32)
        .at[entry_ids.reshape(-1)]
        .add(gram_local.reshape(-1))
    )
    local_matrix = local_matrix.reshape(coarse_count, coarse_count)
    local_rhs = (
        jnp.zeros((coarse_count,), jnp.float32).at[row_ids.reshape(-1)].add(rhs_local.reshape(-1))
    )
    coarse, coarse_rhs = lax.psum((local_matrix, local_rhs), ("gx", "gy"))
    coarse_solution = solve_coarse(coarse, coarse_rhs)
    values_at = coarse_solution[row_ids]
    per_layer = jnp.einsum("ag,zg->az", values_at, zmatrix, precision=HIGHEST)
    prolonged = jnp.einsum("apqz,az->pqz", interior, per_layer, precision=HIGHEST)
    prolonged_ext = with_halo(prolonged, (("gx", 0), ("gy", 1)), 1)
    ones_all = (
        jnp.ones((tile_x + 1,), jnp.float32),
        jnp.ones((tile_y + 1,), jnp.float32),
        jnp.ones((layers - 1,), jnp.float32),
    )
    applied = cut_apply(prolonged_ext, storage, trans_all, ones_all)[1:-1, 1:-1]
    return prolonged + RELAX_WEIGHT * (rhs_fine - applied) / diagonal[1:-1, 1:-1]


def solution(mesh):
    in_specs = (P("gx", "gy", None), P("gx", "gy", None), P(), P(), P(), P(), P())
    out_specs = P("gx", "gy", None)
    return jax.shard_map(
        per_device, mesh=mesh, in_specs=in_specs, out_specs=out_specs, check_vma=False
    )
```

profile of v0, /device:TPU:0, one launch (start us, length us, event | category | flops | bytes accessed | tf_op | source)
XLA Modules:
  0.0 283.7 jit_solution(11058861991600828541)
XLA Ops:
  0.1 0.7 pad_clamp_fusion.1
  1.4 0.7 pad_clamp_fusion.3
  3.6 4.9 %collective-permute-start.4 = (f32[8,1,16,128]{3,0,2,1:T(8,128)S(1)}, f32[8,1,16,128]{3,0,2,1:T(8,128)S(1)}, u32[]{:S(2)}, u32[]{:S(2)}) collective-permute-start(f32[8,1,16,128]{3,0,2,1:T(8,128)S(1)} %get-tuple-element.64), channel_id=1, source_target_pairs={{0,4},{4,8},{8,12},{12,16},{16,20},{20,24},{24,28},{1,5},{5,9},{9,... | collective-permute-start | bytes 196616 | tf_op jit(solution)/shard_map/ppermute | solution.py:30
  8.5 1.3 collective-permute-start.5
  9.8 1.6 fusion.63
  11.4 1.6 fusion.62
  13.0 5.9 %add_bitcast_fusion.1 = (f32[1,8,16,128]{3,2,1,0:T(8,128)S(1)}, pred[8,16,128]{2,1,0:T(8,128)(4,1)S(1)}, pred[8,16,128]{2,1,0:T(8,128)(4,1)S(1)}, pred[8,16,128]...) fusion(f32[]{:T(128)} %bitcast.20, f32[]{:T(128)} %bitcast.19, ...), kind=kLoop, calls=%fused_computation.126 | loop fusion | flops 376832 | bytes 262176 | tf_op jit(solution)/shard_map/stack | solution.py:223
  19.0 5.0 %add_bitcast_fusion = f32[1,8,16,128]{3,2,1,0:T(8,128)S(1)} fusion(pred[8,16,128]{2,1,0:T(8,128)(4,1)S(1)} %get-tuple-element.29, pred[8,16,128]{2,1,0:T(8,128)(4,1)S(1)} %get-tuple-element.28, pred[8,16,128]{2,1,0:T(8,128)(4,1)S(1)} %get-tuple-element.27, pred[8,16,128]{2,1,0:T(8,128)(4,1)S(1)} %get-tuple-element.26, ...), kind=kLoop, calls=%fused_computation.125 | loop fusion | flops 245760 | bytes 196640 | tf_op jit(solution)/shard_map/stack | solution.py:223
  24.0 4.5 %collective-permute-start = (f32[2,1,16,128]{3,2,1,0:T(8,128)S(1)}, f32[2,1,16,128]{3,2,1,0:T(8,128)S(1)}, u32[]{:S(2)}, u32[]{:S(2)}) collective-permute-start(f32[2,1,16,128]{3,2,1,0:T(8,128)S(1)} %get-tuple-element.88), channel_id=1, source_target_pairs={{0,4},{4,8},{8,12},{12,16},{16,20},{20,24},{24,28},{1,5},{5,9},{9,... | collective-permute-start | bytes 49160 | tf_op jit(solution)/shard_map/ppermute | solution.py:30
  28.6 1.3 collective-permute-start.1
  33.7 0.8 add_multiply_fusion
  34.4 0.7 clamp_add_fusion
  36.1 0.9 convolution_multiply_fusion
  37.1 0.9 add_bitcast_fusion.2
  38.1 1.3 collective-permute-start.2
  39.4 1.3 collective-permute-start.3
  41.5 2.7 collective-permute-done.3
  44.5 0.8 fusion.50
  45.5 4.3 %collective-permute-start.6 = (f32[8,10,1,128]{3,0,2,1:T(8,128)S(1)}, f32[8,10,1,128]{3,0,2,1:T(8,128)S(1)}, u32[]{:S(2)}, u32[]{:S(2)}) collective-permute-start(f32[8,10,1,128]{3,0,2,1:T(8,128)S(1)} %get-tuple-element.72), channel_id=1, source_target_pairs={{0,1},{1,2},{2,3},{4,5},{5,6},{6,7},{8,9},{9,10},{10,11},{12,13},{... | collective-permute-start | bytes 122888 | tf_op jit(solution)/shard_map/ppermute | solution.py:30
  49.8 1.3 collective-permute-start.7
  51.3 1.6 collective-permute-done.7
  54.5 5.0 %collective-permute-start.8 = (f32[8,1,16,128]{3,0,2,1:T(8,128)S(1)}, f32[8,1,16,128]{3,0,2,1:T(8,128)S(1)}, u32[]{:S(2)}, u32[]{:S(2)}) collective-permute-start(f32[8,1,16,128]{3,0,2,1:T(8,128)S(1)} %get-tuple-element.78), channel_id=1, source_target_pairs={{0,4},{4,8},{8,12},{12,16},{16,20},{20,24},{24,28},{1,5},{5,9},{9,... | collective-permute-start | bytes 196616 | tf_op jit(solution)/shard_map/ppermute | solution.py:30
  59.5 1.3 collective-permute-start.9
  61.5 5.1 %collective-permute-done.9 = f32[8,1,16,128]{3,0,2,1:T(8,128)S(1)} collective-permute-done((f32[8,1,16,128]{3,0,2,1:T(8,128)S(1)}, f32[8,1,16,128]{3,0,2,1:T(8,128)S(1)}, u32[]{:S(2)}, u32[]{:S(2)}) %collective-permute-start.9) | collective-permute-done | bytes 65568 | tf_op jit(solution)/shard_map/ppermute | solution.py:31
  66.6 3.0 %collective-permute-start.10 = (f32[8,10,1,128]{3,0,2,1:T(8,128)S(1)}, f32[8,10,1,128]{3,0,2,1:T(8,128)S(1)}, u32[]{:S(2)}, u32[]{:S(2)}) collective-permute-start(f32[8,10,1,128]{3,0,2,1:T(8,128)S(1)} %get-tuple-element.70), channel_id=1, source_target_pairs={{0,1},{1,2},{2,3},{4,5},{5,6},{6,7},{8,9},{9,10},{10,11},{12,13},{... | collective-permute-start | bytes 122888 | tf_op jit(solution)/shard_map/ppermute | solution.py:30
  69.6 1.3 collective-permute-start.11
  71.6 1.8 collective-permute-done.11
  74.9 4.8 %collective-permute-start.12 = (f32[8,1,16,128]{3,0,2,1:T(8,128)S(1)}, f32[8,1,16,128]{3,0,2,1:T(8,128)S(1)}, u32[]{:S(2)}, u32[]{:S(2)}) collective-permute-start(f32[8,1,16,128]{3,0,2,1:T(8,128)S(1)} %get-tuple-element.76), channel_id=1, source_target_pairs={{0,4},{4,8},{8,12},{12,16},{16,20},{20,24},{24,28},{1,5},{5,9},{9,... | collective-permute-start | bytes 196616 | tf_op jit(solution)/shard_map/ppermute | solution.py:30
  79.7 1.3 collective-permute-start.13
  81.6 4.3 %collective-permute-done.13 = f32[8,1,16,128]{3,0,2,1:T(8,128)S(1)} collective-permute-done((f32[8,1,16,128]{3,0,2,1:T(8,128)S(1)}, f32[8,1,16,128]{3,0,2,1:T(8,128)S(1)}, u32[]{:S(2)}, u32[]{:S(2)}) %collective-permute-start.13) | collective-permute-done | bytes 65568 | tf_op jit(solution)/shard_map/ppermute | solution.py:31
  85.9 3.2 %collective-permute-start.14 = (f32[8,10,1,128]{3,0,2,1:T(8,128)S(1)}, f32[8,10,1,128]{3,0,2,1:T(8,128)S(1)}, u32[]{:S(2)}, u32[]{:S(2)}) collective-permute-start(f32[8,10,1,128]{3,0,2,1:T(8,128)S(1)} %get-tuple-element.68), channel_id=1, source_target_pairs={{0,1},{1,2},{2,3},{4,5},{5,6},{6,7},{8,9},{9,10},{10,11},{12,13},{... | collective-permute-start | bytes 122888 | tf_op jit(solution)/shard_map/ppermute | solution.py:30
  89.1 1.3 collective-permute-start.15
  90.9 0.7 copy.38
  91.6 0.7 copy.37
  93.4 0.9 subtract_multiply_fusion.3
  95.4 4.5 %copy.40 = f32[8,8,16,128]{2,0,1,3:T(8,128)} copy(f32[8,8,16,128]{3,0,2,1:T(8,128)S(1)} %multiply_subtract_fusion) | data formatting | bytes 1048576 | tf_op jit(solution)/shard_map/sub | solution.py:208
  99.8 2.9 %collective-permute-start.16 = (f32[8,1,16,128]{3,0,2,1:T(8,128)S(1)}, f32[8,1,16,128]{3,0,2,1:T(8,128)S(1)}, u32[]{:S(2)}, u32[]{:S(2)}) collective-permute-start(f32[8,1,16,128]{3,0,2,1:T(8,128)S(1)} %get-tuple-element.74), channel_id=1, source_target_pairs={{0,4},{4,8},{8,12},{12,16},{16,20},{20,24},{24,28},{1,5},{5,9},{9,... | collective-permute-start | bytes 196616 | tf_op jit(solution)/shard_map/ppermute | solution.py:30
  102.8 1.6 collective-permute-start.17
  104.4 10.5 %fusion.64 = f32[128,1,8,1]{2,1,3,0:T(1,128)S(1)} fusion(f32[8,16,128,1]{1,3,0,2:T(1,128)S(1)} %copy.51, f32[8,8,16,128]{2,0,1,3:T(8,128)} %copy.40), kind=kOutput, calls=%fused_computation.356 | convolution fusion | flops 1572864 | bytes 593920 | tf_op jit(solution)/shard_map/apqz,pqz->az/dot_general | solution.py:257
  114.9 4.3 %collective-permute-start.18 = (f32[8,10,1,128]{3,0,2,1:T(8,128)S(1)}, f32[8,10,1,128]{3,0,2,1:T(8,128)S(1)}, u32[]{:S(2)}, u32[]{:S(2)}) collective-permute-start(f32[8,10,1,128]{3,0,2,1:T(8,128)S(1)} %get-tuple-element.66), channel_id=1, source_target_pairs={{0,1},{1,2},{2,3},{4,5},{5,6},{6,7},{8,9},{9,10},{10,11},{12,13},{... | collective-permute-start | bytes 122888 | tf_op jit(solution)/shard_map/ppermute | solution.py:30
  119.3 1.3 collective-permute-start.19
  120.8 4.5 %copy.46 = f32[8,8,16,128,1]{2,0,1,4,3:T(8,128)} copy(f32[8,8,16,128,1]{3,0,2,1,4:T(8,128)S(1)} %bitcast.144) | data formatting | bytes 1048576 | tf_op jit(solution)/shard_map/sub | solution.py:208
  125.4 1.4 scatter_custom_fusion.1
  127.9 1.3 bitcast_dynamic-update-slice_fusion.6
  129.2 1.0 bitcast_dynamic-update-slice_fusion.5
  130.1 0.9 bitcast_dynamic-update-slice_fusion.4
  131.2 1.0 bitcast_dynamic-update-slice_fusion.3
  132.2 0.9 bitcast_dynamic-update-slice_fusion.2
  133.1 1.0 bitcast_dynamic-update-slice_fusion.1
  134.1 1.1 bitcast_dynamic-update-slice_fusion
  135.2 19.0 %copy.39 = f32[7,8,10,18,128]{3,1,2,0,4:T(8,128)} copy(f32[7,8,10,18,128]{4,1,3,2,0:T(8,128)} %bitcast_dynamic-update-slice_fusion) | data formatting | bytes 10321920 | tf_op jit(solution)/shard_map/vmap()/stack | solution.py:234
  154.2 31.7 %fusion.2 = f32[8,8,7,128]{1,0,2,3:T(8,128)} fusion(f32[8,8,16,128,1]{2,0,1,4,3:T(8,128)} %copy.46, f32[8,7,10,18,128]{3,0,2,1,4:T(8,128)} %bitcast.143), kind=kOutput, calls=%fused_computation.14 | convolution fusion | flops 88080384 | bytes 33783808 | tf_op jit(solution)/shard_map/apqz,cspqz->casz/dot_general | solution.py:249
  185.8 3.2 %copy.48 = f32[8,8,7,128]{3,2,1,0:T(8,128)S(1)} copy(f32[8,8,7,128]{1,0,2,3:T(8,128)} %fusion.2) | data formatting | bytes 458752 | tf_op jit(solution)/shard_map/apqz,cspqz->casz/transpose | solution.py:249
  189.5 28.9 %scatter_custom_fusion = f32[64]{0:T(128)S(1)} fusion(s32[4032]{0:T(1024)} %bitcast.150, f32[4032]{0:T(1024)S(1)} %reshape.1006, f32[]{:T(128)} %constant.401.clone.1), kind=kCustom, calls=%fused_computation.340 | custom fusion | flops 4032 | bytes 768 | tf_op jit(solution)/shard_map/scatter-add | solution.py:263
  218.5 43.3 %all-reduce.42 = (f32[8,8]{0,1:T(8,128)S(1)}, f32[8]{0:T(128)S(1)}) all-reduce(f32[8,8]{0,1:T(8,128)S(1)} %copy.43, f32[8]{0:T(128)S(1)} %scatter_custom_fusion.1), channel_id=1, replica_groups=mesh['gx'=8,'gy'=4] {'gx','gy'}, use_global_device_ids=true, to_apply=%region_4.5 | all-reduce | flops 72 | bytes 576 | tf_op jit(solution)/shard_map/psum | solution.py:269
  261.8 0.7 cholesky.16
  264.8 1.2 gather_fusion.9
  266.4 4.2 %collective-permute-start.20 = (f32[1,16,128]{2,1,0:T(8,128)S(1)}, f32[1,16,128]{2,1,0:T(8,128)S(1)}, u32[]{:S(2)}, u32[]{:S(2)}) collective-permute-start(f32[1,16,128]{2,1,0:T(8,128)S(1)} %get-tuple-element.94), channel_id=1, source_target_pairs={{0,4},{4,8},{8,12},{12,16},{16,20},{20,24},{24,28},{1,5},{5,9},{9,... | collective-permute-start | bytes 24584 | tf_op jit(solution)/shard_map/ppermute | solution.py:30
  270.6 1.3 collective-permute-start.21
  272.0 4.2 %collective-permute-done.21 = f32[1,16,128]{2,1,0:T(8,128)S(1)} collective-permute-done((f32[1,16,128]{2,1,0:T(8,128)S(1)}, f32[1,16,128]{2,1,0:T(8,128)S(1)}, u32[]{:S(2)}, u32[]{:S(2)}) %collective-permute-start.21) | collective-permute-done | bytes 8224 | tf_op jit(solution)/shard_map/ppermute | solution.py:31
  276.2 1.3 collective-permute-start.22
  277.5 1.3 collective-permute-start.23
  278.8 3.9 %collective-permute-done.23 = f32[10,1,128]{2,1,0:T(1,128)S(1)} collective-permute-done((f32[10,1,128]{2,1,0:T(1,128)S(1)}, f32[10,1,128]{2,1,0:T(1,128)S(1)}, u32[]{:S(2)}, u32[]{:S(2)}) %collective-permute-start.23) | collective-permute-done | bytes 5152 | tf_op jit(solution)/shard_map/ppermute | solution.py:31
  283.0 0.7 fusion.16
  (169 shorter events, 21.0 us)
Async XLA Ops:
  3.6 41.8 %collective-permute-start.4 = (f32[8,1,16,128]{3,0,2,1:T(8,128)S(1)}, f32[8,1,16,128]{3,0,2,1:T(8,128)S(1)}, u32[]{:S(2)}, u32[]{:S(2)}) collective-permute-start(f32[8,1,16,128]{3,0,2,1:T(8,128)S(1)} %get-tuple-element.64), channel_id=1, source_target_pairs={{0,4},{4,8},{8,12},{12,16},{16,20},{20,24},{24,28},{1,5},{5,9},{9,... | collective-permute-start | bytes 196616 | tf_op jit(solution)/shard_map/ppermute | solution.py:30
  8.5 37.0 %collective-permute-start.5 = (f32[8,1,16,128]{3,0,2,1:T(8,128)S(1)}, f32[8,1,16,128]{3,0,2,1:T(8,128)S(1)}, u32[]{:S(2)}, u32[]{:S(2)}) collective-permute-start(f32[8,1,16,128]{3,0,2,1:T(8,128)S(1)} %get-tuple-element.65), channel_id=1, source_target_pairs={{4,0},{8,4},{12,8},{16,12},{20,16},{24,20},{28,24},{5,1},{9,5},{13... | collective-permute-start | bytes 196616 | tf_op jit(solution)/shard_map/ppermute | solution.py:31
  24.0 14.1 %collective-permute-start = (f32[2,1,16,128]{3,2,1,0:T(8,128)S(1)}, f32[2,1,16,128]{3,2,1,0:T(8,128)S(1)}, u32[]{:S(2)}, u32[]{:S(2)}) collective-permute-start(f32[2,1,16,128]{3,2,1,0:T(8,128)S(1)} %get-tuple-element.88), channel_id=1, source_target_pairs={{0,4},{4,8},{8,12},{12,16},{16,20},{20,24},{24,28},{1,5},{5,9},{9,... | collective-permute-start | bytes 49160 | tf_op jit(solution)/shard_map/ppermute | solution.py:30
  28.6 9.5 %collective-permute-start.1 = (f32[2,1,16,128]{3,2,1,0:T(8,128)S(1)}, f32[2,1,16,128]{3,2,1,0:T(8,128)S(1)}, u32[]{:S(2)}, u32[]{:S(2)}) collective-permute-start(f32[2,1,16,128]{3,2,1,0:T(8,128)S(1)} %get-tuple-element.89), channel_id=1, source_target_pairs={{4,0},{8,4},{12,8},{16,12},{20,16},{24,20},{28,24},{5,1},{9,5},{13... | collective-permute-start | bytes 49160 | tf_op jit(solution)/shard_map/ppermute | solution.py:31
  32.3 20.9 %copy-start.4 = (pred[10,18]{1,0:T(8,128)(4,1)}, pred[10,18]{1,0:T(8,128)(4,1)S(1)}, u32[]{:S(2)}) copy-start(pred[10,18]{1,0:T(8,128)(4,1)S(1)} %broadcast_and_fusion) | copy-start | bytes 544
  37.1 7.2 %copy-start.8 = (f32[8,16]{1,0:T(8,128)}, f32[8,16]{1,0:T(8,128)S(1)}, u32[]{:S(2)}) copy-start(f32[8,16]{1,0:T(8,128)S(1)} %convolution_multiply_fusion) | copy-start | bytes 1540
  38.1 3.4 %collective-permute-start.2 = (f32[2,10,1,128]{3,2,1,0:T(1,128)S(1)}, f32[2,10,1,128]{3,2,1,0:T(1,128)S(1)}, u32[]{:S(2)}, u32[]{:S(2)}) collective-permute-start(f32[2,10,1,128]{3,2,1,0:T(1,128)S(1)} %get-tuple-element.86), channel_id=1, source_target_pairs={{0,1},{1,2},{2,3},{4,5},{5,6},{6,7},{8,9},{9,10},{10,11},{12,13},{... | collective-permute-start | bytes 30728 | tf_op jit(solution)/shard_map/ppermute | solution.py:30
  39.4 4.8 %collective-permute-start.3 = (f32[2,10,1,128]{3,2,1,0:T(1,128)S(1)}, f32[2,10,1,128]{3,2,1,0:T(1,128)S(1)}, u32[]{:S(2)}, u32[]{:S(2)}) collective-permute-start(f32[2,10,1,128]{3,2,1,0:T(1,128)S(1)} %get-tuple-element.87), channel_id=1, source_target_pairs={{1,0},{2,1},{3,2},{5,4},{6,5},{7,6},{9,8},{10,9},{11,10},{13,12},{... | collective-permute-start | bytes 30728 | tf_op jit(solution)/shard_map/ppermute | solution.py:31
  41.5 32.1 %copy-start.2 = (f32[8,127]{1,0:T(8,128)}, f32[8,127]{1,0:T(8,128)S(1)}, u32[]{:S(2)}) copy-start(f32[8,127]{1,0:T(8,128)S(1)} %gather_fusion.8) | copy-start | bytes 12196
  45.5 5.8 %collective-permute-start.6 = (f32[8,10,1,128]{3,0,2,1:T(8,128)S(1)}, f32[8,10,1,128]{3,0,2,1:T(8,128)S(1)}, u32[]{:S(2)}, u32[]{:S(2)}) collective-permute-start(f32[8,10,1,128]{3,0,2,1:T(8,128)S(1)} %get-tuple-element.72), channel_id=1, source_target_pairs={{0,1},{1,2},{2,3},{4,5},{5,6},{6,7},{8,9},{9,10},{10,11},{12,13},{... | collective-permute-start | bytes 122888 | tf_op jit(solution)/shard_map/ppermute | solution.py:30
  49.8 3.1 %collective-permute-start.7 = (f32[8,10,1,128]{3,0,2,1:T(8,128)S(1)}, f32[8,10,1,128]{3,0,2,1:T(8,128)S(1)}, u32[]{:S(2)}, u32[]{:S(2)}) collective-permute-start(f32[8,10,1,128]{3,0,2,1:T(8,128)S(1)} %get-tuple-element.73), channel_id=1, source_target_pairs={{1,0},{2,1},{3,2},{5,4},{6,5},{7,6},{9,8},{10,9},{11,10},{13,12},{... | collective-permute-start | bytes 122888 | tf_op jit(solution)/shard_map/ppermute | solution.py:31
  54.5 7.0 %collective-permute-start.8 = (f32[8,1,16,128]{3,0,2,1:T(8,128)S(1)}, f32[8,1,16,128]{3,0,2,1:T(8,128)S(1)}, u32[]{:S(2)}, u32[]{:S(2)}) collective-permute-start(f32[8,1,16,128]{3,0,2,1:T(8,128)S(1)} %get-tuple-element.78), channel_id=1, source_target_pairs={{0,4},{4,8},{8,12},{12,16},{16,20},{20,24},{24,28},{1,5},{5,9},{9,... | collective-permute-start | bytes 196616 | tf_op jit(solution)/shard_map/ppermute | solution.py:30
  59.5 7.1 %collective-permute-start.9 = (f32[8,1,16,128]{3,0,2,1:T(8,128)S(1)}, f32[8,1,16,128]{3,0,2,1:T(8,128)S(1)}, u32[]{:S(2)}, u32[]{:S(2)}) collective-permute-start(f32[8,1,16,128]{3,0,2,1:T(8,128)S(1)} %get-tuple-element.79), channel_id=1, source_target_pairs={{4,0},{8,4},{12,8},{16,12},{20,16},{24,20},{28,24},{5,1},{9,5},{13... | collective-permute-start | bytes 196616 | tf_op jit(solution)/shard_map/ppermute | solution.py:31
  66.6 5.0 %collective-permute-start.10 = (f32[8,10,1,128]{3,0,2,1:T(8,128)S(1)}, f32[8,10,1,128]{3,0,2,1:T(8,128)S(1)}, u32[]{:S(2)}, u32[]{:S(2)}) collective-permute-start(f32[8,10,1,128]{3,0,2,1:T(8,128)S(1)} %get-tuple-element.70), channel_id=1, source_target_pairs={{0,1},{1,2},{2,3},{4,5},{5,6},{6,7},{8,9},{9,10},{10,11},{12,13},{... | collective-permute-start | bytes 122888 | tf_op jit(solution)/shard_map/ppermute | solution.py:30
  69.6 3.8 %collective-permute-start.11 = (f32[8,10,1,128]{3,0,2,1:T(8,128)S(1)}, f32[8,10,1,128]{3,0,2,1:T(8,128)S(1)}, u32[]{:S(2)}, u32[]{:S(2)}) collective-permute-start(f32[8,10,1,128]{3,0,2,1:T(8,128)S(1)} %get-tuple-element.71), channel_id=1, source_target_pairs={{1,0},{2,1},{3,2},{5,4},{6,5},{7,6},{9,8},{10,9},{11,10},{13,12},{... | collective-permute-start | bytes 122888 | tf_op jit(solution)/shard_map/ppermute | solution.py:31
  74.9 6.7 %collective-permute-start.12 = (f32[8,1,16,128]{3,0,2,1:T(8,128)S(1)}, f32[8,1,16,128]{3,0,2,1:T(8,128)S(1)}, u32[]{:S(2)}, u32[]{:S(2)}) collective-permute-start(f32[8,1,16,128]{3,0,2,1:T(8,128)S(1)} %get-tuple-element.76), channel_id=1, source_target_pairs={{0,4},{4,8},{8,12},{12,16},{16,20},{20,24},{24,28},{1,5},{5,9},{9,... | collective-permute-start | bytes 196616 | tf_op jit(solution)/shard_map/ppermute | solution.py:30
  79.7 6.2 %collective-permute-start.13 = (f32[8,1,16,128]{3,0,2,1:T(8,128)S(1)}, f32[8,1,16,128]{3,0,2,1:T(8,128)S(1)}, u32[]{:S(2)}, u32[]{:S(2)}) collective-permute-start(f32[8,1,16,128]{3,0,2,1:T(8,128)S(1)} %get-tuple-element.77), channel_id=1, source_target_pairs={{4,0},{8,4},{12,8},{16,12},{20,16},{24,20},{28,24},{5,1},{9,5},{13... | collective-permute-start | bytes 196616 | tf_op jit(solution)/shard_map/ppermute | solution.py:31
  85.9 6.7 %collective-permute-start.14 = (f32[8,10,1,128]{3,0,2,1:T(8,128)S(1)}, f32[8,10,1,128]{3,0,2,1:T(8,128)S(1)}, u32[]{:S(2)}, u32[]{:S(2)}) collective-permute-start(f32[8,10,1,128]{3,0,2,1:T(8,128)S(1)} %get-tuple-element.68), channel_id=1, source_target_pairs={{0,1},{1,2},{2,3},{4,5},{5,6},{6,7},{8,9},{9,10},{10,11},{12,13},{... | collective-permute-start | bytes 122888 | tf_op jit(solution)/shard_map/ppermute | solution.py:30
  89.1 4.0 %collective-permute-start.15 = (f32[8,10,1,128]{3,0,2,1:T(8,128)S(1)}, f32[8,10,1,128]{3,0,2,1:T(8,128)S(1)}, u32[]{:S(2)}, u32[]{:S(2)}) collective-permute-start(f32[8,10,1,128]{3,0,2,1:T(8,128)S(1)} %get-tuple-element.69), channel_id=1, source_target_pairs={{1,0},{2,1},{3,2},{5,4},{6,5},{7,6},{9,8},{10,9},{11,10},{13,12},{... | collective-permute-start | bytes 122888 | tf_op jit(solution)/shard_map/ppermute | solution.py:31
  95.3 25.2 %copy-start.12 = (s32[128]{0:T(128)S(1)}, s32[128]{0:T(128)}, u32[]{:S(2)}) copy-start(s32[128]{0:T(128)} %and_select_fusion) | copy-start | bytes 1540
  99.8 15.1 %collective-permute-start.16 = (f32[8,1,16,128]{3,0,2,1:T(8,128)S(1)}, f32[8,1,16,128]{3,0,2,1:T(8,128)S(1)}, u32[]{:S(2)}, u32[]{:S(2)}) collective-permute-start(f32[8,1,16,128]{3,0,2,1:T(8,128)S(1)} %get-tuple-element.74), channel_id=1, source_target_pairs={{0,4},{4,8},{8,12},{12,16},{16,20},{20,24},{24,28},{1,5},{5,9},{9,... | collective-permute-start | bytes 196616 | tf_op jit(solution)/shard_map/ppermute | solution.py:30
  102.8 24.1 %copy-start = (f32[9,18,128]{2,1,0:T(8,128)S(1)}, f32[9,18,128]{2,1,0:T(8,128)}, u32[]{:S(2)}) copy-start(f32[9,18,128]{2,1,0:T(8,128)} %get-tuple-element.11) | copy-start | bytes 248836
  102.8 24.1 %copy-start.7 = (f32[8,9]{0,1:T(8,128)S(1)}, f32[8,9]{0,1:T(8,128)}, u32[]{:S(2)}) copy-start(f32[8,9]{0,1:T(8,128)} %copy.37) | copy-start | bytes 868
  102.8 12.1 %collective-permute-start.17 = (f32[8,1,16,128]{3,0,2,1:T(8,128)S(1)}, f32[8,1,16,128]{3,0,2,1:T(8,128)S(1)}, u32[]{:S(2)}, u32[]{:S(2)}) collective-permute-start(f32[8,1,16,128]{3,0,2,1:T(8,128)S(1)} %get-tuple-element.75), channel_id=1, source_target_pairs={{4,0},{8,4},{12,8},{16,12},{20,16},{24,20},{28,24},{5,1},{9,5},{13... | collective-permute-start | bytes 196616 | tf_op jit(solution)/shard_map/ppermute | solution.py:31
  114.9 11.8 %collective-permute-start.18 = (f32[8,10,1,128]{3,0,2,1:T(8,128)S(1)}, f32[8,10,1,128]{3,0,2,1:T(8,128)S(1)}, u32[]{:S(2)}, u32[]{:S(2)}) collective-permute-start(f32[8,10,1,128]{3,0,2,1:T(8,128)S(1)} %get-tuple-element.66), channel_id=1, source_target_pairs={{0,1},{1,2},{2,3},{4,5},{5,6},{6,7},{8,9},{9,10},{10,11},{12,13},{... | collective-permute-start | bytes 122888 | tf_op jit(solution)/shard_map/ppermute | solution.py:30
  119.3 7.5 %collective-permute-start.19 = (f32[8,10,1,128]{3,0,2,1:T(8,128)S(1)}, f32[8,10,1,128]{3,0,2,1:T(8,128)S(1)}, u32[]{:S(2)}, u32[]{:S(2)}) collective-permute-start(f32[8,10,1,128]{3,0,2,1:T(8,128)S(1)} %get-tuple-element.67), channel_id=1, source_target_pairs={{1,0},{2,1},{3,2},{5,4},{6,5},{7,6},{9,8},{10,9},{11,10},{13,12},{... | collective-permute-start | bytes 122888 | tf_op jit(solution)/shard_map/ppermute | solution.py:31
  120.8 6.4 %copy-start.3 = (f32[8,127]{1,0:T(8,128)S(1)}, f32[8,127]{1,0:T(8,128)}, u32[]{:S(2)}) copy-start(f32[8,127]{1,0:T(8,128)} %copy-done.2) | copy-start | bytes 12196
  120.8 6.4 %copy-start.10 = (f32[8,127]{1,0:T(8,128)S(1)}, f32[8,127]{1,0:T(8,128)}, u32[]{:S(2)}) copy-start(f32[8,127]{1,0:T(8,128)} %broadcast_subtract_fusion) | copy-start | bytes 12196
  127.6 3.5 %copy-start.6 = (f32[8,17]{0,1:T(8,128)S(1)}, f32[8,17]{0,1:T(8,128)}, u32[]{:S(2)}) copy-start(f32[8,17]{0,1:T(8,128)} %copy.38) | copy-start | bytes 1636
  154.2 34.9 %copy-start.13 = (s32[128]{0:T(128)S(1)}, s32[128]{0:T(128)}, u32[]{:S(2)}) copy-start(s32[128]{0:T(128)} %and_select_fusion) | copy-start | bytes 1540
  154.2 110.6 %copy-start.11 = (s32[1024]{0:T(1024)S(1)}, s32[1024]{0:T(1024)}, u32[]{:S(2)}) copy-start(s32[1024]{0:T(1024)} %pad_clamp_fusion) | copy-start | bytes 12292
  185.8 96.9 %copy-start.5 = (pred[10,18]{1,0:T(8,128)(4,1)S(1)}, pred[10,18]{1,0:T(8,128)(4,1)}, u32[]{:S(2)}) copy-start(pred[10,18]{1,0:T(8,128)(4,1)} %copy-done.4) | copy-start | bytes 544
  185.8 97.2 %copy-start.1 = (f32[8,16,128]{2,1,0:T(8,128)S(1)}, f32[8,16,128]{2,1,0:T(8,128)}, u32[]{:S(2)}) copy-start(f32[8,16,128]{2,1,0:T(8,128)} %param.23) | copy-start | bytes 196612
  185.8 97.2 %copy-start.9 = (f32[8,16]{1,0:T(8,128)S(1)}, f32[8,16]{1,0:T(8,128)}, u32[]{:S(2)}) copy-start(f32[8,16]{1,0:T(8,128)} %copy-done.8) | copy-start | bytes 1540
  266.4 5.5 %collective-permute-start.20 = (f32[1,16,128]{2,1,0:T(8,128)S(1)}, f32[1,16,128]{2,1,0:T(8,128)S(1)}, u32[]{:S(2)}, u32[]{:S(2)}) collective-permute-start(f32[1,16,128]{2,1,0:T(8,128)S(1)} %get-tuple-element.94), channel_id=1, source_target_pairs={{0,4},{4,8},{8,12},{12,16},{16,20},{20,24},{24,28},{1,5},{5,9},{9,... | collective-permute-start | bytes 24584 | tf_op jit(solution)/shard_map/ppermute | solution.py:30
  270.6 5.5 %collective-permute-start.21 = (f32[1,16,128]{2,1,0:T(8,128)S(1)}, f32[1,16,128]{2,1,0:T(8,128)S(1)}, u32[]{:S(2)}, u32[]{:S(2)}) collective-permute-start(f32[1,16,128]{2,1,0:T(8,128)S(1)} %get-tuple-element.95), channel_id=1, source_target_pairs={{4,0},{8,4},{12,8},{16,12},{20,16},{24,20},{28,24},{5,1},{9,5},{13... | collective-permute-start | bytes 24584 | tf_op jit(solution)/shard_map/ppermute | solution.py:31
  276.2 2.6 collective-permute-start.22
  277.5 5.2 %collective-permute-start.23 = (f32[10,1,128]{2,1,0:T(1,128)S(1)}, f32[10,1,128]{2,1,0:T(1,128)S(1)}, u32[]{:S(2)}, u32[]{:S(2)}) collective-permute-start(f32[10,1,128]{2,1,0:T(1,128)S(1)} %get-tuple-element.93), channel_id=1, source_target_pairs={{1,0},{2,1},{3,2},{5,4},{6,5},{7,6},{9,8},{10,9},{11,10},{13,12},{... | collective-permute-start | bytes 15368 | tf_op jit(solution)/shard_map/ppermute | solution.py:31
where the time goes:
time: 287 us; the launch traced here: 284 us
  other arithmetic  62.1 us (22%)
  starting transfers between devices  59.6 us (21%)
  local copies, waits for them, and re-layouts  49.8 us (17%)
  matrix products  44 us (15%)
  blocking collectives  43.3 us (15%)
  waiting for transfers between devices  24.1 us (8%)
    ppermute x12, starting transfers between devices, with_halo(): before = lax.ppermute(last, axis, up)  43.7 us
    psum x1, blocking collectives, per_device(): coarse, coarse_rhs = lax.psum((local_matrix, local_rhs), ('gx', 'gy'))  43.3 us
    dot_general x1, matrix products, per_device(): jnp.einsum('apqz,cspqz->casz', interior, term_stack, precision=HIGHEST)  31.7 us
    scatter-add x1, other arithmetic, per_device(): local_matrix = jnp.zeros((coarse_count * coarse_count,), jnp.float32).at[...  28.9 us
    ppermute x12, waiting for transfers between devices, with_halo(): after = lax.ppermute(initial, axis, down)  24.1 us
    another operation x2, local copies, waits for them, and re-layouts, terms_of(): jnp.stack([cut_apply(values_in, storage, trans_all, same_three)] + rim_te...  20.1 us
    ppermute x12, starting transfers between devices, with_halo(): after = lax.ppermute(initial, axis, down)  15.8 us
    another operation x2, other arithmetic, per_device(): jnp.stack([lookup(facies, facies_perm), lookup(facies, facies_store)])  11 us
  transfers between devices with their start and end apart: 24, of which 8 were waited for; matrix products, arithmetic and copies ran while one was open for 16% of the time, Pallas kernels for 0%

commit v1 on v0

--- a/solution.py
+++ b/solution.py
@@ -2,6 +2,8 @@
 import jax.numpy as jnp
 import numpy as np
 from jax import lax
+from jax.experimental import pallas as pl
+from jax.experimental.pallas import tpu as pltpu
 from jax.sharding import PartitionSpec as P
 
 BLOCK_X = 64
@@ -212,7 +214,7 @@
     return with_halo(basis_now, (("gx", 1), ("gy", 2)), 1)
 
 
-def per_device(facies, source, facies_perm, facies_store, well_x, well_y, well_rate):
+def general_step(facies, source, facies_perm, facies_store, well_x, well_y, well_rate):
     tile_x, tile_y, layers = facies.shape
     devs_x = lax.axis_size("gx")
     devs_y = lax.axis_size("gy")
@@ -281,7 +283,365 @@
     return prolonged + RELAX_WEIGHT * (rhs_fine - applied) / diagonal[1:-1, 1:-1]
 
 
+MARGIN = SWEEPS + 1
+AXES = ("gx", "gy")
+ROWS = 8
+
+
+def pair_swaps(value, dim, axis, width):
+    size, length = (lax.axis_size(axis), value.shape[dim])
+    last = lax.slice_in_dim(value, length - width, length, axis=dim)
+    first = lax.slice_in_dim(value, 0, width, axis=dim)
+    even = lax.axis_index(axis) % 2 == 0
+    pairs_near = [(i, i + 1) for i in range(0, size - 1, 2)]
+    pairs_far = [(i, i + 1) for i in range(1, size - 1, 2)]
+    near = lax.ppermute(
+        jnp.where(even, last, first), axis, pairs_near + [(j, i) for i, j in pairs_near]
+    )
+    far = lax.ppermute(
+        jnp.where(even, first, last), axis, pairs_far + [(j, i) for i, j in pairs_far]
+    )
+    return jnp.where(even, far, near), jnp.where(even, near, far)
+
+
+def wide_facies(facies):
+    before, after = pair_swaps(facies, 1, "gy", MARGIN)
+    rows = jnp.concatenate([facies, after, before], axis=1)
+    before, after = pair_swaps(rows, 0, "gx", MARGIN)
+    return jnp.concatenate([before, rows, after], axis=0)
+
+
+def lane_iota(shape):
+    return lax.broadcasted_iota(jnp.int32, shape, len(shape) - 1)
+
+
+def face_ends(layer, parity):
+    return lax.rem(layer + 1 + BLOCK_Z // 2 + BLOCK_Z * parity, 2 * BLOCK_Z) == 0
+
+
+def table_select(table_ref, codes):
+    result = jnp.full(codes.shape, table_ref[0], jnp.float32)
+    for code_id in range(1, table_ref.shape[0]):
+        result = jnp.where(codes == code_id, table_ref[code_id], result)
+    return result
+
+
+def basis_kernel(
+    facies_ref, source_ref, perm_ref, store_ref, well_x_ref, well_y_ref, well_rate_ref,
+    rows_ref, basis_ref, side_ref, rhs_ref, store_out_ref, up_ref, down_ref,
+    trans_x, trans_y, trans_z0, trans_z1, scale, storage, field_a, field_b,
+):
+    planes, rows, layers = facies_ref.shape
+    tile_x, tile_y = (source_ref.shape[0], source_ref.shape[1])
+    anchor_x = lax.axis_index("gx") * tile_x
+    anchor_y = lax.axis_index("gy") * tile_y
+    total_x = lax.axis_size("gx") * tile_x
+    total_y = lax.axis_size("gy") * tile_y
+    shape = (rows, layers)
+    layer = lane_iota(shape)
+    row = lax.broadcasted_iota(jnp.int32, shape, 0)
+    offset_y = jnp.where(row < tile_y + MARGIN, row, row - rows)
+    face_y = (
+        (anchor_y + offset_y >= 0)
+        & (anchor_y + offset_y + 1 < total_y)
+        & (row != tile_y + MARGIN - 1)
+    )
+    top = layer == layers - 1
+    ends_0 = face_ends(layer, 0)
+    ends_1 = face_ends(layer, 1)
+    start = jnp.where(lax.rem(layer // BLOCK_Z, 2) == 0, 1.0, 0.0)
+
+    def row_up(value):
+        return pltpu.roll(value, rows - 1, 0)
+
+    def row_down(value):
+        return pltpu.roll(value, 1, 0)
+
+    def layer_up(value):
+        return pltpu.roll(value, layers - 1, 1)
+
+    def layer_down(value):
+        return pltpu.roll(value, 1, 1)
+
+    def coefficients(plane, carry):
+        resist, store, face_before = carry
+        codes = facies_ref[plane]
+        resist_next = 1.0 / table_select(perm_ref, codes)
+        store_next = table_select(store_ref, codes)
+        here = anchor_x + plane - 1 - MARGIN
+        face_x = 2.0 / (resist + resist_next)
+        face_x = jnp.where((here >= 0) & (here + 1 < total_x), face_x, 0.0)
+        y_face = jnp.where(face_y, 2.0 / (resist + row_up(resist)), 0.0)
+        z_face = jnp.where(top, 0.0, 2.0 / (resist + layer_up(resist)))
+        diagonal = (
+            store + face_x + face_before + y_face + row_down(y_face) + z_face + layer_down(z_face)
+        )
+        trans_x[plane - 1] = face_x
+        trans_y[plane - 1] = y_face
+        trans_z0[plane - 1] = jnp.where(ends_0, 0.0, z_face)
+        trans_z1[plane - 1] = jnp.where(ends_1, 0.0, z_face)
+        scale[plane - 1] = RELAX_WEIGHT / diagonal
+        storage[plane - 1] = store
+        field_a[plane - 1] = start
+        return resist_next, store_next, face_x
+
+    codes = facies_ref[0]
+    carry = (
+        1.0 / table_select(perm_ref, codes),
+        table_select(store_ref, codes),
+        jnp.zeros(shape, jnp.float32),
+    )
+    lax.fori_loop(1, planes, coefficients, carry)
+    field_a[planes - 1] = start
+
+    def sweep(old_ref, new_ref, low, high):
+        def step(plane, carry):
+            here, flux_before = carry
+            beyond = old_ref[plane + 1]
+            flux = trans_x[plane] * (beyond - here)
+            flux_y = trans_y[plane] * (row_up(here) - here)
+            above = layer_up(here)
+            gain = above * (1.0 - here)
+            loss = here * (1.0 - above)
+            z0, z1 = (trans_z0[plane], trans_z1[plane])
+            total = (flux - flux_before) + (flux_y - row_down(flux_y))
+            total = total + (z0 * gain - z1 * loss) + layer_down(z0 * loss - z1 * gain)
+            new_ref[plane] = here + scale[plane] * total
+            return beyond, flux
+
+        here = old_ref[low]
+        lax.fori_loop(low, high, step, (here, trans_x[low - 1] * (here - old_ref[low - 1])))
+
+    refs = (field_a, field_b)
+    for sweep_id in range(SWEEPS):
+        sweep(
+            refs[sweep_id % 2], refs[(sweep_id + 1) % 2], 1 + sweep_id, planes - 1 - sweep_id
+        )
+    final = refs[SWEEPS % 2]
+
+    tile = (tile_y, layers)
+    tile_layer = lane_iota(tile)
+    cut_0 = face_ends(tile_layer, 0)
+    cut_any = cut_0 | face_ends(tile_layer, 1)
+    well_hit_y = (
+        lax.broadcasted_iota(jnp.int32, (tile_y, well_y_ref.shape[1]), 0) + anchor_y
+        == well_y_ref[...]
+    )
+
+    def inner(value):
+        return value[:tile_y]
+
+    def gather(plane, sums):
+        at = plane + MARGIN
+        here_all = final[at]
+        here = inner(here_all)
+        y_all = trans_y[at]
+        flux_y_all = y_all * (row_up(here_all) - here_all)
+        step_y = inner(row_up(here_all)) - here
+        step_x = inner(final[at + 1]) - here
+        flux_x = inner(trans_x[at]) * step_x
+        flux_before = inner(trans_x[at - 1]) * (here - inner(final[at - 1]))
+        flux_y = inner(flux_y_all)
+        z_face = jnp.maximum(inner(trans_z0[at]), inner(trans_z1[at]))
+        above = layer_up(here)
+        step_z = above - here
+        energy_z = z_face * step_z * step_z
+        other = 1.0 - here
+        store = inner(storage[at])
+        factor = inner(scale[at])
+        hit = well_hit_y & (well_x_ref[...] == anchor_x + plane)
+        column = jnp.sum(jnp.where(hit, well_rate_ref[...], 0.0), axis=1, keepdims=True)
+        rhs = source_ref[plane] + column / layers
+        below_end = jnp.where(cut_0, here, other)
+        above_end = jnp.where(cut_0, above, 1.0 - above)
+        z_cut = jnp.where(cut_any, z_face, 0.0)
+        basis_ref[plane] = here
+        side_ref[plane] = factor * (
+            (flux_before - flux_x) + (inner(row_down(flux_y_all)) - flux_y)
+        )
+        rhs_ref[plane] = factor * rhs
+        store_out_ref[plane] = factor * store
+        up_ref[plane] = factor * z_face
+        down_ref[plane] = factor * layer_down(z_face)
+        terms = (
+            store * here * here,
+            store * here * other,
+            store * other * other,
+            flux_x * step_x + flux_y * step_y + jnp.where(cut_any, 0.0, energy_z),
+            jnp.where(cut_any, energy_z, 0.0),
+            z_cut * below_end * below_end,
+            z_cut * above_end * above_end,
+            z_cut * below_end * above_end,
+            here * rhs,
+            other * rhs,
+        )
+        return tuple(total + term for total, term in zip(sums, terms))
+
+    sums = lax.fori_loop(0, tile_x, gather, (jnp.zeros(tile, jnp.float32),) * 10)
+    mass_00, mass_01, mass_11, energy, cut, low_2, high_2, low_high, rhs_0, rhs_1 = (
+        jnp.sum(total, axis=0, keepdims=True) for total in sums
+    )
+    line = lane_iota((1, layers))
+    ends_0 = face_ends(line, 0)
+    ends_1 = face_ends(line, 1)
+
+    def layer_after(value):
+        return pltpu.roll(value, 1, 1)
+
+    rows_ref[0:1] = (
+        mass_00
+        + energy
+        + jnp.where(ends_0, low_2, cut)
+        + layer_after(jnp.where(ends_0, high_2, 0.0))
+    )
+    rows_ref[1:2] = (
+        mass_11
+        + energy
+        + jnp.where(ends_1, low_2, cut)
+        + layer_after(jnp.where(ends_1, high_2, 0.0))
+    )
+    rows_ref[2:3] = mass_01 - energy + (low_high - low_2) + layer_after(low_high - high_2)
+    rows_ref[3:4] = -low_high
+    rows_ref[4:5] = rhs_0
+    rows_ref[5:6] = rhs_1
+    rows_ref[6:8] = jnp.zeros((2, layers), jnp.float32)
+
+
+def pressure_kernel(
+    rows_ref, basis_ref, side_ref, rhs_ref, store_ref, up_ref, down_ref, out_ref, entries
+):
+    tile_x, tile_y, layers = basis_ref.shape
+    count = layers // BLOCK_Z
+    shape = (count, layers)
+    node = lax.broadcasted_iota(jnp.int32, shape, 0)
+    layer = lane_iota(shape)
+    base = node * BLOCK_Z
+    half = BLOCK_Z // 2
+    inside = (layer >= base - half) & (layer < base + 3 * half)
+    even = lax.rem(node, 2) == 0
+    rows = REDUCE(rows_ref)
+    total = [rows[i : i + 1] for i in range(6)]
+    parts = (
+        jnp.where(inside, jnp.where(even, total[0], total[1]), 0.0),
+        jnp.where((layer >= base + half) & (layer < base + 3 * half), total[2], 0.0),
+        jnp.where(layer == base + 3 * half - 1, total[3], 0.0),
+        jnp.where(inside, jnp.where(even, total[4], total[5]), 0.0),
+    )
+    for part_id, part in enumerate(parts):
+        entries[part_id] = jnp.broadcast_to(jnp.sum(part, axis=1, keepdims=True), shape)
+    diagonal, first, second, right = (
+        [entries[part_id, k : k + 1] for k in range(count)] for part_id in range(4)
+    )
+    inverses, firsts, seconds = ([], [], [])
+    for k in range(count):
+        inverse = 1.0 / diagonal[k]
+        inverses.append(inverse)
+        if k + 1 < count:
+            lower = first[k] * inverse
+            firsts.append(lower)
+            diagonal[k + 1] = diagonal[k + 1] - lower * first[k]
+            right[k + 1] = right[k + 1] - lower * right[k]
+        if k + 2 < count:
+            far = second[k] * inverse
+            seconds.append(far)
+            first[k + 1] = first[k + 1] - firsts[k] * second[k]
+            diagonal[k + 2] = diagonal[k + 2] - far * second[k]
+            right[k + 2] = right[k + 2] - far * right[k]
+    values = [None] * count
+    for k in reversed(range(count)):
+        value = right[k] * inverses[k]
+        if k + 1 < count:
+            value = value - firsts[k] * values[k + 1]
+        if k + 2 < count:
+            value = value - seconds[k] * values[k + 2]
+        values[k] = value
+    line = lane_iota((1, layers))
+    fields = [jnp.zeros((1, layers), jnp.float32)] * 2
+    for k in range(count):
+        held = (line >= k * BLOCK_Z - half) & (line < k * BLOCK_Z + 3 * half)
+        fields[k % 2] = jnp.where(held, values[k], fields[k % 2])
+    value_1 = jnp.broadcast_to(fields[1], (tile_y, layers))
+    value_0 = jnp.broadcast_to(fields[0], (tile_y, layers))
+    apart = value_0 - value_1
+    for plane in range(tile_x):
+        here = basis_ref[plane]
+        prolonged = here * value_0 + (1.0 - here) * value_1
+        above = pltpu.roll(prolonged, layers - 1, 1)
+        below = pltpu.roll(prolonged, 1, 1)
+        applied = (
+            store_ref[plane] * prolonged
+            + apart * side_ref[plane]
+            + up_ref[plane] * (prolonged - above)
+            + down_ref[plane] * (prolonged - below)
+        )
+        out_ref[plane] = prolonged + (rhs_ref[plane] - applied)
+
+
+def column_step(facies, source, facies_perm, facies_store, well_x, well_y, well_rate):
+    tile_x, tile_y, layers = facies.shape
+    planes, rows = (tile_x + 2 * MARGIN, tile_y + 2 * MARGIN)
+    wide = wide_facies(facies)
+    f32 = jnp.float32
+    tile = jax.ShapeDtypeStruct(facies.shape, f32)
+    vmem = pl.BlockSpec(memory_space=pltpu.VMEM)
+    smem = pl.BlockSpec(memory_space=pltpu.SMEM)
+    partial, *fields = pl.pallas_call(
+        basis_kernel,
+        out_shape=(jax.ShapeDtypeStruct((ROWS, layers), f32),) + (tile,) * 6,
+        in_specs=[vmem, vmem, smem, smem, vmem, vmem, vmem],
+        out_specs=(vmem,) * 7,
+        scratch_shapes=[pltpu.VMEM((planes, rows, layers), f32)] * 8,
+        compiler_params=pltpu.CompilerParams(vmem_limit_bytes=VMEM_BYTES),
+        name="basis",
+    )(
+        wide,
+        source,
+        facies_perm,
+        facies_store,
+        well_x[None, :],
+        well_y[None, :],
+        well_rate[None, :],
+    )
+    total = reduce_rows(partial)
+    return pl.pallas_call(
+        pressure_kernel,
+        out_shape=tile,
+        in_specs=[vmem] * 7,
+        out_specs=vmem,
+        scratch_shapes=[pltpu.VMEM((4, layers // BLOCK_Z, layers), f32)],
+        compiler_params=pltpu.CompilerParams(vmem_limit_bytes=VMEM_BYTES),
+        name="pressure",
+    )(total, *fields)
+
+
+VMEM_BYTES = 16 * 2**20
+
+
+def REDUCE(rows_ref):
+    return rows_ref[...]
+
+
+def reduce_rows(partial):
+    size = lax.axis_size(AXES)
+    if size & (size - 1):
+        return lax.psum(partial, AXES)
+    step = 1
+    while step < size:
+        partial = partial + lax.ppermute(partial, AXES, [(i, i ^ step) for i in range(size)])
+        step *= 2
+    return partial
+
+
 def solution(mesh):
+    def per_device(facies, *others):
+        tile_x, tile_y, layers = facies.shape
+        total_x = tile_x * mesh.shape["gx"]
+        total_y = tile_y * mesh.shape["gy"]
+        one_column = total_x == BLOCK_X and total_y == BLOCK_Y
+        fits = layers % 128 == 0 and tile_y % 8 == 0 and min(tile_x, tile_y) >= MARGIN
+        step = column_step if one_column and fits else general_step
+        return step(facies, *others)
+
     in_specs = (P("gx", "gy", None), P("gx", "gy", None), P(), P(), P(), P(), P())
     out_specs = P("gx", "gy", None)
     return jax.shard_map(

time: 287 us -> 41.6 us (0.14); the launches traced: 284 us -> 41.4 us
  other arithmetic: 62.1 us -> 0.86 us
  local copies, waits for them, and re-layouts: 49.8 us -> 0.78 us
  matrix products: 44 us -> 0 us
  blocking collectives: 43.3 us -> 0 us
  starting transfers between devices: 59.6 us -> 20.2 us
  waiting for transfers between devices: 24.1 us -> 9.49 us
  Pallas kernels: 0 us -> 9.89 us
    dot_general x6 -> x0, matrix products: 43.7 us -> none  [the longest x1 31.7 us: per_device(): jnp.einsum('apqz,cspqz->casz', interior, term_stack, precision=HIGHEST)]
    psum x1 -> x0, blocking collectives: 43.3 us -> none  [per_device(): coarse, coarse_rhs = lax.psum((local_matrix, local_rhs), ('gx', 'gy'))]
    ppermute x24 -> x9, starting transfers between devices: 59.6 us -> 20.2 us  [the longest x5 12.7 us: reduce_rows(): lax.ppermute(partial, AXES, [(i, i ^ step) for i in range(size)])]
    scatter-add x2 -> x0, other arithmetic: 30.2 us -> none  [the longest x1 28.9 us: per_device(): local_matrix = jnp.zeros((coarse_count * coarse_count,), jnp.float32).at[...]
    another operation x2 -> x0, local copies, waits for them, and re-layouts: 20.1 us -> none  [terms_of(): jnp.stack([cut_apply(values_in, storage, trans_all, same_three)] + rim_te...]
    ppermute x24 -> x9, waiting for transfers between devices: 24.1 us -> 9.49 us  [the longest x5 7.25 us: reduce_rows(): lax.ppermute(partial, AXES, [(i, i ^ step) for i in range(size)])]
    another operation x13 -> x0, other arithmetic: 14 us -> none  [the longest x2 11 us: per_device(): jnp.stack([lookup(facies, facies_perm), lookup(facies, facies_store)])]
    sub x4 -> x0, local copies, waits for them, and re-layouts: 10.3 us -> none  [the longest x2 9 us: smooth(): return interior + changes - interior * change_sum[None]]
  transfers between devices with their start and end apart: 24 -> 9, of which waited for: 8 -> 7; matrix products, arithmetic and copies ran while one was open for 16% -> 0% of each run, Pallas kernels for 0% -> 0%
where the time goes in v1:
time: 41.6 us; the launch traced here: 41.4 us
  starting transfers between devices  20.2 us (49%)
  Pallas kernels  9.89 us (24%)
  waiting for transfers between devices  9.49 us (23%)
  other arithmetic  0.86 us (2%)
  local copies, waits for them, and re-layouts  0.78 us (2%)
    ppermute x5, starting transfers between devices, reduce_rows(): lax.ppermute(partial, AXES, [(i, i ^ step) for i in range(size)])  12.7 us
    pallas_call x1, Pallas kernels, column_step(): pl.pallas_call(basis_kernel, out_shape=(jax.ShapeDtypeStruct((ROWS, layer...  8.96 us
    ppermute x5, waiting for transfers between devices, reduce_rows(): lax.ppermute(partial, AXES, [(i, i ^ step) for i in range(size)])  7.25 us
    ppermute x2, starting transfers between devices, pair_swaps(): lax.ppermute(jnp.where(even, last, first), axis, pairs_near + [(j, i) for...  6.24 us
    ppermute x2, waiting for transfers between devices, pair_swaps(): lax.ppermute(jnp.where(even, last, first), axis, pairs_near + [(j, i) for...  2.23 us
    ppermute x2, starting transfers between devices, pair_swaps(): lax.ppermute(jnp.where(even, first, last), axis, pairs_far + [(j, i) for...  1.31 us
    pallas_call x1, Pallas kernels, column_step(): pl.pallas_call(pressure_kernel, out_shape=tile, in_specs=[vmem] * 7, out_...  0.93 us
  transfers between devices with their start and end apart: 9, of which 7 were waited for; matrix products, arithmetic and copies ran while one was open for 0% of the time, Pallas kernels for 0%

profile of v1, /device:TPU:0, one launch (start us, length us, event | category | flops | bytes accessed | tf_op | source)
XLA Modules:
  0.0 41.4 jit_solution(469123029540856305)
XLA Ops:
  0.0 0.8 %slice_select_fusion.3 = (s32[8,4,128]{2,1,0:T(4,128)S(1)}, s32[8,4,128]{2,1,0:T(4,128)S(1)}) fusion(s32[8,16,128]{2,1,0:T(8,128)} %param.7, pred[]{:T(512)S(6)} %eq.10), kind=kLoop, calls=%fused_computation.7 | loop fusion | flops 8192 | bytes 65537 | tf_op jit(solution)/shard_map/jit(_where)/select_n | solution.py:299
  0.8 0.0 copy-start.6
  0.8 0.6 %collective-permute-start = (s32[8,4,128]{2,1,0:T(4,128)S(1)}, s32[8,4,128]{2,1,0:T(4,128)S(1)}, u32[]{:S(2)}, u32[]{:S(2)}) collective-permute-start(s32[8,4,128]{2,1,0:T(4,128)S(1)} %get-tuple-element.23), channel_id=1, source_target_pairs={{0,1},{2,3},{1,0},{3,2},{4,5},{6,7},{5,4},{7,6},{8,9},{10,11},{9,8... | collective-permute-start | bytes 49160 | tf_op jit(solution)/shard_map/ppermute | solution.py:298
  1.3 0.7 %collective-permute-start.1 = (s32[8,4,128]{2,1,0:T(4,128)S(1)}, s32[8,4,128]{2,1,0:T(4,128)S(1)}, u32[]{:S(2)}, u32[]{:S(2)}) collective-permute-start(s32[8,4,128]{2,1,0:T(4,128)S(1)} %get-tuple-element.24), channel_id=1, source_target_pairs={{1,2},{2,1},{5,6},{6,5},{9,10},{10,9},{13,14},{14,13},{17,18},{18,... | collective-permute-start | bytes 49160 | tf_op jit(solution)/shard_map/ppermute | solution.py:301
  2.0 0.2 collective-permute-done
  2.2 0.0 collective-permute-done.1
  2.2 0.0 copy-done.6
  2.3 0.7 %collective-permute-start.2 = (s32[4,24,128]{2,1,0:T(8,128)S(1)}, s32[4,24,128]{2,1,0:T(8,128)S(1)}, u32[]{:S(2)}, u32[]{:S(2)}) collective-permute-start(s32[4,24,128]{2,1,0:T(8,128)S(1)} %get-tuple-element.21), channel_id=1, source_target_pairs={{4,8},{12,16},{20,24},{8,4},{16,12},{24,20},{5,9},{13,17},{21,25},... | collective-permute-start | bytes 147464 | tf_op jit(solution)/shard_map/ppermute | solution.py:301
  2.9 5.7 %collective-permute-start.3 = (s32[4,24,128]{2,1,0:T(8,128)S(1)}, s32[4,24,128]{2,1,0:T(8,128)S(1)}, u32[]{:S(2)}, u32[]{:S(2)}) collective-permute-start(s32[4,24,128]{2,1,0:T(8,128)S(1)} %get-tuple-element.22), channel_id=1, source_target_pairs={{0,4},{8,12},{16,20},{24,28},{4,0},{12,8},{20,16},{28,24},{1,5},{9... | collective-permute-start | bytes 147464 | tf_op jit(solution)/shard_map/ppermute | solution.py:298
  8.6 0.0 collective-permute-done.2
  8.6 2.1 %collective-permute-done.3 = s32[4,24,128]{2,1,0:T(8,128)S(1)} collective-permute-done((s32[4,24,128]{2,1,0:T(8,128)S(1)}, s32[4,24,128]{2,1,0:T(8,128)S(1)}, u32[]{:S(2)}, u32[]{:S(2)}) %collective-permute-start.3) | collective-permute-done | bytes 49184 | tf_op jit(solution)/shard_map/ppermute | solution.py:298
  10.7 0.0 copy-start
  10.7 0.0 copy-start.4
  10.7 0.0 copy-start.5
  10.7 0.0 copy-start.1
  10.8 0.0 copy-start.2
  10.8 0.0 copy-start.3
  10.8 0.7 %copy-done = f32[8,16,128]{2,1,0:T(8,128)S(1)} copy-done((f32[8,16,128]{2,1,0:T(8,128)S(1)}, f32[8,16,128]{2,1,0:T(8,128)}, u32[]{:S(2)}) %copy-start) | copy-done | bytes 65560
  11.5 0.0 copy-done.4
  11.5 0.0 copy-done.5
  11.5 0.0 copy-done.1
  11.5 0.0 copy-done.2
  11.5 0.0 copy-done.3
  11.6 9.0 %basis.1 = (f32[8,128]{1,0:T(8,128)S(1)}, f32[8,16,128]{2,1,0:T(8,128)S(1)}, f32[8,16,128]{2,1,0:T(8,128)S(1)}, f32[8,16,128]{2,1,0:T(8,128)S(1)}, f32[8,16,128]...) custom-call(s32[16,24,128]{2,1,0:T(8,128)S(1)} %pad_add_fusion.facies_ref, ...), custom_call_target="tpu_custom_call" | custom-call | tf_op jit(solution)/shard_map/basis/pallas_call | solution.py:588
  20.5 3.2 %collective-permute-start.4 = (f32[8,128]{1,0:T(8,128)S(1)}, f32[8,128]{1,0:T(8,128)S(1)}, u32[]{:S(2)}, u32[]{:S(2)}) collective-permute-start(f32[8,128]{1,0:T(8,128)S(1)} %get-tuple-element.12), channel_id=1, source_target_pairs={{0,1},{1,0},{2,3},{3,2},{4,5},{5,4},{6,7},{7,6},{8,9},{9,8},{10,11... | collective-permute-start | bytes 12296 | tf_op jit(solution)/shard_map/ppermute | solution.py:630
  23.7 0.8 %collective-permute-done.4 = f32[8,128]{1,0:T(8,128)S(1)} collective-permute-done((f32[8,128]{1,0:T(8,128)S(1)}, f32[8,128]{1,0:T(8,128)S(1)}, u32[]{:S(2)}, u32[]{:S(2)}) %collective-permute-start.4) | collective-permute-done | bytes 4128 | tf_op jit(solution)/shard_map/ppermute | solution.py:630
  24.6 2.5 %collective-permute-start.5 = (f32[8,128]{1,0:T(8,128)S(1)}, f32[8,128]{1,0:T(8,128)S(1)}, u32[]{:S(2)}, u32[]{:S(2)}) collective-permute-start(f32[8,128]{1,0:T(8,128)S(1)} %add.24), channel_id=1, source_target_pairs={{0,2},{1,3},{2,0},{3,1},{4,6},{5,7},{6,4},{7,5},{8,10},{9,11},{10,... | collective-permute-start | bytes 12296 | tf_op jit(solution)/shard_map/ppermute | solution.py:630
  27.1 1.6 %collective-permute-done.5 = f32[8,128]{1,0:T(8,128)S(1)} collective-permute-done((f32[8,128]{1,0:T(8,128)S(1)}, f32[8,128]{1,0:T(8,128)S(1)}, u32[]{:S(2)}, u32[]{:S(2)}) %collective-permute-start.5) | collective-permute-done | bytes 4128 | tf_op jit(solution)/shard_map/ppermute | solution.py:630
  28.7 2.0 %collective-permute-start.6 = (f32[8,128]{1,0:T(8,128)S(1)}, f32[8,128]{1,0:T(8,128)S(1)}, u32[]{:S(2)}, u32[]{:S(2)}) collective-permute-start(f32[8,128]{1,0:T(8,128)S(1)} %add.25), channel_id=1, source_target_pairs={{0,4},{1,5},{2,6},{3,7},{4,0},{5,1},{6,2},{7,3},{8,12},{9,13},{10,... | collective-permute-start | bytes 12296 | tf_op jit(solution)/shard_map/ppermute | solution.py:630
  30.7 1.6 %collective-permute-done.6 = f32[8,128]{1,0:T(8,128)S(1)} collective-permute-done((f32[8,128]{1,0:T(8,128)S(1)}, f32[8,128]{1,0:T(8,128)S(1)}, u32[]{:S(2)}, u32[]{:S(2)}) %collective-permute-start.6) | collective-permute-done | bytes 4128 | tf_op jit(solution)/shard_map/ppermute | solution.py:630
  32.3 1.9 %collective-permute-start.7 = (f32[8,128]{1,0:T(8,128)S(1)}, f32[8,128]{1,0:T(8,128)S(1)}, u32[]{:S(2)}, u32[]{:S(2)}) collective-permute-start(f32[8,128]{1,0:T(8,128)S(1)} %add.26), channel_id=1, source_target_pairs={{0,8},{1,9},{2,10},{3,11},{4,12},{5,13},{6,14},{7,15},{8,0},{9,1},... | collective-permute-start | bytes 12296 | tf_op jit(solution)/shard_map/ppermute | solution.py:630
  34.2 1.7 %collective-permute-done.7 = f32[8,128]{1,0:T(8,128)S(1)} collective-permute-done((f32[8,128]{1,0:T(8,128)S(1)}, f32[8,128]{1,0:T(8,128)S(1)}, u32[]{:S(2)}, u32[]{:S(2)}) %collective-permute-start.7) | collective-permute-done | bytes 4128 | tf_op jit(solution)/shard_map/ppermute | solution.py:630
  35.9 2.9 %collective-permute-start.8 = (f32[8,128]{1,0:T(8,128)S(1)}, f32[8,128]{1,0:T(8,128)S(1)}, u32[]{:S(2)}, u32[]{:S(2)}) collective-permute-start(f32[8,128]{1,0:T(8,128)S(1)} %add.27), channel_id=1, source_target_pairs={{0,16},{1,17},{2,18},{3,19},{4,20},{5,21},{6,22},{7,23},{8,24},{9,... | collective-permute-start | bytes 12296 | tf_op jit(solution)/shard_map/ppermute | solution.py:630
  38.9 1.6 %collective-permute-done.8 = f32[8,128]{1,0:T(8,128)S(1)} collective-permute-done((f32[8,128]{1,0:T(8,128)S(1)}, f32[8,128]{1,0:T(8,128)S(1)}, u32[]{:S(2)}, u32[]{:S(2)}) %collective-permute-start.8) | collective-permute-done | bytes 4128 | tf_op jit(solution)/shard_map/ppermute | solution.py:630
  40.4 0.9 %pressure.1 = f32[8,16,128]{2,1,0:T(8,128)} custom-call(f32[8,128]{1,0:T(8,128)S(1)} %add.28.rows_ref, f32[8,16,128]{2,1,0:T(8,128)S(1)} %get-tuple-element.13.basis_ref, f32[8,16,128]{2,1,0:T(8,128)S(1)} %get-tuple-element.14.side_ref, f32[8,16,128]{2,1,0:T(8,128)S(1)} %get-tuple-element.15.rhs_ref, f32[8,16,128]{2,1,0:T(8,128)S(1)} %get-tuple-element.16.store_ref, ...), custom_call_target="tpu_custom_call" | custom-call | tf_op jit(solution)/shard_map/pressure/pallas_call | solution.py:606
  (10 shorter events, 0.1 us)
Async XLA Ops:
  0.8 1.4 %copy-start.6 = (s32[8,16,128]{2,1,0:T(8,128)S(1)}, s32[8,16,128]{2,1,0:T(8,128)}, u32[]{:S(2)}) copy-start(s32[8,16,128]{2,1,0:T(8,128)} %param.7) | copy-start | bytes 196612
  0.8 1.4 %collective-permute-start = (s32[8,4,128]{2,1,0:T(4,128)S(1)}, s32[8,4,128]{2,1,0:T(4,128)S(1)}, u32[]{:S(2)}, u32[]{:S(2)}) collective-permute-start(s32[8,4,128]{2,1,0:T(4,128)S(1)} %get-tuple-element.23), channel_id=1, source_target_pairs={{0,1},{2,3},{1,0},{3,2},{4,5},{6,7},{5,4},{7,6},{8,9},{10,11},{9,8... | collective-permute-start | bytes 49160 | tf_op jit(solution)/shard_map/ppermute | solution.py:298
  1.3 0.8 %collective-permute-start.1 = (s32[8,4,128]{2,1,0:T(4,128)S(1)}, s32[8,4,128]{2,1,0:T(4,128)S(1)}, u32[]{:S(2)}, u32[]{:S(2)}) collective-permute-start(s32[8,4,128]{2,1,0:T(4,128)S(1)} %get-tuple-element.24), channel_id=1, source_target_pairs={{1,2},{2,1},{5,6},{6,5},{9,10},{10,9},{13,14},{14,13},{17,18},{18,... | collective-permute-start | bytes 49160 | tf_op jit(solution)/shard_map/ppermute | solution.py:301
  2.3 6.4 %collective-permute-start.2 = (s32[4,24,128]{2,1,0:T(8,128)S(1)}, s32[4,24,128]{2,1,0:T(8,128)S(1)}, u32[]{:S(2)}, u32[]{:S(2)}) collective-permute-start(s32[4,24,128]{2,1,0:T(8,128)S(1)} %get-tuple-element.21), channel_id=1, source_target_pairs={{4,8},{12,16},{20,24},{8,4},{16,12},{24,20},{5,9},{13,17},{21,25},... | collective-permute-start | bytes 147464 | tf_op jit(solution)/shard_map/ppermute | solution.py:301
  2.9 7.7 %collective-permute-start.3 = (s32[4,24,128]{2,1,0:T(8,128)S(1)}, s32[4,24,128]{2,1,0:T(8,128)S(1)}, u32[]{:S(2)}, u32[]{:S(2)}) collective-permute-start(s32[4,24,128]{2,1,0:T(8,128)S(1)} %get-tuple-element.22), channel_id=1, source_target_pairs={{0,4},{8,12},{16,20},{24,28},{4,0},{12,8},{20,16},{28,24},{1,5},{9... | collective-permute-start | bytes 147464 | tf_op jit(solution)/shard_map/ppermute | solution.py:298
  10.7 0.8 %copy-start = (f32[8,16,128]{2,1,0:T(8,128)S(1)}, f32[8,16,128]{2,1,0:T(8,128)}, u32[]{:S(2)}) copy-start(f32[8,16,128]{2,1,0:T(8,128)} %source_ref.1) | copy-start | bytes 196612
  10.7 0.8 %copy-start.4 = (s32[64]{0:T(128)S(1)}, s32[64]{0:T(128)}, u32[]{:S(2)}) copy-start(s32[64]{0:T(128)} %param.12) | copy-start | bytes 772
  10.7 0.8 %copy-start.5 = (f32[64]{0:T(128)S(1)}, f32[64]{0:T(128)}, u32[]{:S(2)}) copy-start(f32[64]{0:T(128)} %param.13) | copy-start | bytes 772
  10.7 0.8 %copy-start.1 = (f32[8]{0:T(128)S(1)}, f32[8]{0:T(128)}, u32[]{:S(2)}) copy-start(f32[8]{0:T(128)} %perm_ref.1) | copy-start | bytes 100
  10.8 0.8 %copy-start.2 = (f32[8]{0:T(128)S(1)}, f32[8]{0:T(128)}, u32[]{:S(2)}) copy-start(f32[8]{0:T(128)} %store_ref.1) | copy-start | bytes 100
  10.8 0.8 %copy-start.3 = (s32[64]{0:T(128)S(1)}, s32[64]{0:T(128)}, u32[]{:S(2)}) copy-start(s32[64]{0:T(128)} %param.11) | copy-start | bytes 772
  20.5 4.0 %collective-permute-start.4 = (f32[8,128]{1,0:T(8,128)S(1)}, f32[8,128]{1,0:T(8,128)S(1)}, u32[]{:S(2)}, u32[]{:S(2)}) collective-permute-start(f32[8,128]{1,0:T(8,128)S(1)} %get-tuple-element.12), channel_id=1, source_target_pairs={{0,1},{1,0},{2,3},{3,2},{4,5},{5,4},{6,7},{7,6},{8,9},{9,8},{10,11... | collective-permute-start | bytes 12296 | tf_op jit(solution)/shard_map/ppermute | solution.py:630
  24.6 4.1 %collective-permute-start.5 = (f32[8,128]{1,0:T(8,128)S(1)}, f32[8,128]{1,0:T(8,128)S(1)}, u32[]{:S(2)}, u32[]{:S(2)}) collective-permute-start(f32[8,128]{1,0:T(8,128)S(1)} %add.24), channel_id=1, source_target_pairs={{0,2},{1,3},{2,0},{3,1},{4,6},{5,7},{6,4},{7,5},{8,10},{9,11},{10,... | collective-permute-start | bytes 12296 | tf_op jit(solution)/shard_map/ppermute | solution.py:630
  28.7 3.6 %collective-permute-start.6 = (f32[8,128]{1,0:T(8,128)S(1)}, f32[8,128]{1,0:T(8,128)S(1)}, u32[]{:S(2)}, u32[]{:S(2)}) collective-permute-start(f32[8,128]{1,0:T(8,128)S(1)} %add.25), channel_id=1, source_target_pairs={{0,4},{1,5},{2,6},{3,7},{4,0},{5,1},{6,2},{7,3},{8,12},{9,13},{10,... | collective-permute-start | bytes 12296 | tf_op jit(solution)/shard_map/ppermute | solution.py:630
  32.3 3.6 %collective-permute-start.7 = (f32[8,128]{1,0:T(8,128)S(1)}, f32[8,128]{1,0:T(8,128)S(1)}, u32[]{:S(2)}, u32[]{:S(2)}) collective-permute-start(f32[8,128]{1,0:T(8,128)S(1)} %add.26), channel_id=1, source_target_pairs={{0,8},{1,9},{2,10},{3,11},{4,12},{5,13},{6,14},{7,15},{8,0},{9,1},... | collective-permute-start | bytes 12296 | tf_op jit(solution)/shard_map/ppermute | solution.py:630
  35.9 4.5 %collective-permute-start.8 = (f32[8,128]{1,0:T(8,128)S(1)}, f32[8,128]{1,0:T(8,128)S(1)}, u32[]{:S(2)}, u32[]{:S(2)}) collective-permute-start(f32[8,128]{1,0:T(8,128)S(1)} %add.27), channel_id=1, source_target_pairs={{0,16},{1,17},{2,18},{3,19},{4,20},{5,21},{6,22},{7,23},{8,24},{9,... | collective-permute-start | bytes 12296 | tf_op jit(solution)/shard_map/ppermute | solution.py:630

commit v2 on v0

--- a/solution.py
+++ b/solution.py
@@ -2,6 +2,8 @@
 import jax.numpy as jnp
 import numpy as np
 from jax import lax
+from jax.experimental import pallas as pl
+from jax.experimental.pallas import tpu as pltpu
 from jax.sharding import PartitionSpec as P
 
 BLOCK_X = 64
@@ -212,7 +214,7 @@
     return with_halo(basis_now, (("gx", 1), ("gy", 2)), 1)
 
 
-def per_device(facies, source, facies_perm, facies_store, well_x, well_y, well_rate):
+def general_step(facies, source, facies_perm, facies_store, well_x, well_y, well_rate):
     tile_x, tile_y, layers = facies.shape
     devs_x = lax.axis_size("gx")
     devs_y = lax.axis_size("gy")
@@ -281,7 +283,399 @@
     return prolonged + RELAX_WEIGHT * (rhs_fine - applied) / diagonal[1:-1, 1:-1]
 
 
+MARGIN = SWEEPS + 1
+AXES = ("gx", "gy")
+VMEM_BYTES = 16 * 2**20
+
+
+def pair_swaps(value, dim, axis, width):
+    size, length = (lax.axis_size(axis), value.shape[dim])
+    last = lax.slice_in_dim(value, length - width, length, axis=dim)
+    first = lax.slice_in_dim(value, 0, width, axis=dim)
+    even = lax.axis_index(axis) % 2 == 0
+    pairs_near = [(i, i + 1) for i in range(0, size - 1, 2)]
+    pairs_far = [(i, i + 1) for i in range(1, size - 1, 2)]
+    near = lax.ppermute(
+        jnp.where(even, last, first), axis, pairs_near + [(j, i) for i, j in pairs_near]
+    )
+    far = lax.ppermute(
+        jnp.where(even, first, last), axis, pairs_far + [(j, i) for i, j in pairs_far]
+    )
+    return jnp.where(even, far, near), jnp.where(even, near, far)
+
+
+def lane_iota(shape):
+    return lax.broadcasted_iota(jnp.int32, shape, len(shape) - 1)
+
+
+def face_ends(layer, parity):
+    return lax.rem(layer + 1 + BLOCK_Z // 2 + BLOCK_Z * parity, 2 * BLOCK_Z) == 0
+
+
+def in_grid(layer, parity, count):
+    shifted = layer + BLOCK_Z // 2 + BLOCK_Z * parity
+    node = 2 * (shifted // (2 * BLOCK_Z)) - parity
+    return (node >= 0) & (node < count)
+
+
+def up(value, axis):
+    return pltpu.roll(value, value.shape[axis] - 1, axis)
+
+
+def down(value, axis):
+    return pltpu.roll(value, 1, axis)
+
+
+def code_select(table, codes):
+    result = jnp.broadcast_to(table[0], codes.shape)
+    for code_id in range(1, len(table)):
+        result = jnp.where(codes == code_id, table[code_id], result)
+    return result
+
+
+def plane_faces(resist, store, face_y):
+    layer = lane_iota(resist.shape)
+    y_face = jnp.where(face_y, 2.0 / (resist + up(resist, 0)), 0.0)
+    z_face = jnp.where(layer == resist.shape[1] - 1, 0.0, 2.0 / (resist + up(resist, 1)))
+    part = store + y_face + down(y_face, 0) + z_face + down(z_face, 1)
+    z_faces = [jnp.where(face_ends(layer, parity), 0.0, z_face) for parity in (0, 1)]
+    return y_face, z_faces[0], z_faces[1], part
+
+
+def y_face_mask(shape, tile_y):
+    row = lax.broadcasted_iota(jnp.int32, shape, 0)
+    place = lax.axis_index("gy") * tile_y + jnp.where(row < tile_y + MARGIN, row, row - shape[0])
+    inside = (place >= 0) & (place + 1 < lax.axis_size("gy") * tile_y)
+    return inside & (row != tile_y + MARGIN - 1)
+
+
+def tile_kernel(
+    rows_ref, source_ref, perm_ref, store_ref, well_x_ref, well_y_ref, well_rate_ref,
+    table_ref, resist_ref, storage_ref, x_ref, y_ref, z0_ref, z1_ref, part_ref, rhs_ref,
+):
+    tile_x, rows, layers = rows_ref.shape
+    tile_y = source_ref.shape[1]
+    anchor_x = lax.axis_index("gx") * tile_x
+    anchor_y = lax.axis_index("gy") * tile_y
+    codes = perm_ref.shape[0]
+    resists = [
+        1.0 / jnp.full((1, layers), perm_ref[code], jnp.float32) for code in range(codes)
+    ]
+    stores = [jnp.full((1, layers), store_ref[code], jnp.float32) for code in range(codes)]
+    for code in range(codes):
+        table_ref[code : code + 1] = resists[code]
+        table_ref[codes + code : codes + code + 1] = stores[code]
+    face_y = y_face_mask((rows, layers), tile_y)
+    hit_y = (
+        lax.broadcasted_iota(jnp.int32, (tile_y, well_y_ref.shape[1]), 0) + anchor_y
+        == well_y_ref[...]
+    )
+    before = None
+    for plane in range(tile_x):
+        resist = code_select(resists, rows_ref[plane])
+        store = code_select(stores, rows_ref[plane])
+        y_face, z0, z1, part = plane_faces(resist, store, face_y)
+        resist_ref[plane] = resist
+        storage_ref[plane] = store
+        y_ref[plane] = y_face
+        z0_ref[plane] = z0
+        z1_ref[plane] = z1
+        part_ref[plane] = part
+        if plane:
+            x_ref[plane - 1] = 2.0 / (before + resist)
+        before = resist
+        hit = hit_y & (well_x_ref[...] == anchor_x + plane)
+        column = jnp.sum(jnp.where(hit, well_rate_ref[...], 0.0), axis=1, keepdims=True)
+        rhs_ref[plane] = source_ref[plane] + column / layers
+
+
+def basis_kernel(
+    before_ref, after_ref,
+    table_ref, resist_ref, storage_ref, x_ref, y_ref, z0_ref, z1_ref, part_ref, rhs_ref,
+    packed_ref, basis_ref, side_ref, rhs_out_ref, store_out_ref, up_ref, down_ref,
+    scale, field_a, field_b, x_far, y_far, z0_far, z1_far, sums_ref,
+):
+    tile_x, tile_y, layers = rhs_ref.shape
+    rows = resist_ref.shape[1]
+    planes = tile_x + 2 * MARGIN
+    shape = (rows, layers)
+    anchor_x = lax.axis_index("gx") * tile_x
+    total_x = lax.axis_size("gx") * tile_x
+    face_y = y_face_mask(shape, tile_y)
+    codes = table_ref.shape[0] // 2
+    table = [table_ref[i : i + 1] for i in range(2 * codes)]
+    start = jnp.where(lax.rem(lane_iota(shape) // BLOCK_Z, 2) == 0, 1.0, 0.0)
+
+    def own(plane):
+        return MARGIN <= plane < MARGIN + tile_x
+
+    def face_x(plane):
+        inner = own(plane) and own(plane + 1)
+        return x_ref[plane - MARGIN] if inner else x_far[plane]
+
+    def other_face(near, far, plane):
+        return near[plane - MARGIN] if own(plane) else far[plane]
+
+    resist_last = None
+    x_last = None
+    part_last = None
+    for plane in range(planes):
+        if own(plane):
+            resist = resist_ref[plane - MARGIN]
+            part = part_ref[plane - MARGIN]
+        else:
+            strip = before_ref if plane < MARGIN else after_ref
+            facies = strip[plane if plane < MARGIN else plane - MARGIN - tile_x]
+            resist = code_select(table[:codes], facies)
+            store = code_select(table[codes:], facies)
+            y_far[plane], z0_far[plane], z1_far[plane], part = plane_faces(resist, store, face_y)
+        if plane:
+            if own(plane - 1) and own(plane):
+                x_face = face_x(plane - 1)
+            else:
+                here = anchor_x + plane - 1 - MARGIN
+                x_face = 2.0 / (resist_last + resist)
+                x_face = jnp.where((here >= 0) & (here + 1 < total_x), x_face, 0.0)
+                x_far[plane - 1] = x_face
+            if plane > 1:
+                scale[plane - 1] = RELAX_WEIGHT / (part_last + x_face + x_last)
+            x_last = x_face
+        resist_last, part_last = (resist, part)
+
+    def sweep(read, new_ref, low, high):
+        here = read(low)
+        flux_before = face_x(low - 1) * (here - read(low - 1))
+        for plane in range(low, high):
+            beyond = read(plane + 1)
+            flux = face_x(plane) * (beyond - here)
+            flux_y = other_face(y_ref, y_far, plane) * (up(here, 0) - here)
+            above = up(here, 1)
+            gain = above * (1.0 - here)
+            loss = here * (1.0 - above)
+            z0 = other_face(z0_ref, z0_far, plane)
+            z1 = other_face(z1_ref, z1_far, plane)
+            total = (flux - flux_before) + (flux_y - down(flux_y, 0))
+            total = total + (z0 * gain - z1 * loss) + down(z0 * loss - z1 * gain, 1)
+            new_ref[plane] = here + scale[plane] * total
+            here, flux_before = (beyond, flux)
+
+    fields = (field_a, field_b)
+    read = lambda plane: start
+    for sweep_id in range(SWEEPS):
+        target = fields[sweep_id % 2]
+        sweep(read, target, 1 + sweep_id, planes - 1 - sweep_id)
+        read = lambda plane, ref=target: ref[plane]
+
+    tile = (tile_y, layers)
+    cut_0 = face_ends(lane_iota(tile), 0)
+    cut_any = cut_0 | face_ends(lane_iota(tile), 1)
+
+    def inner(value):
+        return value[:tile_y]
+
+    sums = None
+    for plane in range(tile_x):
+        at = plane + MARGIN
+        here_all = read(at)
+        here = inner(here_all)
+        step_y_all = up(here_all, 0) - here_all
+        flux_y_all = y_ref[plane] * step_y_all
+        flux_y = inner(flux_y_all)
+        step_x = inner(read(at + 1)) - here
+        flux_x = inner(face_x(at)) * step_x
+        flux_before = inner(face_x(at - 1)) * (here - inner(read(at - 1)))
+        z_face = jnp.maximum(inner(z0_ref[plane]), inner(z1_ref[plane]))
+        above = up(here, 1)
+        step_z = above - here
+        energy_z = z_face * step_z * step_z
+        other = 1.0 - here
+        store = inner(storage_ref[plane])
+        factor = inner(scale[at])
+        rhs = rhs_ref[plane]
+        below_end = jnp.where(cut_0, here, other)
+        above_end = jnp.where(cut_0, above, 1.0 - above)
+        z_cut = jnp.where(cut_any, z_face, 0.0)
+        basis_ref[plane] = here
+        side_ref[plane] = factor * (
+            (flux_before - flux_x) + (inner(down(flux_y_all, 0)) - flux_y)
+        )
+        rhs_out_ref[plane] = factor * rhs
+        store_out_ref[plane] = factor * store
+        up_ref[plane] = factor * z_face
+        down_ref[plane] = factor * down(z_face, 1)
+        terms = (
+            store * here * here,
+            store * here * other,
+            store * other * other,
+            flux_x * step_x + flux_y * inner(step_y_all) + jnp.where(cut_any, 0.0, energy_z),
+            jnp.where(cut_any, energy_z, 0.0),
+            z_cut * below_end * below_end,
+            z_cut * above_end * above_end,
+            z_cut * below_end * above_end,
+            here * rhs,
+            other * rhs,
+        )
+        sums = terms if sums is None else [a + b for a, b in zip(sums, terms)]
+    mass_00, mass_01, mass_11, energy, cut, low_2, high_2, low_high, rhs_0, rhs_1 = (
+        jnp.sum(total, axis=0, keepdims=True) for total in sums
+    )
+    line = lane_iota((1, layers))
+    count = layers // BLOCK_Z
+    ends = (face_ends(line, 0), face_ends(line, 1))
+    inside = (in_grid(line, 0, count), in_grid(line, 1, count))
+    for parity, mass, right in ((0, mass_00, rhs_0), (1, mass_11, rhs_1)):
+        own_end = jnp.where(ends[parity], low_2, cut)
+        beyond_end = down(jnp.where(ends[parity], high_2, 0.0), 1)
+        entry = mass + energy + own_end + beyond_end
+        sums_ref[parity : parity + 1] = jnp.where(inside[parity], entry, 0.0)
+        sums_ref[4 + parity : 5 + parity] = jnp.where(inside[parity], right, 0.0)
+    sums_ref[2:3] = mass_01 - energy + (low_high - low_2) + down(low_high - high_2, 1)
+    sums_ref[3:4] = -low_high
+    sums_ref[6:8] = jnp.zeros((2, layers), jnp.float32)
+    window = pltpu.roll(sums_ref[...], 0, 1, stride=1, stride_axis=0)
+    width = 1
+    while width < BLOCK_Z:
+        window = window + pltpu.roll(window, width, 1)
+        width *= 2
+    row = lax.broadcasted_iota(jnp.int32, window.shape, 0)
+    keep = lax.rem(lane_iota(window.shape) + layers - BLOCK_Z // 2 + 1 - row, BLOCK_Z) == 0
+    packed = jnp.sum(jnp.where(keep, window, 0.0), axis=0, keepdims=True)
+    packed_ref[...] = jnp.broadcast_to(packed, packed_ref.shape)
+
+
+def pressure_kernel(
+    rows_ref, basis_ref, side_ref, rhs_ref, store_ref, up_ref, down_ref, out_ref, entries
+):
+    tile_x, tile_y, layers = basis_ref.shape
+    count = layers // BLOCK_Z
+    half = BLOCK_Z // 2
+    shape = (count, layers)
+    node = lax.broadcasted_iota(jnp.int32, shape, 0)
+    layer = lane_iota(shape)
+    packed = jnp.sum(rows_ref[...], axis=0, keepdims=True)
+
+    def held(segment, kind):
+        return layer == lax.rem(segment * BLOCK_Z + half - 1 + kind, layers)
+
+    parity = lax.rem(node, 2)
+    own = held(node, parity) | held(node + 1, parity)
+    right = held(node, parity + 4) | held(node + 1, parity + 4)
+    masks = (own, held(node + 1, 2), held(node + 1, 3), right)
+    for part_id, mask in enumerate(masks):
+        part = jnp.where(mask, packed, 0.0)
+        entries[part_id] = jnp.broadcast_to(jnp.sum(part, axis=1, keepdims=True), shape)
+    diagonal, first, second, right = (
+        [entries[part_id, k : k + 1] for k in range(count)] for part_id in range(4)
+    )
+    inverses, firsts, seconds = ([], [], [])
+    for k in range(count):
+        inverse = 1.0 / diagonal[k]
+        inverses.append(inverse)
+        if k + 1 < count:
+            lower = first[k] * inverse
+            firsts.append(lower)
+            diagonal[k + 1] = diagonal[k + 1] - lower * first[k]
+            right[k + 1] = right[k + 1] - lower * right[k]
+        if k + 2 < count:
+            far = second[k] * inverse
+            seconds.append(far)
+            first[k + 1] = first[k + 1] - firsts[k] * second[k]
+            diagonal[k + 2] = diagonal[k + 2] - far * second[k]
+            right[k + 2] = right[k + 2] - far * right[k]
+    values = [None] * count
+    for k in reversed(range(count)):
+        value = right[k] * inverses[k]
+        if k + 1 < count:
+            value = value - firsts[k] * values[k + 1]
+        if k + 2 < count:
+            value = value - seconds[k] * values[k + 2]
+        values[k] = value
+    line = lane_iota((1, layers))
+    fields = [jnp.zeros((1, layers), jnp.float32)] * 2
+    for k in range(count):
+        support = (line >= k * BLOCK_Z - half) & (line < k * BLOCK_Z + 3 * half)
+        fields[k % 2] = jnp.where(support, values[k], fields[k % 2])
+    value_0 = jnp.broadcast_to(fields[0], (tile_y, layers))
+    value_1 = jnp.broadcast_to(fields[1], (tile_y, layers))
+    apart = value_0 - value_1
+    for plane in range(tile_x):
+        here = basis_ref[plane]
+        prolonged = here * value_0 + (1.0 - here) * value_1
+        applied = (
+            store_ref[plane] * prolonged
+            + apart * side_ref[plane]
+            + up_ref[plane] * (prolonged - up(prolonged, 1))
+            + down_ref[plane] * (prolonged - down(prolonged, 1))
+        )
+        out_ref[plane] = prolonged + (rhs_ref[plane] - applied)
+
+
+def column_step(facies, source, facies_perm, facies_store, well_x, well_y, well_rate):
+    tile_x, tile_y, layers = facies.shape
+    rows = tile_y + 2 * MARGIN
+    planes = tile_x + 2 * MARGIN
+    size = lax.axis_size(AXES)
+    f32 = jnp.float32
+    tile = jax.ShapeDtypeStruct(facies.shape, f32)
+    wide = jax.ShapeDtypeStruct((tile_x, rows, layers), f32)
+    vmem = pl.BlockSpec(memory_space=pltpu.VMEM)
+    smem = pl.BlockSpec(memory_space=pltpu.SMEM)
+    params = pltpu.CompilerParams(vmem_limit_bytes=VMEM_BYTES)
+
+    before, after = pair_swaps(facies, 1, "gy", MARGIN)
+    own = jnp.concatenate([facies, after, before], axis=1)
+    before, after = pair_swaps(own, 0, "gx", MARGIN)
+    near = pl.pallas_call(
+        tile_kernel,
+        out_shape=(jax.ShapeDtypeStruct((2 * facies_perm.shape[0], layers), f32),)
+        + (wide,) * 7
+        + (tile,),
+        in_specs=[vmem, vmem, smem, smem, vmem, vmem, vmem],
+        out_specs=(vmem,) * 9,
+        compiler_params=params,
+        cost_estimate=pl.CostEstimate(flops=3000000, bytes_accessed=1000000, transcendentals=0),
+        name="tile",
+    )(
+        own,
+        source,
+        facies_perm,
+        facies_store,
+        well_x[None, :],
+        well_y[None, :],
+        well_rate[None, :],
+    )
+    copies, *fields = pl.pallas_call(
+        basis_kernel,
+        out_shape=(jax.ShapeDtypeStruct((size, layers), f32),) + (tile,) * 6,
+        in_specs=[vmem] * 11,
+        out_specs=(vmem,) * 7,
+        scratch_shapes=[pltpu.VMEM((planes, rows, layers), f32)] * 7
+        + [pltpu.VMEM((8, layers), f32)],
+        compiler_params=params,
+        name="basis",
+    )(before, after, *near)
+    everyone = lax.all_to_all(copies, AXES, 0, 0, tiled=True)
+    return pl.pallas_call(
+        pressure_kernel,
+        out_shape=tile,
+        in_specs=[vmem] * 7,
+        out_specs=vmem,
+        scratch_shapes=[pltpu.VMEM((4, layers // BLOCK_Z, layers), f32)],
+        compiler_params=params,
+        name="pressure",
+    )(everyone, *fields)
+
+
 def solution(mesh):
+    def per_device(facies, *others):
+        tile_x, tile_y, layers = facies.shape
+        total_x = tile_x * mesh.shape["gx"]
+        total_y = tile_y * mesh.shape["gy"]
+        one_column = total_x == BLOCK_X and total_y == BLOCK_Y
+        fits = layers % 128 == 0 and tile_y % 8 == 0 and min(tile_x, tile_y) >= MARGIN
+        step = column_step if one_column and fits else general_step
+        return step(facies, *others)
+
     in_specs = (P("gx", "gy", None), P("gx", "gy", None), P(), P(), P(), P(), P())
     out_specs = P("gx", "gy", None)
     return jax.shard_map(

time: 287 us -> 30.1 us (0.10); the launches traced: 284 us -> 29.9 us
  other arithmetic: 62.1 us -> 0.83 us
  starting transfers between devices: 59.6 us -> 4.74 us
  local copies, waits for them, and re-layouts: 49.8 us -> 0.66 us
  matrix products: 44 us -> 0 us
  waiting for transfers between devices: 24.1 us -> 0.18 us
  blocking collectives: 43.3 us -> 20.3 us
  Pallas kernels: 0 us -> 3.03 us
    ppermute x24 -> x4, starting transfers between devices: 59.6 us -> 4.74 us  [the longest x2 3.44 us: pair_swaps(): lax.ppermute(jnp.where(even, last, first), axis, pairs_near + [(j, i) for...]
    dot_general x6 -> x0, matrix products: 43.7 us -> none  [the longest x1 31.7 us: per_device(): jnp.einsum('apqz,cspqz->casz', interior, term_stack, precision=HIGHEST)]
    psum x1 -> x0, blocking collectives: 43.3 us -> none  [per_device(): coarse, coarse_rhs = lax.psum((local_matrix, local_rhs), ('gx', 'gy'))]
    scatter-add x2 -> x0, other arithmetic: 30.2 us -> none  [the longest x1 28.9 us: per_device(): local_matrix = jnp.zeros((coarse_count * coarse_count,), jnp.float32).at[...]
    ppermute x24 -> x4, waiting for transfers between devices: 24.1 us -> 0.18 us  [the longest x2 0.17 us: pair_swaps(): lax.ppermute(jnp.where(even, last, first), axis, pairs_near + [(j, i) for...]
    all_to_all x0 -> x1, blocking collectives: none -> 20.3 us  [column_step(): everyone = lax.all_to_all(copies, AXES, 0, 0, tiled=True)]
    another operation x2 -> x0, local copies, waits for them, and re-layouts: 20.1 us -> none  [terms_of(): jnp.stack([cut_apply(values_in, storage, trans_all, same_three)] + rim_te...]
    another operation x13 -> x0, other arithmetic: 14 us -> none  [the longest x2 11 us: per_device(): jnp.stack([lookup(facies, facies_perm), lookup(facies, facies_store)])]
  transfers between devices with their start and end apart: 24 -> 4, of which waited for: 8 -> 1; matrix products, arithmetic and copies ran while one was open for 16% -> 0% of each run, Pallas kernels for 0% -> 3%
where the time goes in v2:
time: 30.1 us; the launch traced here: 29.9 us
  blocking collectives  20.3 us (67%)
  starting transfers between devices  4.74 us (16%)
  Pallas kernels  3.03 us (10%)
  other arithmetic  0.83 us (3%)
  local copies, waits for them, and re-layouts  0.66 us (2%)
    all_to_all x1, blocking collectives, column_step(): everyone = lax.all_to_all(copies, AXES, 0, 0, tiled=True)  20.3 us
    ppermute x2, starting transfers between devices, pair_swaps(): lax.ppermute(jnp.where(even, last, first), axis, pairs_near + [(j, i) for...  3.44 us
    ppermute x2, starting transfers between devices, pair_swaps(): lax.ppermute(jnp.where(even, first, last), axis, pairs_far + [(j, i) for...  1.3 us
    pallas_call x1, Pallas kernels, column_step(): pl.pallas_call(basis_kernel, out_shape=(jax.ShapeDtypeStruct((size, layer...  1.09 us
    pallas_call x1, Pallas kernels, column_step(): pl.pallas_call(tile_kernel, out_shape=(jax.ShapeDtypeStruct((2 * facies_p...  1.01 us
    pallas_call x1, Pallas kernels, column_step(): pl.pallas_call(pressure_kernel, out_shape=tile, in_specs=[vmem] * 7, out_...  0.93 us
    select_n x2, other arithmetic, pair_swaps(): jnp.where(even, last, first)  0.79 us
    unnamed x14, local copies, waits for them, and re-layouts  0.66 us
  transfers between devices with their start and end apart: 4, of which 1 were waited for; matrix products, arithmetic and copies ran while one was open for 0% of the time, Pallas kernels for 3%

profile of v2, /device:TPU:0, one launch (start us, length us, event | category | flops | bytes accessed | tf_op | source)
XLA Modules:
  0.0 29.9 jit_solution(7650627454726581536)
XLA Ops:
  0.0 0.8 %slice_select_fusion.3 = (s32[8,4,128]{2,1,0:T(4,128)S(1)}, s32[8,4,128]{2,1,0:T(4,128)S(1)}) fusion(s32[8,16,128]{2,1,0:T(8,128)} %param.7, pred[]{:T(512)S(6)} %eq.10), kind=kLoop, calls=%fused_computation.6 | loop fusion | flops 8192 | bytes 65537 | tf_op jit(solution)/shard_map/jit(_where)/select_n | solution.py:299
  0.8 0.0 copy-start.6
  0.8 0.6 %collective-permute-start = (s32[8,4,128]{2,1,0:T(4,128)S(1)}, s32[8,4,128]{2,1,0:T(4,128)S(1)}, u32[]{:S(2)}, u32[]{:S(2)}) collective-permute-start(s32[8,4,128]{2,1,0:T(4,128)S(1)} %get-tuple-element.41), channel_id=1, source_target_pairs={{0,1},{2,3},{1,0},{3,2},{4,5},{6,7},{5,4},{7,6},{8,9},{10,11},{9,8... | collective-permute-start | bytes 49160 | tf_op jit(solution)/shard_map/ppermute | solution.py:298
  1.3 0.7 %collective-permute-start.1 = (s32[8,4,128]{2,1,0:T(4,128)S(1)}, s32[8,4,128]{2,1,0:T(4,128)S(1)}, u32[]{:S(2)}, u32[]{:S(2)}) collective-permute-start(s32[8,4,128]{2,1,0:T(4,128)S(1)} %get-tuple-element.42), channel_id=1, source_target_pairs={{1,2},{2,1},{5,6},{6,5},{9,10},{10,9},{13,14},{14,13},{17,18},{18,... | collective-permute-start | bytes 49160 | tf_op jit(solution)/shard_map/ppermute | solution.py:301
  2.0 0.2 collective-permute-done
  2.2 0.0 collective-permute-done.1
  2.2 0.0 copy-done.6
  2.2 0.0 copy-start
  2.3 0.0 copy-start.4
  2.3 0.0 copy-start.5
  2.3 2.9 %collective-permute-start.3 = (s32[4,24,128]{2,1,0:T(8,128)S(1)}, s32[4,24,128]{2,1,0:T(8,128)S(1)}, u32[]{:S(2)}, u32[]{:S(2)}) collective-permute-start(s32[4,24,128]{2,1,0:T(8,128)S(1)} %get-tuple-element.39), channel_id=1, source_target_pairs={{0,4},{8,12},{16,20},{24,28},{4,0},{12,8},{20,16},{28,24},{1,5},{9... | collective-permute-start | bytes 147464 | tf_op jit(solution)/shard_map/ppermute | solution.py:298
  5.2 0.7 %collective-permute-start.2 = (s32[4,24,128]{2,1,0:T(8,128)S(1)}, s32[4,24,128]{2,1,0:T(8,128)S(1)}, u32[]{:S(2)}, u32[]{:S(2)}) collective-permute-start(s32[4,24,128]{2,1,0:T(8,128)S(1)} %get-tuple-element.40), channel_id=1, source_target_pairs={{4,8},{12,16},{20,24},{8,4},{16,12},{24,20},{5,9},{13,17},{21,25},... | collective-permute-start | bytes 147464 | tf_op jit(solution)/shard_map/ppermute | solution.py:301
  5.8 0.0 copy-start.1
  5.8 0.0 copy-start.2
  5.9 0.0 copy-start.3
  5.9 0.0 copy-done
  5.9 0.0 copy-done.4
  5.9 0.0 copy-done.5
  5.9 0.6 %copy-done.1 = f32[8]{0:T(128)S(1)} copy-done((f32[8]{0:T(128)S(1)}, f32[8]{0:T(128)}, u32[]{:S(2)}) %copy-start.1) | copy-done | bytes 56
  6.5 0.0 copy-done.2
  6.5 0.0 copy-done.3
  6.5 1.0 %tile.1 = (f32[16,128]{1,0:T(8,128)S(1)}, f32[8,24,128]{2,1,0:T(8,128)S(1)}, f32[8,24,128]{2,1,0:T(8,128)S(1)}, f32[8,24,128]{2,1,0:T(8,128)S(1)}, f32[8,24,128]...) custom-call(s32[8,24,128]{2,1,0:T(8,128)S(1)} %pad_add_fusion.rows_r, ...), custom_call_target="tpu_custom_call" | custom-call | flops 3000000 | bytes 1000000 | tf_op jit(solution)/shard_map/tile/pallas_call | solution.py:628
  7.5 0.0 collective-permute-done.3
  7.5 0.0 collective-permute-done.2
  7.6 1.1 %basis.1 = (f32[32,128]{1,0:T(8,128)S(1)}, f32[8,16,128]{2,1,0:T(8,128)S(1)}, f32[8,16,128]{2,1,0:T(8,128)S(1)}, f32[8,16,128]{2,1,0:T(8,128)S(1)}, f32[8,16,128...) custom-call(s32[4,24,128]{2,1,0:T(8,128)S(1)} %get-tuple-element.38.before_ref, ...), custom_call_target="tpu_custom_call" | custom-call | tf_op jit(solution)/shard_map/basis/pallas_call | solution.py:647
  8.7 20.3 %all_to_all.11 = f32[32,1,128]{2,1,0:T(1,128)S(1)} all-to-all(f32[32,1,128]{2,1,0:T(1,128)S(1)} %bitcast.12), channel_id=1, replica_groups=mesh['gx'=8,'gy'=4] {'gx','gy'}, dimensions={0} | all-to-all | bytes 32768 | tf_op jit(solution)/shard_map/all_to_all | solution.py:657
  28.9 0.9 %pressure.1 = f32[8,16,128]{2,1,0:T(8,128)} custom-call(f32[32,128]{1,0:T(8,128)S(1)} %bitcast.11, f32[8,16,128]{2,1,0:T(8,128)S(1)} %get-tuple-element.31.basis_ref, f32[8,16,128]{2,1,0:T(8,128)S(1)} %get-tuple-element.32.side_ref, f32[8,16,128]{2,1,0:T(8,128)S(1)} %get-tuple-element.33.rhs_ref, f32[8,16,128]{2,1,0:T(8,128)S(1)} %get-tuple-element.34.store_ref, ...), custom_call_target="tpu_custom_call" | custom-call | tf_op jit(solution)/shard_map/pressure/pallas_call | solution.py:658
  (4 shorter events, 0.0 us)
Async XLA Ops:
  0.8 1.4 %copy-start.6 = (s32[8,16,128]{2,1,0:T(8,128)S(1)}, s32[8,16,128]{2,1,0:T(8,128)}, u32[]{:S(2)}) copy-start(s32[8,16,128]{2,1,0:T(8,128)} %param.7) | copy-start | bytes 196612
  0.8 1.4 %collective-permute-start = (s32[8,4,128]{2,1,0:T(4,128)S(1)}, s32[8,4,128]{2,1,0:T(4,128)S(1)}, u32[]{:S(2)}, u32[]{:S(2)}) collective-permute-start(s32[8,4,128]{2,1,0:T(4,128)S(1)} %get-tuple-element.41), channel_id=1, source_target_pairs={{0,1},{2,3},{1,0},{3,2},{4,5},{6,7},{5,4},{7,6},{8,9},{10,11},{9,8... | collective-permute-start | bytes 49160 | tf_op jit(solution)/shard_map/ppermute | solution.py:298
  1.3 0.8 %collective-permute-start.1 = (s32[8,4,128]{2,1,0:T(4,128)S(1)}, s32[8,4,128]{2,1,0:T(4,128)S(1)}, u32[]{:S(2)}, u32[]{:S(2)}) collective-permute-start(s32[8,4,128]{2,1,0:T(4,128)S(1)} %get-tuple-element.42), channel_id=1, source_target_pairs={{1,2},{2,1},{5,6},{6,5},{9,10},{10,9},{13,14},{14,13},{17,18},{18,... | collective-permute-start | bytes 49160 | tf_op jit(solution)/shard_map/ppermute | solution.py:301
  2.2 3.6 %copy-start = (f32[8,16,128]{2,1,0:T(8,128)S(1)}, f32[8,16,128]{2,1,0:T(8,128)}, u32[]{:S(2)}) copy-start(f32[8,16,128]{2,1,0:T(8,128)} %source_ref.1) | copy-start | bytes 196612
  2.3 3.6 %copy-start.4 = (s32[64]{0:T(128)S(1)}, s32[64]{0:T(128)}, u32[]{:S(2)}) copy-start(s32[64]{0:T(128)} %param.12) | copy-start | bytes 772
  2.3 3.6 %copy-start.5 = (f32[64]{0:T(128)S(1)}, f32[64]{0:T(128)}, u32[]{:S(2)}) copy-start(f32[64]{0:T(128)} %param.13) | copy-start | bytes 772
  2.3 5.3 %collective-permute-start.3 = (s32[4,24,128]{2,1,0:T(8,128)S(1)}, s32[4,24,128]{2,1,0:T(8,128)S(1)}, u32[]{:S(2)}, u32[]{:S(2)}) collective-permute-start(s32[4,24,128]{2,1,0:T(8,128)S(1)} %get-tuple-element.39), channel_id=1, source_target_pairs={{0,4},{8,12},{16,20},{24,28},{4,0},{12,8},{20,16},{28,24},{1,5},{9... | collective-permute-start | bytes 147464 | tf_op jit(solution)/shard_map/ppermute | solution.py:298
  5.2 2.4 %collective-permute-start.2 = (s32[4,24,128]{2,1,0:T(8,128)S(1)}, s32[4,24,128]{2,1,0:T(8,128)S(1)}, u32[]{:S(2)}, u32[]{:S(2)}) collective-permute-start(s32[4,24,128]{2,1,0:T(8,128)S(1)} %get-tuple-element.40), channel_id=1, source_target_pairs={{4,8},{12,16},{20,24},{8,4},{16,12},{24,20},{5,9},{13,17},{21,25},... | collective-permute-start | bytes 147464 | tf_op jit(solution)/shard_map/ppermute | solution.py:301
  5.8 0.7 %copy-start.1 = (f32[8]{0:T(128)S(1)}, f32[8]{0:T(128)}, u32[]{:S(2)}) copy-start(f32[8]{0:T(128)} %perm_ref.1) | copy-start | bytes 100
  5.8 0.7 %copy-start.2 = (f32[8]{0:T(128)S(1)}, f32[8]{0:T(128)}, u32[]{:S(2)}) copy-start(f32[8]{0:T(128)} %store_ref.1) | copy-start | bytes 100
  5.9 0.7 %copy-start.3 = (s32[64]{0:T(128)S(1)}, s32[64]{0:T(128)}, u32[]{:S(2)}) copy-start(s32[64]{0:T(128)} %param.11) | copy-start | bytes 772

commit v3 on v2

--- a/solution.py
+++ b/solution.py
@@ -195,7 +195,7 @@
 
 
 def smooth(basis_ext, geo_set):
-    storage, trans_all, diagonal, same_all, starts = geo_set
+    storage, trans_all, diagonal, same_all, _ = geo_set
 
     def change_of(values_in, same_x, same_y, same_z):
         return (
@@ -226,10 +226,10 @@
     coeff_wide = with_halo(coeffs, (("gx", 1), ("gy", 2)), 1)
     geo_one = geometry(coeff_wide, 1, anchor_x, anchor_y, total_x, total_y)
     basis_now = initial(geo_one)[:, 1:-1, 1:-1]
-    for sweep_id in range(SWEEPS):
+    for _ in range(SWEEPS):
         basis_now = smooth(basis_halo(basis_now), geo_one)
     basis_now = basis_halo(basis_now)
-    storage, trans_all, diagonal, same_all, starts = geo_one
+    storage, trans_all, diagonal, same_all, _ = geo_one
 
     def terms_of(values_in, same_x, same_y, same_z):
         same_three = (same_x, same_y, same_z)
@@ -288,6 +288,10 @@
 VMEM_BYTES = 16 * 2**20
 
 
+def named_permute(value, axis, pairs):
+    return lax.ppermute(value, axis, pairs + [(j, i) for i, j in pairs])
+
+
 def pair_swaps(value, dim, axis, width):
     size, length = (lax.axis_size(axis), value.shape[dim])
     last = lax.slice_in_dim(value, length - width, length, axis=dim)
@@ -295,12 +299,8 @@
     even = lax.axis_index(axis) % 2 == 0
     pairs_near = [(i, i + 1) for i in range(0, size - 1, 2)]
     pairs_far = [(i, i + 1) for i in range(1, size - 1, 2)]
-    near = lax.ppermute(
-        jnp.where(even, last, first), axis, pairs_near + [(j, i) for i, j in pairs_near]
-    )
-    far = lax.ppermute(
-        jnp.where(even, first, last), axis, pairs_far + [(j, i) for i, j in pairs_far]
-    )
+    far = named_permute(jnp.where(even, first, last), axis, pairs_far)
+    near = named_permute(jnp.where(even, last, first), axis, pairs_near)
     return jnp.where(even, far, near), jnp.where(even, near, far)
 
 

time: 30.1 us -> 30.1 us (level)
  no operation moved by 1% of the time
where the time goes in v3:
time: 30.1 us; the launch traced here: 29.9 us
  blocking collectives  20.3 us (67%)
  starting transfers between devices  4.74 us (16%)
  Pallas kernels  3.03 us (10%)
  other arithmetic  0.83 us (3%)
  local copies, waits for them, and re-layouts  0.66 us (2%)
    all_to_all x1, blocking collectives, column_step(): everyone = lax.all_to_all(copies, AXES, 0, 0, tiled=True)  20.3 us
    ppermute x4, starting transfers between devices, named_permute(): return lax.ppermute(value, axis, pairs + [(j, i) for i, j in pairs])  4.74 us
    pallas_call x1, Pallas kernels, column_step(): pl.pallas_call(basis_kernel, out_shape=(jax.ShapeDtypeStruct((size, layer...  1.09 us
    pallas_call x1, Pallas kernels, column_step(): pl.pallas_call(tile_kernel, out_shape=(jax.ShapeDtypeStruct((2 * facies_p...  1.01 us
    pallas_call x1, Pallas kernels, column_step(): pl.pallas_call(pressure_kernel, out_shape=tile, in_specs=[vmem] * 7, out_...  0.93 us
    select_n x2, other arithmetic, pair_swaps(): near = named_permute(jnp.where(even, last, first), axis, pairs_near)  0.79 us
    unnamed x14, local copies, waits for them, and re-layouts  0.66 us
  transfers between devices with their start and end apart: 4, of which 1 were waited for; matrix products, arithmetic and copies ran while one was open for 0% of the time, Pallas kernels for 3%

profile of v3, /device:TPU:0, one launch (start us, length us, event | category | flops | bytes accessed | tf_op | source)
XLA Modules:
  0.0 29.9 jit_solution(7650627454726581536)
XLA Ops:
  0.0 0.8 %slice_select_fusion.3 = (s32[8,4,128]{2,1,0:T(4,128)S(1)}, s32[8,4,128]{2,1,0:T(4,128)S(1)}) fusion(s32[8,16,128]{2,1,0:T(8,128)} %param.7, pred[]{:T(512)S(6)} %eq.10), kind=kLoop, calls=%fused_computation.6 | loop fusion | flops 8192 | bytes 65537 | tf_op jit(solution)/shard_map/jit(_where)/select_n | solution.py:303
  0.8 0.0 copy-start.6
  0.8 0.6 %collective-permute-start = (s32[8,4,128]{2,1,0:T(4,128)S(1)}, s32[8,4,128]{2,1,0:T(4,128)S(1)}, u32[]{:S(2)}, u32[]{:S(2)}) collective-permute-start(s32[8,4,128]{2,1,0:T(4,128)S(1)} %get-tuple-element.41), channel_id=1, source_target_pairs={{0,1},{2,3},{1,0},{3,2},{4,5},{6,7},{5,4},{7,6},{8,9},{10,11},{9,8... | collective-permute-start | bytes 49160 | tf_op jit(solution)/shard_map/ppermute | solution.py:292
  1.3 0.7 %collective-permute-start.1 = (s32[8,4,128]{2,1,0:T(4,128)S(1)}, s32[8,4,128]{2,1,0:T(4,128)S(1)}, u32[]{:S(2)}, u32[]{:S(2)}) collective-permute-start(s32[8,4,128]{2,1,0:T(4,128)S(1)} %get-tuple-element.42), channel_id=1, source_target_pairs={{1,2},{2,1},{5,6},{6,5},{9,10},{10,9},{13,14},{14,13},{17,18},{18,... | collective-permute-start | bytes 49160 | tf_op jit(solution)/shard_map/ppermute | solution.py:292
  2.0 0.2 collective-permute-done
  2.2 0.0 collective-permute-done.1
  2.2 0.0 copy-done.6
  2.2 0.0 copy-start
  2.3 0.0 copy-start.4
  2.3 0.0 copy-start.5
  2.3 2.9 %collective-permute-start.3 = (s32[4,24,128]{2,1,0:T(8,128)S(1)}, s32[4,24,128]{2,1,0:T(8,128)S(1)}, u32[]{:S(2)}, u32[]{:S(2)}) collective-permute-start(s32[4,24,128]{2,1,0:T(8,128)S(1)} %get-tuple-element.39), channel_id=1, source_target_pairs={{0,4},{8,12},{16,20},{24,28},{4,0},{12,8},{20,16},{28,24},{1,5},{9... | collective-permute-start | bytes 147464 | tf_op jit(solution)/shard_map/ppermute | solution.py:292
  5.2 0.7 %collective-permute-start.2 = (s32[4,24,128]{2,1,0:T(8,128)S(1)}, s32[4,24,128]{2,1,0:T(8,128)S(1)}, u32[]{:S(2)}, u32[]{:S(2)}) collective-permute-start(s32[4,24,128]{2,1,0:T(8,128)S(1)} %get-tuple-element.40), channel_id=1, source_target_pairs={{4,8},{12,16},{20,24},{8,4},{16,12},{24,20},{5,9},{13,17},{21,25},... | collective-permute-start | bytes 147464 | tf_op jit(solution)/shard_map/ppermute | solution.py:292
  5.8 0.0 copy-start.1
  5.8 0.0 copy-start.2
  5.9 0.0 copy-start.3
  5.9 0.0 copy-done
  5.9 0.0 copy-done.4
  5.9 0.0 copy-done.5
  5.9 0.6 %copy-done.1 = f32[8]{0:T(128)S(1)} copy-done((f32[8]{0:T(128)S(1)}, f32[8]{0:T(128)}, u32[]{:S(2)}) %copy-start.1) | copy-done | bytes 56
  6.5 0.0 copy-done.2
  6.5 0.0 copy-done.3
  6.5 1.0 %tile.1 = (f32[16,128]{1,0:T(8,128)S(1)}, f32[8,24,128]{2,1,0:T(8,128)S(1)}, f32[8,24,128]{2,1,0:T(8,128)S(1)}, f32[8,24,128]{2,1,0:T(8,128)S(1)}, f32[8,24,128]...) custom-call(s32[8,24,128]{2,1,0:T(8,128)S(1)} %pad_add_fusion.rows_r, ...), custom_call_target="tpu_custom_call" | custom-call | flops 3000000 | bytes 1000000 | tf_op jit(solution)/shard_map/tile/pallas_call | solution.py:628
  7.5 0.0 collective-permute-done.3
  7.5 0.0 collective-permute-done.2
  7.6 1.1 %basis.1 = (f32[32,128]{1,0:T(8,128)S(1)}, f32[8,16,128]{2,1,0:T(8,128)S(1)}, f32[8,16,128]{2,1,0:T(8,128)S(1)}, f32[8,16,128]{2,1,0:T(8,128)S(1)}, f32[8,16,128...) custom-call(s32[4,24,128]{2,1,0:T(8,128)S(1)} %get-tuple-element.38.before_ref, ...), custom_call_target="tpu_custom_call" | custom-call | tf_op jit(solution)/shard_map/basis/pallas_call | solution.py:647
  8.7 20.3 %all_to_all.11 = f32[32,1,128]{2,1,0:T(1,128)S(1)} all-to-all(f32[32,1,128]{2,1,0:T(1,128)S(1)} %bitcast.12), channel_id=1, replica_groups=mesh['gx'=8,'gy'=4] {'gx','gy'}, dimensions={0} | all-to-all | bytes 32768 | tf_op jit(solution)/shard_map/all_to_all | solution.py:657
  28.9 0.9 %pressure.1 = f32[8,16,128]{2,1,0:T(8,128)} custom-call(f32[32,128]{1,0:T(8,128)S(1)} %bitcast.11, f32[8,16,128]{2,1,0:T(8,128)S(1)} %get-tuple-element.31.basis_ref, f32[8,16,128]{2,1,0:T(8,128)S(1)} %get-tuple-element.32.side_ref, f32[8,16,128]{2,1,0:T(8,128)S(1)} %get-tuple-element.33.rhs_ref, f32[8,16,128]{2,1,0:T(8,128)S(1)} %get-tuple-element.34.store_ref, ...), custom_call_target="tpu_custom_call" | custom-call | tf_op jit(solution)/shard_map/pressure/pallas_call | solution.py:658
  (4 shorter events, 0.0 us)
Async XLA Ops:
  0.8 1.4 %copy-start.6 = (s32[8,16,128]{2,1,0:T(8,128)S(1)}, s32[8,16,128]{2,1,0:T(8,128)}, u32[]{:S(2)}) copy-start(s32[8,16,128]{2,1,0:T(8,128)} %param.7) | copy-start | bytes 196612
  0.8 1.4 %collective-permute-start = (s32[8,4,128]{2,1,0:T(4,128)S(1)}, s32[8,4,128]{2,1,0:T(4,128)S(1)}, u32[]{:S(2)}, u32[]{:S(2)}) collective-permute-start(s32[8,4,128]{2,1,0:T(4,128)S(1)} %get-tuple-element.41), channel_id=1, source_target_pairs={{0,1},{2,3},{1,0},{3,2},{4,5},{6,7},{5,4},{7,6},{8,9},{10,11},{9,8... | collective-permute-start | bytes 49160 | tf_op jit(solution)/shard_map/ppermute | solution.py:292
  1.3 0.8 %collective-permute-start.1 = (s32[8,4,128]{2,1,0:T(4,128)S(1)}, s32[8,4,128]{2,1,0:T(4,128)S(1)}, u32[]{:S(2)}, u32[]{:S(2)}) collective-permute-start(s32[8,4,128]{2,1,0:T(4,128)S(1)} %get-tuple-element.42), channel_id=1, source_target_pairs={{1,2},{2,1},{5,6},{6,5},{9,10},{10,9},{13,14},{14,13},{17,18},{18,... | collective-permute-start | bytes 49160 | tf_op jit(solution)/shard_map/ppermute | solution.py:292
  2.2 3.6 %copy-start = (f32[8,16,128]{2,1,0:T(8,128)S(1)}, f32[8,16,128]{2,1,0:T(8,128)}, u32[]{:S(2)}) copy-start(f32[8,16,128]{2,1,0:T(8,128)} %source_ref.1) | copy-start | bytes 196612
  2.3 3.6 %copy-start.4 = (s32[64]{0:T(128)S(1)}, s32[64]{0:T(128)}, u32[]{:S(2)}) copy-start(s32[64]{0:T(128)} %param.12) | copy-start | bytes 772
  2.3 3.6 %copy-start.5 = (f32[64]{0:T(128)S(1)}, f32[64]{0:T(128)}, u32[]{:S(2)}) copy-start(f32[64]{0:T(128)} %param.13) | copy-start | bytes 772
  2.3 5.3 %collective-permute-start.3 = (s32[4,24,128]{2,1,0:T(8,128)S(1)}, s32[4,24,128]{2,1,0:T(8,128)S(1)}, u32[]{:S(2)}, u32[]{:S(2)}) collective-permute-start(s32[4,24,128]{2,1,0:T(8,128)S(1)} %get-tuple-element.39), channel_id=1, source_target_pairs={{0,4},{8,12},{16,20},{24,28},{4,0},{12,8},{20,16},{28,24},{1,5},{9... | collective-permute-start | bytes 147464 | tf_op jit(solution)/shard_map/ppermute | solution.py:292
  5.2 2.4 %collective-permute-start.2 = (s32[4,24,128]{2,1,0:T(8,128)S(1)}, s32[4,24,128]{2,1,0:T(8,128)S(1)}, u32[]{:S(2)}, u32[]{:S(2)}) collective-permute-start(s32[4,24,128]{2,1,0:T(8,128)S(1)} %get-tuple-element.40), channel_id=1, source_target_pairs={{4,8},{12,16},{20,24},{8,4},{16,12},{24,20},{5,9},{13,17},{21,25},... | collective-permute-start | bytes 147464 | tf_op jit(solution)/shard_map/ppermute | solution.py:292
  5.8 0.7 %copy-start.1 = (f32[8]{0:T(128)S(1)}, f32[8]{0:T(128)}, u32[]{:S(2)}) copy-start(f32[8]{0:T(128)} %perm_ref.1) | copy-start | bytes 100
  5.8 0.7 %copy-start.2 = (f32[8]{0:T(128)S(1)}, f32[8]{0:T(128)}, u32[]{:S(2)}) copy-start(f32[8]{0:T(128)} %store_ref.1) | copy-start | bytes 100
  5.9 0.7 %copy-start.3 = (s32[64]{0:T(128)S(1)}, s32[64]{0:T(128)}, u32[]{:S(2)}) copy-start(s32[64]{0:T(128)} %param.11) | copy-start | bytes 772

commit v4 on v3

--- a/solution.py
+++ b/solution.py
@@ -288,19 +288,31 @@
 VMEM_BYTES = 16 * 2**20
 
 
-def named_permute(value, axis, pairs):
-    return lax.ppermute(value, axis, pairs + [(j, i) for i, j in pairs])
+def swap_along(value, axis, first):
+    sizes = {name_: lax.axis_size(name_) for name_ in AXES}
+    other = AXES[1 - AXES.index(axis)]
+    pairs = []
+    for gx in range(sizes[AXES[0]]):
+        for gy in range(sizes[AXES[1]]):
+            place = {AXES[0]: gx, AXES[1]: gy}
+            partner = dict(place)
+            along = first + ((place[axis] - first) ^ 1) if place[axis] >= first else -1
+            if 0 <= along < sizes[axis]:
+                partner[axis] = along
+            else:
+                partner[other] = place[other] ^ 1
+            if partner[other] < sizes[other]:
+                pairs.append(tuple(p[AXES[0]] * sizes[AXES[1]] + p[AXES[1]] for p in (place, partner)))
+    return lax.ppermute(value, AXES, pairs)
 
 
 def pair_swaps(value, dim, axis, width):
-    size, length = (lax.axis_size(axis), value.shape[dim])
+    length = value.shape[dim]
     last = lax.slice_in_dim(value, length - width, length, axis=dim)
     first = lax.slice_in_dim(value, 0, width, axis=dim)
     even = lax.axis_index(axis) % 2 == 0
-    pairs_near = [(i, i + 1) for i in range(0, size - 1, 2)]
-    pairs_far = [(i, i + 1) for i in range(1, size - 1, 2)]
-    far = named_permute(jnp.where(even, first, last), axis, pairs_far)
-    near = named_permute(jnp.where(even, last, first), axis, pairs_near)
+    far = swap_along(jnp.where(even, first, last), axis, 1)
+    near = swap_along(jnp.where(even, last, first), axis, 0)
     return jnp.where(even, far, near), jnp.where(even, near, far)
 
 
@@ -349,9 +361,33 @@
     return inside & (row != tile_y + MARGIN - 1)
 
 
+def sweep_planes(low, high, read, write, face_x, face_y, face_z, scale):
+    if low >= high:
+        return
+    here = read(low)
+    flux_before = face_x(low - 1) * (here - read(low - 1))
+    for plane in range(low, high):
+        beyond = read(plane + 1)
+        flux = face_x(plane) * (beyond - here)
+        flux_y = face_y(plane) * (up(here, 0) - here)
+        above = up(here, 1)
+        gain = above * (1.0 - here)
+        loss = here * (1.0 - above)
+        z0, z1 = face_z(plane)
+        total = (flux - flux_before) + (flux_y - down(flux_y, 0))
+        total = total + (z0 * gain - z1 * loss) + down(z0 * loss - z1 * gain, 1)
+        write(plane, here + scale(plane) * total)
+        here, flux_before = (beyond, flux)
+
+
+def start_field(shape):
+    return jnp.where(lax.rem(lane_iota(shape) // BLOCK_Z, 2) == 0, 1.0, 0.0)
+
+
 def tile_kernel(
     rows_ref, source_ref, perm_ref, store_ref, well_x_ref, well_y_ref, well_rate_ref,
-    table_ref, resist_ref, storage_ref, x_ref, y_ref, z0_ref, z1_ref, part_ref, rhs_ref,
+    table_ref, resist_ref, storage_ref, x_ref, y_ref, z0_ref, z1_ref, part_ref, scale_ref, rhs_ref,
+    *field_refs,
 ):
     tile_x, rows, layers = rows_ref.shape
     tile_y = source_ref.shape[1]
@@ -370,7 +406,7 @@
         lax.broadcasted_iota(jnp.int32, (tile_y, well_y_ref.shape[1]), 0) + anchor_y
         == well_y_ref[...]
     )
-    before = None
+    before, x_before, part_before = (None, None, None)
     for plane in range(tile_x):
         resist = code_select(resists, rows_ref[plane])
         store = code_select(stores, rows_ref[plane])
@@ -382,44 +418,66 @@
         z1_ref[plane] = z1
         part_ref[plane] = part
         if plane:
-            x_ref[plane - 1] = 2.0 / (before + resist)
-        before = resist
+            x_face = 2.0 / (before + resist)
+            x_ref[plane - 1] = x_face
+            if plane > 1:
+                scale_ref[plane - 1] = RELAX_WEIGHT / (part_before + x_face + x_before)
+            x_before = x_face
+        before, part_before = (resist, part)
         hit = hit_y & (well_x_ref[...] == anchor_x + plane)
         column = jnp.sum(jnp.where(hit, well_rate_ref[...], 0.0), axis=1, keepdims=True)
         rhs_ref[plane] = source_ref[plane] + column / layers
-
-
-def basis_kernel(
-    before_ref, after_ref,
-    table_ref, resist_ref, storage_ref, x_ref, y_ref, z0_ref, z1_ref, part_ref, rhs_ref,
-    packed_ref, basis_ref, side_ref, rhs_out_ref, store_out_ref, up_ref, down_ref,
-    scale, field_a, field_b, x_far, y_far, z0_far, z1_far, sums_ref,
-):
+    start = start_field((rows, layers))
+    read = lambda plane: start
+    for sweep_id, field in enumerate(field_refs):
+        sweep_planes(
+            1 + sweep_id,
+            tile_x - 1 - sweep_id,
+            read,
+            field.__setitem__,
+            x_ref.__getitem__,
+            y_ref.__getitem__,
+            lambda plane: (z0_ref[plane], z1_ref[plane]),
+            scale_ref.__getitem__,
+        )
+        read = field.__getitem__
+
+
+def basis_kernel(*refs):
+    before_ref, after_ref, table_ref, resist_ref, storage_ref, x_ref, y_ref, z0_ref, z1_ref = refs[:9]
+    part_ref, scale_ref, rhs_ref = refs[9:12]
+    near_fields = refs[12 : 12 + SWEEPS]
+    refs = refs[12 + SWEEPS :]
+    packed_ref, basis_ref, side_ref, rhs_out_ref, store_out_ref, up_ref, down_ref = refs[:7]
+    scale_far, x_far, y_far, z0_far, z1_far, sums_ref = refs[7:13]
+    far_fields = refs[13:]
     tile_x, tile_y, layers = rhs_ref.shape
     rows = resist_ref.shape[1]
     planes = tile_x + 2 * MARGIN
     shape = (rows, layers)
     anchor_x = lax.axis_index("gx") * tile_x
     total_x = lax.axis_size("gx") * tile_x
-    face_y = y_face_mask(shape, tile_y)
+    face_mask_y = y_face_mask(shape, tile_y)
     codes = table_ref.shape[0] // 2
     table = [table_ref[i : i + 1] for i in range(2 * codes)]
-    start = jnp.where(lax.rem(lane_iota(shape) // BLOCK_Z, 2) == 0, 1.0, 0.0)
-
-    def own(plane):
-        return MARGIN <= plane < MARGIN + tile_x
+
+    def own(plane, depth=0):
+        return MARGIN + depth <= plane < MARGIN + tile_x - depth
 
     def face_x(plane):
         inner = own(plane) and own(plane + 1)
         return x_ref[plane - MARGIN] if inner else x_far[plane]
 
-    def other_face(near, far, plane):
-        return near[plane - MARGIN] if own(plane) else far[plane]
-
-    resist_last = None
-    x_last = None
-    part_last = None
+    def near_or_far(near, far, depth=0):
+        return lambda plane: near[plane - MARGIN] if own(plane, depth) else far[plane]
+
+    face_y = near_or_far(y_ref, y_far)
+    face_z0 = near_or_far(z0_ref, z0_far)
+    face_z1 = near_or_far(z1_ref, z1_far)
+    scale = near_or_far(scale_ref, scale_far, 1)
+    resist_last, x_last, part_last = (None, None, None)
     for plane in range(planes):
+        part = None
         if own(plane):
             resist = resist_ref[plane - MARGIN]
             part = part_ref[plane - MARGIN]
@@ -427,8 +485,11 @@
             strip = before_ref if plane < MARGIN else after_ref
             facies = strip[plane if plane < MARGIN else plane - MARGIN - tile_x]
             resist = code_select(table[:codes], facies)
-            store = code_select(table[codes:], facies)
-            y_far[plane], z0_far[plane], z1_far[plane], part = plane_faces(resist, store, face_y)
+            if 0 < plane < planes - 1:
+                store = code_select(table[codes:], facies)
+                y_far[plane], z0_far[plane], z1_far[plane], part = plane_faces(
+                    resist, store, face_mask_y
+                )
         if plane:
             if own(plane - 1) and own(plane):
                 x_face = face_x(plane - 1)
@@ -437,34 +498,29 @@
                 x_face = 2.0 / (resist_last + resist)
                 x_face = jnp.where((here >= 0) & (here + 1 < total_x), x_face, 0.0)
                 x_far[plane - 1] = x_face
-            if plane > 1:
-                scale[plane - 1] = RELAX_WEIGHT / (part_last + x_face + x_last)
+            if plane > 1 and not own(plane - 1, 1):
+                scale_far[plane - 1] = RELAX_WEIGHT / (part_last + x_face + x_last)
             x_last = x_face
         resist_last, part_last = (resist, part)
 
-    def sweep(read, new_ref, low, high):
-        here = read(low)
-        flux_before = face_x(low - 1) * (here - read(low - 1))
-        for plane in range(low, high):
-            beyond = read(plane + 1)
-            flux = face_x(plane) * (beyond - here)
-            flux_y = other_face(y_ref, y_far, plane) * (up(here, 0) - here)
-            above = up(here, 1)
-            gain = above * (1.0 - here)
-            loss = here * (1.0 - above)
-            z0 = other_face(z0_ref, z0_far, plane)
-            z1 = other_face(z1_ref, z1_far, plane)
-            total = (flux - flux_before) + (flux_y - down(flux_y, 0))
-            total = total + (z0 * gain - z1 * loss) + down(z0 * loss - z1 * gain, 1)
-            new_ref[plane] = here + scale[plane] * total
-            here, flux_before = (beyond, flux)
-
-    fields = (field_a, field_b)
+    start = start_field(shape)
     read = lambda plane: start
     for sweep_id in range(SWEEPS):
-        target = fields[sweep_id % 2]
-        sweep(read, target, 1 + sweep_id, planes - 1 - sweep_id)
-        read = lambda plane, ref=target: ref[plane]
+        depth = 1 + sweep_id
+        first_end = min(MARGIN + depth, planes - depth)
+        last_start = max(first_end, MARGIN + tile_x - depth)
+        for low, high in ((depth, first_end), (last_start, planes - depth)):
+            sweep_planes(
+                low,
+                high,
+                read,
+                far_fields[sweep_id].__setitem__,
+                face_x,
+                face_y,
+                lambda plane: (face_z0(plane), face_z1(plane)),
+                scale,
+            )
+        read = near_or_far(near_fields[sweep_id], far_fields[sweep_id], depth)
 
     tile = (tile_y, layers)
     cut_0 = face_ends(lane_iota(tile), 0)
@@ -490,7 +546,7 @@
         energy_z = z_face * step_z * step_z
         other = 1.0 - here
         store = inner(storage_ref[plane])
-        factor = inner(scale[at])
+        factor = inner(scale(at))
         rhs = rhs_ref[plane]
         below_end = jnp.where(cut_0, here, other)
         above_end = jnp.where(cut_0, above, 1.0 - above)
@@ -543,6 +599,38 @@
     packed_ref[...] = jnp.broadcast_to(packed, packed_ref.shape)
 
 
+def solve_band(diagonal, first, second, right):
+    count = len(diagonal)
+    matrix = {(k, k): diagonal[k] for k in range(count)}
+    for distance, band in ((1, first), (2, second)):
+        for k in range(count - distance):
+            matrix[k, k + distance] = band[k]
+            matrix[k + distance, k] = band[k]
+    left = list(range(count))
+    steps = []
+    while left:
+        pivot = left.pop(0 if len(steps) % 2 == 0 else -1)
+        inverse = 1.0 / matrix[pivot, pivot]
+        linked = [k for k in left if (pivot, k) in matrix]
+        lower = {k: matrix[pivot, k] * inverse for k in linked}
+        for k in linked:
+            right[k] = right[k] - lower[k] * right[pivot]
+            for other in linked:
+                if other >= k:
+                    change = lower[k] * matrix[pivot, other]
+                    entry = matrix[k, other] - change if (k, other) in matrix else -change
+                    matrix[k, other] = entry
+                    matrix[other, k] = entry
+        steps.append((pivot, inverse, lower))
+    values = [None] * count
+    for pivot, inverse, lower in reversed(steps):
+        value = right[pivot] * inverse
+        for k, factor in lower.items():
+            value = value - factor * values[k]
+        values[pivot] = value
+    return values
+
+
 def pressure_kernel(
     rows_ref, basis_ref, side_ref, rhs_ref, store_ref, up_ref, down_ref, out_ref, entries
 ):
@@ -564,32 +652,9 @@
     for part_id, mask in enumerate(masks):
         part = jnp.where(mask, packed, 0.0)
         entries[part_id] = jnp.broadcast_to(jnp.sum(part, axis=1, keepdims=True), shape)
-    diagonal, first, second, right = (
-        [entries[part_id, k : k + 1] for k in range(count)] for part_id in range(4)
-    )
-    inverses, firsts, seconds = ([], [], [])
-    for k in range(count):
-        inverse = 1.0 / diagonal[k]
-        inverses.append(inverse)
-        if k + 1 < count:
-            lower = first[k] * inverse
-            firsts.append(lower)
-            diagonal[k + 1] = diagonal[k + 1] - lower * first[k]
-            right[k + 1] = right[k + 1] - lower * right[k]
-        if k + 2 < count:
-            far = second[k] * inverse
-            seconds.append(far)
-            first[k + 1] = first[k + 1] - firsts[k] * second[k]
-            diagonal[k + 2] = diagonal[k + 2] - far * second[k]
-            right[k + 2] = right[k + 2] - far * right[k]
-    values = [None] * count
-    for k in reversed(range(count)):
-        value = right[k] * inverses[k]
-        if k + 1 < count:
-            value = value - firsts[k] * values[k + 1]
-        if k + 2 < count:
-            value = value - seconds[k] * values[k + 2]
-        values[k] = value
+    values = solve_band(
+        *([entries[part_id, k : k + 1] for k in range(count)] for part_id in range(4))
+    )
     line = lane_iota((1, layers))
     fields = [jnp.zeros((1, layers), jnp.float32)] * 2
     for k in range(count):
@@ -628,10 +693,11 @@
     near = pl.pallas_call(
         tile_kernel,
         out_shape=(jax.ShapeDtypeStruct((2 * facies_perm.shape[0], layers), f32),)
-        + (wide,) * 7
-        + (tile,),
+        + (wide,) * 8
+        + (tile,)
+        + (wide,) * SWEEPS,
         in_specs=[vmem, vmem, smem, smem, vmem, vmem, vmem],
-        out_specs=(vmem,) * 9,
+        out_specs=(vmem,) * (10 + SWEEPS),
         compiler_params=params,
         cost_estimate=pl.CostEstimate(flops=3000000, bytes_accessed=1000000, transcendentals=0),
         name="tile",
@@ -647,10 +713,11 @@
     copies, *fields = pl.pallas_call(
         basis_kernel,
         out_shape=(jax.ShapeDtypeStruct((size, layers), f32),) + (tile,) * 6,
-        in_specs=[vmem] * 11,
+        in_specs=[vmem] * (12 + SWEEPS),
         out_specs=(vmem,) * 7,
-        scratch_shapes=[pltpu.VMEM((planes, rows, layers), f32)] * 7
-        + [pltpu.VMEM((8, layers), f32)],
+        scratch_shapes=[pltpu.VMEM((planes, rows, layers), f32)] * 5
+        + [pltpu.VMEM((8, layers), f32)]
+        + [pltpu.VMEM((planes, rows, layers), f32)] * SWEEPS,
         compiler_params=params,
         name="basis",
     )(before, after, *near)

time: 30.1 us -> 26.3 us (0.87)
  blocking collectives: 20.3 us -> 14.2 us
  waiting for transfers between devices: 0.18 us -> 2.04 us
  starting transfers between devices: 4.74 us -> 5.2 us
    all_to_all x1, blocking collectives: 20.3 us -> 14.2 us  [column_step(): everyone = lax.all_to_all(copies, AXES, 0, 0, tiled=True)]
    ppermute x4, waiting for transfers between devices: 0.18 us -> 2.04 us  [swap_along(): return lax.ppermute(value, AXES, pairs)]
    ppermute x4, starting transfers between devices: 4.74 us -> 5.2 us  [swap_along(): return lax.ppermute(value, AXES, pairs)]
  transfers between devices with their start and end apart: 4 -> 4, of which waited for: 1 -> 2; matrix products, arithmetic and copies ran while one was open for 0% -> 0% of each run, Pallas kernels for 3% -> 4%
where the time goes in v4:
time: 26.3 us; the launch traced here: 26.1 us
  blocking collectives  14.2 us (54%)
  starting transfers between devices  5.2 us (20%)
  Pallas kernels  3.1 us (12%)
  waiting for transfers between devices  2.04 us (8%)
  other arithmetic  0.82 us (3%)
  local copies, waits for them, and re-layouts  0.67 us (3%)
    all_to_all x1, blocking collectives, column_step(): everyone = lax.all_to_all(copies, AXES, 0, 0, tiled=True)  14.2 us
    ppermute x4, starting transfers between devices, swap_along(): return lax.ppermute(value, AXES, pairs)  5.2 us
    ppermute x4, waiting for transfers between devices, swap_along(): return lax.ppermute(value, AXES, pairs)  2.04 us
    pallas_call x1, Pallas kernels, column_step(): pl.pallas_call(tile_kernel, out_shape=(jax.ShapeDtypeStruct((2 * facies_p...  1.16 us
    pallas_call x1, Pallas kernels, column_step(): pl.pallas_call(basis_kernel, out_shape=(jax.ShapeDtypeStruct((size, layer...  1.05 us
    pallas_call x1, Pallas kernels, column_step(): pl.pallas_call(pressure_kernel, out_shape=tile, in_specs=[vmem] * 7, out_...  0.89 us
    select_n x2, other arithmetic, pair_swaps(): near = swap_along(jnp.where(even, last, first), axis, 0)  0.79 us
    unnamed x14, local copies, waits for them, and re-layouts  0.67 us
  transfers between devices with their start and end apart: 4, of which 2 were waited for; matrix products, arithmetic and copies ran while one was open for 0% of the time, Pallas kernels for 4%

profile of v4, /device:TPU:0, one launch (start us, length us, event | category | flops | bytes accessed | tf_op | source)
XLA Modules:
  0.0 26.1 jit_solution(17618711323602507016)
XLA Ops:
  0.0 0.8 %slice_select_fusion.3 = (s32[8,4,128]{2,1,0:T(4,128)S(1)}, s32[8,4,128]{2,1,0:T(4,128)S(1)}) fusion(s32[8,16,128]{2,1,0:T(8,128)} %param.7, pred[]{:T(512)S(6)} %eq.10), kind=kLoop, calls=%fused_computation.6 | loop fusion | flops 8192 | bytes 65537 | tf_op jit(solution)/shard_map/jit(_where)/select_n | solution.py:315
  0.8 0.0 copy-start.6
  0.8 0.6 %collective-permute-start = (s32[8,4,128]{2,1,0:T(4,128)S(1)}, s32[8,4,128]{2,1,0:T(4,128)S(1)}, u32[]{:S(2)}, u32[]{:S(2)}) collective-permute-start(s32[8,4,128]{2,1,0:T(4,128)S(1)} %get-tuple-element.49), channel_id=1, source_target_pairs={{0,1},{1,0},{2,3},{3,2},{4,5},{5,4},{6,7},{7,6},{8,9},{9,8},{10,11... | collective-permute-start | bytes 49160 | tf_op jit(solution)/shard_map/ppermute | solution.py:306
  1.3 2.6 %collective-permute-start.1 = (s32[8,4,128]{2,1,0:T(4,128)S(1)}, s32[8,4,128]{2,1,0:T(4,128)S(1)}, u32[]{:S(2)}, u32[]{:S(2)}) collective-permute-start(s32[8,4,128]{2,1,0:T(4,128)S(1)} %get-tuple-element.50), channel_id=1, source_target_pairs={{0,4},{1,2},{2,1},{3,7},{4,0},{5,6},{6,5},{7,3},{8,12},{9,10},{10,... | collective-permute-start | bytes 49160 | tf_op jit(solution)/shard_map/ppermute | solution.py:306
  3.9 0.0 collective-permute-done
  3.9 1.7 %collective-permute-done.1 = s32[8,4,128]{2,1,0:T(4,128)S(1)} collective-permute-done((s32[8,4,128]{2,1,0:T(4,128)S(1)}, s32[8,4,128]{2,1,0:T(4,128)S(1)}, u32[]{:S(2)}, u32[]{:S(2)}) %collective-permute-start.1) | collective-permute-done | bytes 16416 | tf_op jit(solution)/shard_map/ppermute | solution.py:306
  5.6 0.0 copy-done.6
  5.7 0.0 copy-start
  5.7 0.0 copy-start.4
  5.7 0.0 copy-start.5
  5.7 2.1 %collective-permute-start.3 = (s32[4,24,128]{2,1,0:T(8,128)S(1)}, s32[4,24,128]{2,1,0:T(8,128)S(1)}, u32[]{:S(2)}, u32[]{:S(2)}) collective-permute-start(s32[4,24,128]{2,1,0:T(8,128)S(1)} %get-tuple-element.47), channel_id=1, source_target_pairs={{0,4},{1,5},{2,6},{3,7},{4,0},{5,1},{6,2},{7,3},{8,12},{9,13},{10,... | collective-permute-start | bytes 147464 | tf_op jit(solution)/shard_map/ppermute | solution.py:306
  7.8 0.0 collective-permute-start.2
  7.8 0.0 copy-start.1
  7.8 0.0 copy-start.2
  7.8 0.0 copy-start.3
  7.8 0.0 copy-done
  7.8 0.0 copy-done.4
  7.8 0.0 copy-done.5
  7.8 0.6 %copy-done.1 = f32[8]{0:T(128)S(1)} copy-done((f32[8]{0:T(128)S(1)}, f32[8]{0:T(128)}, u32[]{:S(2)}) %copy-start.1) | copy-done | bytes 56
  8.5 0.0 copy-done.2
  8.5 0.0 copy-done.3
  8.5 1.2 %tile.1 = (f32[16,128]{1,0:T(8,128)S(1)}, f32[8,24,128]{2,1,0:T(8,128)S(1)}, f32[8,24,128]{2,1,0:T(8,128)S(1)}, f32[8,24,128]{2,1,0:T(8,128)S(1)}, f32[8,24,128]...) custom-call(s32[8,24,128]{2,1,0:T(8,128)S(1)} %pad_add_fusion.rows_r, ...), custom_call_target="tpu_custom_call" | custom-call | flops 3000000 | bytes 1000000 | tf_op jit(solution)/shard_map/tile/pallas_call | solution.py:693
  9.6 0.3 %collective-permute-done.3 = s32[4,24,128]{2,1,0:T(8,128)S(1)} collective-permute-done((s32[4,24,128]{2,1,0:T(8,128)S(1)}, s32[4,24,128]{2,1,0:T(8,128)S(1)}, u32[]{:S(2)}, u32[]{:S(2)}) %collective-permute-start.3) | collective-permute-done | bytes 49184 | tf_op jit(solution)/shard_map/ppermute | solution.py:306
  10.0 0.0 collective-permute-done.2
  10.0 1.0 %basis.1 = (f32[32,128]{1,0:T(8,128)S(1)}, f32[8,16,128]{2,1,0:T(8,128)S(1)}, f32[8,16,128]{2,1,0:T(8,128)S(1)}, f32[8,16,128]{2,1,0:T(8,128)S(1)}, f32[8,16,128...) custom-call(s32[4,24,128]{2,1,0:T(8,128)S(1)} %get-tuple-element.46.refs_0_, ...), custom_call_target="tpu_custom_call" | custom-call | tf_op jit(solution)/shard_map/basis/pallas_call | solution.py:713
  11.0 14.2 %all_to_all.11 = f32[32,1,128]{2,1,0:T(1,128)S(1)} all-to-all(f32[32,1,128]{2,1,0:T(1,128)S(1)} %bitcast.12), channel_id=1, replica_groups=mesh['gx'=8,'gy'=4] {'gx','gy'}, dimensions={0} | all-to-all | bytes 32768 | tf_op jit(solution)/shard_map/all_to_all | solution.py:724
  25.2 0.9 %pressure.1 = f32[8,16,128]{2,1,0:T(8,128)} custom-call(f32[32,128]{1,0:T(8,128)S(1)} %bitcast.11, f32[8,16,128]{2,1,0:T(8,128)S(1)} %get-tuple-element.39.basis_ref, f32[8,16,128]{2,1,0:T(8,128)S(1)} %get-tuple-element.40.side_ref, f32[8,16,128]{2,1,0:T(8,128)S(1)} %get-tuple-element.41.rhs_ref, f32[8,16,128]{2,1,0:T(8,128)S(1)} %get-tuple-element.42.store_ref, ...), custom_call_target="tpu_custom_call" | custom-call | tf_op jit(solution)/shard_map/pressure/pallas_call | solution.py:725
  (4 shorter events, 0.0 us)
Async XLA Ops:
  0.8 4.8 %copy-start.6 = (s32[8,16,128]{2,1,0:T(8,128)S(1)}, s32[8,16,128]{2,1,0:T(8,128)}, u32[]{:S(2)}) copy-start(s32[8,16,128]{2,1,0:T(8,128)} %param.7) | copy-start | bytes 196612
  0.8 3.1 %collective-permute-start = (s32[8,4,128]{2,1,0:T(4,128)S(1)}, s32[8,4,128]{2,1,0:T(4,128)S(1)}, u32[]{:S(2)}, u32[]{:S(2)}) collective-permute-start(s32[8,4,128]{2,1,0:T(4,128)S(1)} %get-tuple-element.49), channel_id=1, source_target_pairs={{0,1},{1,0},{2,3},{3,2},{4,5},{5,4},{6,7},{7,6},{8,9},{9,8},{10,11... | collective-permute-start | bytes 49160 | tf_op jit(solution)/shard_map/ppermute | solution.py:306
  1.3 4.3 %collective-permute-start.1 = (s32[8,4,128]{2,1,0:T(4,128)S(1)}, s32[8,4,128]{2,1,0:T(4,128)S(1)}, u32[]{:S(2)}, u32[]{:S(2)}) collective-permute-start(s32[8,4,128]{2,1,0:T(4,128)S(1)} %get-tuple-element.50), channel_id=1, source_target_pairs={{0,4},{1,2},{2,1},{3,7},{4,0},{5,6},{6,5},{7,3},{8,12},{9,10},{10,... | collective-permute-start | bytes 49160 | tf_op jit(solution)/shard_map/ppermute | solution.py:306
  5.7 2.2 %copy-start = (f32[8,16,128]{2,1,0:T(8,128)S(1)}, f32[8,16,128]{2,1,0:T(8,128)}, u32[]{:S(2)}) copy-start(f32[8,16,128]{2,1,0:T(8,128)} %source_ref.1) | copy-start | bytes 196612
  5.7 2.1 %copy-start.4 = (s32[64]{0:T(128)S(1)}, s32[64]{0:T(128)}, u32[]{:S(2)}) copy-start(s32[64]{0:T(128)} %param.12) | copy-start | bytes 772
  5.7 2.1 %copy-start.5 = (f32[64]{0:T(128)S(1)}, f32[64]{0:T(128)}, u32[]{:S(2)}) copy-start(f32[64]{0:T(128)} %param.13) | copy-start | bytes 772
  5.7 4.3 %collective-permute-start.3 = (s32[4,24,128]{2,1,0:T(8,128)S(1)}, s32[4,24,128]{2,1,0:T(8,128)S(1)}, u32[]{:S(2)}, u32[]{:S(2)}) collective-permute-start(s32[4,24,128]{2,1,0:T(8,128)S(1)} %get-tuple-element.47), channel_id=1, source_target_pairs={{0,4},{1,5},{2,6},{3,7},{4,0},{5,1},{6,2},{7,3},{8,12},{9,13},{10,... | collective-permute-start | bytes 147464 | tf_op jit(solution)/shard_map/ppermute | solution.py:306
  7.8 2.2 %collective-permute-start.2 = (s32[4,24,128]{2,1,0:T(8,128)S(1)}, s32[4,24,128]{2,1,0:T(8,128)S(1)}, u32[]{:S(2)}, u32[]{:S(2)}) collective-permute-start(s32[4,24,128]{2,1,0:T(8,128)S(1)} %get-tuple-element.48), channel_id=1, source_target_pairs={{0,1},{1,0},{2,3},{3,2},{4,8},{5,9},{6,10},{7,11},{8,4},{9,5},{10,... | collective-permute-start | bytes 147464 | tf_op jit(solution)/shard_map/ppermute | solution.py:306
  7.8 0.7 %copy-start.1 = (f32[8]{0:T(128)S(1)}, f32[8]{0:T(128)}, u32[]{:S(2)}) copy-start(f32[8]{0:T(128)} %perm_ref.1) | copy-start | bytes 100
  7.8 0.7 %copy-start.2 = (f32[8]{0:T(128)S(1)}, f32[8]{0:T(128)}, u32[]{:S(2)}) copy-start(f32[8]{0:T(128)} %store_ref.1) | copy-start | bytes 100
  7.8 0.7 %copy-start.3 = (s32[64]{0:T(128)S(1)}, s32[64]{0:T(128)}, u32[]{:S(2)}) copy-start(s32[64]{0:T(128)} %param.11) | copy-start | bytes 772

commit v5 on v4

--- a/solution.py
+++ b/solution.py
@@ -687,7 +687,11 @@
     smem = pl.BlockSpec(memory_space=pltpu.SMEM)
     params = pltpu.CompilerParams(vmem_limit_bytes=VMEM_BYTES)
 
-    before, after = pair_swaps(facies, 1, "gy", MARGIN)
+    far = swap_along(facies, "gy", 1)
+    near = swap_along(facies, "gy", 0)
+    even = lax.axis_index("gy") % 2 == 0
+    before = jnp.where(even, far[:, -MARGIN:], near[:, -MARGIN:])
+    after = jnp.where(even, near[:, :MARGIN], far[:, :MARGIN])
     own = jnp.concatenate([facies, after, before], axis=1)
     before, after = pair_swaps(own, 0, "gx", MARGIN)
     near = pl.pallas_call(

time: 26.3 us -> 26 us (0.989)
  other arithmetic: 0.82 us -> 0.05 us
  waiting for transfers between devices: 2.04 us -> 2.74 us
    select_n x2 -> x1, other arithmetic: 0.79 us -> 0.01 us  [pair_swaps(): near = swap_along(jnp.where(even, last, first), axis, 0)]
    ppermute x4, waiting for transfers between devices: 2.04 us -> 2.74 us  [swap_along(): return lax.ppermute(value, AXES, pairs)]
where the time goes in v5:
time: 26 us; the launch traced here: 25.9 us
  blocking collectives  14.2 us (55%)
  starting transfers between devices  5.06 us (19%)
  Pallas kernels  3.1 us (12%)
  waiting for transfers between devices  2.74 us (11%)
  local copies, waits for them, and re-layouts  0.69 us (3%)
    all_to_all x1, blocking collectives, column_step(): everyone = lax.all_to_all(copies, AXES, 0, 0, tiled=True)  14.2 us
    ppermute x4, starting transfers between devices, swap_along(): return lax.ppermute(value, AXES, pairs)  5.06 us
    ppermute x4, waiting for transfers between devices, swap_along(): return lax.ppermute(value, AXES, pairs)  2.74 us
    pallas_call x1, Pallas kernels, column_step(): pl.pallas_call(tile_kernel, out_shape=(jax.ShapeDtypeStruct((2 * facies_p...  1.16 us
    pallas_call x1, Pallas kernels, column_step(): pl.pallas_call(basis_kernel, out_shape=(jax.ShapeDtypeStruct((size, layer...  1.05 us
    pallas_call x1, Pallas kernels, column_step(): pl.pallas_call(pressure_kernel, out_shape=tile, in_specs=[vmem] * 7, out_...  0.89 us
    unnamed x14, local copies, waits for them, and re-layouts  0.69 us
  transfers between devices with their start and end apart: 4, of which 2 were waited for; matrix products, arithmetic and copies ran while one was open for 0% of the time, Pallas kernels for 4%

profile of v5, /device:TPU:0, one launch (start us, length us, event | category | flops | bytes accessed | tf_op | source)
XLA Modules:
  0.0 25.9 jit_solution(1128879879544502067)
XLA Ops:
  0.0 0.5 %collective-permute-start = (s32[8,16,128]{2,1,0:T(8,128)}, s32[8,16,128]{2,1,0:T(8,128)S(1)}, u32[]{:S(2)}, u32[]{:S(2)}) collective-permute-start(s32[8,16,128]{2,1,0:T(8,128)} %param.7), channel_id=1, source_target_pairs={{0,1},{1,0},{2,3},{3,2},{4,5},{5,4},{6,7},{7,6},{8,9},{9,8},{10,11... | collective-permute-start | bytes 196616 | tf_op jit(solution)/shard_map/ppermute | solution.py:306
  0.5 2.5 %collective-permute-start.1 = (s32[8,16,128]{2,1,0:T(8,128)}, s32[8,16,128]{2,1,0:T(8,128)S(1)}, u32[]{:S(2)}, u32[]{:S(2)}) collective-permute-start(s32[8,16,128]{2,1,0:T(8,128)} %param.7), channel_id=1, source_target_pairs={{0,4},{1,2},{2,1},{3,7},{4,0},{5,6},{6,5},{7,3},{8,12},{9,10},{10,... | collective-permute-start | bytes 196616 | tf_op jit(solution)/shard_map/ppermute | solution.py:306
  3.0 0.0 copy-start.6
  3.0 0.0 collective-permute-done
  3.0 2.4 %collective-permute-done.1 = s32[8,16,128]{2,1,0:T(8,128)S(1)} collective-permute-done((s32[8,16,128]{2,1,0:T(8,128)}, s32[8,16,128]{2,1,0:T(8,128)S(1)}, u32[]{:S(2)}, u32[]{:S(2)}) %collective-permute-start.1) | collective-permute-done | bytes 65568 | tf_op jit(solution)/shard_map/ppermute | solution.py:306
  5.4 0.0 copy-done.6
  5.5 0.0 copy-start
  5.5 2.1 %collective-permute-start.3 = (s32[4,24,128]{2,1,0:T(8,128)S(1)}, s32[4,24,128]{2,1,0:T(8,128)S(1)}, u32[]{:S(2)}, u32[]{:S(2)}) collective-permute-start(s32[4,24,128]{2,1,0:T(8,128)S(1)} %get-tuple-element.49), channel_id=1, source_target_pairs={{0,4},{1,5},{2,6},{3,7},{4,0},{5,1},{6,2},{7,3},{8,12},{9,13},{10,... | collective-permute-start | bytes 147464 | tf_op jit(solution)/shard_map/ppermute | solution.py:306
  7.6 0.0 copy-start.4
  7.6 0.0 copy-start.5
  7.6 0.0 collective-permute-start.2
  7.6 0.0 copy-start.1
  7.6 0.0 copy-start.2
  7.6 0.0 copy-start.3
  7.6 0.0 copy-done
  7.6 0.6 %copy-done.4 = s32[64]{0:T(128)S(1)} copy-done((s32[64]{0:T(128)S(1)}, s32[64]{0:T(128)}, u32[]{:S(2)}) %copy-start.4) | copy-done | bytes 280
  8.2 0.0 copy-done.5
  8.3 0.0 copy-done.1
  8.3 0.0 copy-done.2
  8.3 0.0 copy-done.3
  8.3 1.2 %tile.1 = (f32[16,128]{1,0:T(8,128)S(1)}, f32[8,24,128]{2,1,0:T(8,128)S(1)}, f32[8,24,128]{2,1,0:T(8,128)S(1)}, f32[8,24,128]{2,1,0:T(8,128)S(1)}, f32[8,24,128]...) custom-call(s32[8,24,128]{2,1,0:T(8,128)S(1)} %pad_add_fusion.rows_r, ...), custom_call_target="tpu_custom_call" | custom-call | flops 3000000 | bytes 1000000 | tf_op jit(solution)/shard_map/tile/pallas_call | solution.py:697
  9.5 0.3 %collective-permute-done.3 = s32[4,24,128]{2,1,0:T(8,128)S(1)} collective-permute-done((s32[4,24,128]{2,1,0:T(8,128)S(1)}, s32[4,24,128]{2,1,0:T(8,128)S(1)}, u32[]{:S(2)}, u32[]{:S(2)}) %collective-permute-start.3) | collective-permute-done | bytes 49184 | tf_op jit(solution)/shard_map/ppermute | solution.py:306
  9.8 0.0 collective-permute-done.2
  9.8 1.0 %basis.1 = (f32[32,128]{1,0:T(8,128)S(1)}, f32[8,16,128]{2,1,0:T(8,128)S(1)}, f32[8,16,128]{2,1,0:T(8,128)S(1)}, f32[8,16,128]{2,1,0:T(8,128)S(1)}, f32[8,16,128...) custom-call(s32[4,24,128]{2,1,0:T(8,128)S(1)} %get-tuple-element.48.refs_0_, ...), custom_call_target="tpu_custom_call" | custom-call | tf_op jit(solution)/shard_map/basis/pallas_call | solution.py:717
  10.8 14.2 %all_to_all.11 = f32[32,1,128]{2,1,0:T(1,128)S(1)} all-to-all(f32[32,1,128]{2,1,0:T(1,128)S(1)} %bitcast.8), channel_id=1, replica_groups=mesh['gx'=8,'gy'=4] {'gx','gy'}, dimensions={0} | all-to-all | bytes 32768 | tf_op jit(solution)/shard_map/all_to_all | solution.py:728
  25.0 0.9 %pressure.1 = f32[8,16,128]{2,1,0:T(8,128)} custom-call(f32[32,128]{1,0:T(8,128)S(1)} %bitcast.7, f32[8,16,128]{2,1,0:T(8,128)S(1)} %get-tuple-element.39.basis_ref, f32[8,16,128]{2,1,0:T(8,128)S(1)} %get-tuple-element.40.side_ref, f32[8,16,128]{2,1,0:T(8,128)S(1)} %get-tuple-element.41.rhs_ref, f32[8,16,128]{2,1,0:T(8,128)S(1)} %get-tuple-element.42.store_ref, ...), custom_call_target="tpu_custom_call" | custom-call | tf_op jit(solution)/shard_map/pressure/pallas_call | solution.py:729
  (4 shorter events, 0.0 us)
Async XLA Ops:
  0.0 3.0 %collective-permute-start = (s32[8,16,128]{2,1,0:T(8,128)}, s32[8,16,128]{2,1,0:T(8,128)S(1)}, u32[]{:S(2)}, u32[]{:S(2)}) collective-permute-start(s32[8,16,128]{2,1,0:T(8,128)} %param.7), channel_id=1, source_target_pairs={{0,1},{1,0},{2,3},{3,2},{4,5},{5,4},{6,7},{7,6},{8,9},{9,8},{10,11... | collective-permute-start | bytes 196616 | tf_op jit(solution)/shard_map/ppermute | solution.py:306
  0.5 4.9 %collective-permute-start.1 = (s32[8,16,128]{2,1,0:T(8,128)}, s32[8,16,128]{2,1,0:T(8,128)S(1)}, u32[]{:S(2)}, u32[]{:S(2)}) collective-permute-start(s32[8,16,128]{2,1,0:T(8,128)} %param.7), channel_id=1, source_target_pairs={{0,4},{1,2},{2,1},{3,7},{4,0},{5,6},{6,5},{7,3},{8,12},{9,10},{10,... | collective-permute-start | bytes 196616 | tf_op jit(solution)/shard_map/ppermute | solution.py:306
  3.0 2.5 %copy-start.6 = (s32[8,16,128]{2,1,0:T(8,128)S(1)}, s32[8,16,128]{2,1,0:T(8,128)}, u32[]{:S(2)}) copy-start(s32[8,16,128]{2,1,0:T(8,128)} %param.7) | copy-start | bytes 196612
  5.5 2.2 %copy-start = (f32[8,16,128]{2,1,0:T(8,128)S(1)}, f32[8,16,128]{2,1,0:T(8,128)}, u32[]{:S(2)}) copy-start(f32[8,16,128]{2,1,0:T(8,128)} %source_ref.1) | copy-start | bytes 196612
  5.5 4.3 %collective-permute-start.3 = (s32[4,24,128]{2,1,0:T(8,128)S(1)}, s32[4,24,128]{2,1,0:T(8,128)S(1)}, u32[]{:S(2)}, u32[]{:S(2)}) collective-permute-start(s32[4,24,128]{2,1,0:T(8,128)S(1)} %get-tuple-element.49), channel_id=1, source_target_pairs={{0,4},{1,5},{2,6},{3,7},{4,0},{5,1},{6,2},{7,3},{8,12},{9,13},{10,... | collective-permute-start | bytes 147464 | tf_op jit(solution)/shard_map/ppermute | solution.py:306
  7.6 0.7 %copy-start.4 = (s32[64]{0:T(128)S(1)}, s32[64]{0:T(128)}, u32[]{:S(2)}) copy-start(s32[64]{0:T(128)} %param.12) | copy-start | bytes 772
  7.6 0.7 %copy-start.5 = (f32[64]{0:T(128)S(1)}, f32[64]{0:T(128)}, u32[]{:S(2)}) copy-start(f32[64]{0:T(128)} %param.13) | copy-start | bytes 772
  7.6 2.2 %collective-permute-start.2 = (s32[4,24,128]{2,1,0:T(8,128)S(1)}, s32[4,24,128]{2,1,0:T(8,128)S(1)}, u32[]{:S(2)}, u32[]{:S(2)}) collective-permute-start(s32[4,24,128]{2,1,0:T(8,128)S(1)} %get-tuple-element.50), channel_id=1, source_target_pairs={{0,1},{1,0},{2,3},{3,2},{4,8},{5,9},{6,10},{7,11},{8,4},{9,5},{10,... | collective-permute-start | bytes 147464 | tf_op jit(solution)/shard_map/ppermute | solution.py:306
  7.6 0.7 %copy-start.1 = (f32[8]{0:T(128)S(1)}, f32[8]{0:T(128)}, u32[]{:S(2)}) copy-start(f32[8]{0:T(128)} %perm_ref.1) | copy-start | bytes 100
  7.6 0.7 %copy-start.2 = (f32[8]{0:T(128)S(1)}, f32[8]{0:T(128)}, u32[]{:S(2)}) copy-start(f32[8]{0:T(128)} %store_ref.1) | copy-start | bytes 100
  7.6 0.7 %copy-start.3 = (s32[64]{0:T(128)S(1)}, s32[64]{0:T(128)}, u32[]{:S(2)}) copy-start(s32[64]{0:T(128)} %param.11) | copy-start | bytes 772

commit v6 on v4

--- a/solution.py
+++ b/solution.py
@@ -306,14 +306,24 @@
     return lax.ppermute(value, AXES, pairs)
 
 
-def pair_swaps(value, dim, axis, width):
-    length = value.shape[dim]
-    last = lax.slice_in_dim(value, length - width, length, axis=dim)
-    first = lax.slice_in_dim(value, 0, width, axis=dim)
-    even = lax.axis_index(axis) % 2 == 0
-    far = swap_along(jnp.where(even, first, last), axis, 1)
-    near = swap_along(jnp.where(even, last, first), axis, 0)
-    return jnp.where(even, far, near), jnp.where(even, near, far)
+def wide_tile(facies):
+    count = facies.shape[0]
+    even_x, even_y = (lax.axis_index(axis) % 2 == 0 for axis in AXES)
+
+    def end_planes(value, at_first):
+        return jnp.where(at_first, value[:MARGIN], value[count - MARGIN :])
+
+    far = swap_along(facies, "gy", 1)
+    near = swap_along(facies, "gy", 0)
+    beside = swap_along(end_planes(facies, ~even_x), "gx", 0)
+    before = jnp.where(even_y, far[:, -MARGIN:], near[:, -MARGIN:])
+    after = jnp.where(even_y, near[:, :MARGIN], far[:, :MARGIN])
+    rest = jnp.concatenate([after, before], axis=1)
+    own = jnp.concatenate([facies, rest], axis=1)
+    far = swap_along(end_planes(own, even_x), "gx", 1)
+    corners = swap_along(end_planes(rest, ~even_x), "gx", 0)
+    near = jnp.concatenate([beside, corners], axis=1)
+    return own, jnp.where(even_x, far, near), jnp.where(even_x, near, far)
 
 
 def lane_iota(shape):
@@ -687,9 +697,7 @@
     smem = pl.BlockSpec(memory_space=pltpu.SMEM)
     params = pltpu.CompilerParams(vmem_limit_bytes=VMEM_BYTES)
 
-    before, after = pair_swaps(facies, 1, "gy", MARGIN)
-    own = jnp.concatenate([facies, after, before], axis=1)
-    before, after = pair_swaps(own, 0, "gx", MARGIN)
+    own, before, after = wide_tile(facies)
     near = pl.pallas_call(
         tile_kernel,
         out_shape=(jax.ShapeDtypeStruct((2 * facies_perm.shape[0], layers), f32),)

time: 26.3 us -> 27.3 us (1.038)
  waiting for transfers between devices: 2.04 us -> 4.07 us
  blocking collectives: 14.2 us -> 13.2 us
    ppermute x4 -> x5, waiting for transfers between devices: 2.04 us -> 4.07 us  [swap_along(): return lax.ppermute(value, AXES, pairs)]
    all_to_all x1, blocking collectives: 14.2 us -> 13.2 us  [column_step(): everyone = lax.all_to_all(copies, AXES, 0, 0, tiled=True)]
    ppermute x4 -> x5, starting transfers between devices: 5.2 us -> 5.09 us  [swap_along(): return lax.ppermute(value, AXES, pairs)]
    select_n x4 -> x5, other arithmetic: 0.81 us -> 0.88 us  [the longest x3 0.86 us: end_planes(): return jnp.where(at_first, value[:MARGIN], value[count - MARGIN:])]
    unnamed x14 -> x15, local copies, waits for them, and re-layouts: 0.67 us -> 0.69 us
  transfers between devices with their start and end apart: 4 -> 5, of which waited for: 2 -> 3; matrix products, arithmetic and copies ran while one was open for 0% -> 0% of each run, Pallas kernels for 4% -> 4%
where the time goes in v6:
time: 27.3 us; the launch traced here: 27.1 us
  blocking collectives  13.2 us (48%)
  starting transfers between devices  5.09 us (19%)
  waiting for transfers between devices  4.07 us (15%)
  Pallas kernels  3.1 us (11%)
  other arithmetic  0.9 us (3%)
  local copies, waits for them, and re-layouts  0.69 us (3%)
    all_to_all x1, blocking collectives, column_step(): everyone = lax.all_to_all(copies, AXES, 0, 0, tiled=True)  13.2 us
    ppermute x5, starting transfers between devices, swap_along(): return lax.ppermute(value, AXES, pairs)  5.09 us
    ppermute x5, waiting for transfers between devices, swap_along(): return lax.ppermute(value, AXES, pairs)  4.07 us
    pallas_call x1, Pallas kernels, column_step(): pl.pallas_call(tile_kernel, out_shape=(jax.ShapeDtypeStruct((2 * facies_p...  1.16 us
    pallas_call x1, Pallas kernels, column_step(): pl.pallas_call(basis_kernel, out_shape=(jax.ShapeDtypeStruct((size, layer...  1.05 us
    pallas_call x1, Pallas kernels, column_step(): pl.pallas_call(pressure_kernel, out_shape=tile, in_specs=[vmem] * 7, out_...  0.89 us
    select_n x3, other arithmetic, end_planes(): return jnp.where(at_first, value[:MARGIN], value[count - MARGIN:])  0.86 us
    unnamed x15, local copies, waits for them, and re-layouts  0.69 us
  transfers between devices with their start and end apart: 5, of which 3 were waited for; matrix products, arithmetic and copies ran while one was open for 0% of the time, Pallas kernels for 4%

profile of v6, /device:TPU:0, one launch (start us, length us, event | category | flops | bytes accessed | tf_op | source)
XLA Modules:
  0.0 27.1 jit_solution(4268892345647985177)
XLA Ops:
  0.0 0.0 copy-start.6
  0.0 0.8 %slice_select_fusion.1 = s32[4,16,128]{2,1,0:T(8,128)S(1)} fusion(s32[8,16,128]{2,1,0:T(8,128)} %param.7, pred[]{:T(512)S(6)} %not.4), kind=kLoop, calls=%fused_computation.4 | loop fusion | flops 8192 | bytes 98305 | tf_op jit(solution)/shard_map/jit(_where)/select_n | solution.py:314
  0.8 3.0 %collective-permute-start.3 = (s32[4,16,128]{2,1,0:T(8,128)S(1)}, s32[4,16,128]{2,1,0:T(8,128)S(1)}, u32[]{:S(2)}, u32[]{:S(2)}) collective-permute-start(s32[4,16,128]{2,1,0:T(8,128)S(1)} %slice_select_fusion.1), channel_id=1, source_target_pairs={{0,4},{1,5},{2,6},{3,7},{4,0},{5,1},{6,2},{7,3},{8,12},{9,13},{10,... | collective-permute-start | bytes 98312 | tf_op jit(solution)/shard_map/ppermute | solution.py:306
  3.8 0.0 copy-done.6
  3.8 0.1 collective-permute-start.1
  3.9 1.6 %collective-permute-start = (s32[8,16,128]{2,1,0:T(8,128)S(1)}, s32[8,16,128]{2,1,0:T(8,128)S(1)}, u32[]{:S(2)}, u32[]{:S(2)}) collective-permute-start(s32[8,16,128]{2,1,0:T(8,128)S(1)} %copy-done.6), channel_id=1, source_target_pairs={{0,1},{1,0},{2,3},{3,2},{4,5},{5,4},{6,7},{7,6},{8,9},{9,8},{10,11... | collective-permute-start | bytes 196616 | tf_op jit(solution)/shard_map/ppermute | solution.py:306
  5.4 0.3 collective-permute-done.3
  5.7 2.4 %collective-permute-done.1 = s32[8,16,128]{2,1,0:T(8,128)S(1)} collective-permute-done((s32[8,16,128]{2,1,0:T(8,128)S(1)}, s32[8,16,128]{2,1,0:T(8,128)S(1)}, u32[]{:S(2)}, u32[]{:S(2)}) %collective-permute-start.1) | collective-permute-done | bytes 65568 | tf_op jit(solution)/shard_map/ppermute | solution.py:306
  8.1 0.0 collective-permute-done
  8.1 0.0 copy-start
  8.2 0.4 %collective-permute-start.4 = (s32[4,8,128]{2,1,0:T(8,128)S(1)}, s32[4,8,128]{2,1,0:T(8,128)S(1)}, u32[]{:S(2)}, u32[]{:S(2)}) collective-permute-start(s32[4,8,128]{2,1,0:T(8,128)S(1)} %fusion.1), channel_id=1, source_target_pairs={{0,4},{1,5},{2,6},{3,7},{4,0},{5,1},{6,2},{7,3},{8,12},{9,13},{10,... | collective-permute-start | bytes 49160 | tf_op jit(solution)/shard_map/ppermute | solution.py:306
  8.6 0.0 copy-start.4
  8.6 0.0 copy-start.5
  8.6 0.1 collective-permute-start.2
  8.7 0.0 copy-start.1
  8.7 0.0 copy-start.2
  8.7 0.0 copy-start.3
  8.7 0.3 %copy-done = f32[8,16,128]{2,1,0:T(8,128)S(1)} copy-done((f32[8,16,128]{2,1,0:T(8,128)S(1)}, f32[8,16,128]{2,1,0:T(8,128)}, u32[]{:S(2)}) %copy-start) | copy-done | bytes 65560
  9.0 0.2 copy-done.4
  9.2 0.0 copy-done.5
  9.2 0.1 copy-done.1
  9.3 0.0 copy-done.2
  9.3 0.0 copy-done.3
  9.4 1.2 %tile.1 = (f32[16,128]{1,0:T(8,128)S(1)}, f32[8,24,128]{2,1,0:T(8,128)S(1)}, f32[8,24,128]{2,1,0:T(8,128)S(1)}, f32[8,24,128]{2,1,0:T(8,128)S(1)}, f32[8,24,128]...) custom-call(s32[8,24,128]{2,1,0:T(8,128)S(1)} %pad_add_fusion.rows_r, ...), custom_call_target="tpu_custom_call" | custom-call | flops 3000000 | bytes 1000000 | tf_op jit(solution)/shard_map/tile/pallas_call | solution.py:701
  10.5 1.4 %collective-permute-done.4 = s32[4,8,128]{2,1,0:T(8,128)S(1)} collective-permute-done((s32[4,8,128]{2,1,0:T(8,128)S(1)}, s32[4,8,128]{2,1,0:T(8,128)S(1)}, u32[]{:S(2)}, u32[]{:S(2)}) %collective-permute-start.4) | collective-permute-done | bytes 16416 | tf_op jit(solution)/shard_map/ppermute | solution.py:306
  12.0 0.0 collective-permute-done.2
  12.0 1.0 %basis.1 = (f32[32,128]{1,0:T(8,128)S(1)}, f32[8,16,128]{2,1,0:T(8,128)S(1)}, f32[8,16,128]{2,1,0:T(8,128)S(1)}, f32[8,16,128]{2,1,0:T(8,128)S(1)}, f32[8,16,128...) custom-call(s32[4,24,128]{2,1,0:T(8,128)S(1)} %get-tuple-element.48.refs_0_, ...), custom_call_target="tpu_custom_call" | custom-call | tf_op jit(solution)/shard_map/basis/pallas_call | solution.py:721
  13.0 13.2 %all_to_all.11 = f32[32,1,128]{2,1,0:T(1,128)S(1)} all-to-all(f32[32,1,128]{2,1,0:T(1,128)S(1)} %bitcast.8), channel_id=1, replica_groups=mesh['gx'=8,'gy'=4] {'gx','gy'}, dimensions={0} | all-to-all | bytes 32768 | tf_op jit(solution)/shard_map/all_to_all | solution.py:732
  26.2 0.9 %pressure.1 = f32[8,16,128]{2,1,0:T(8,128)} custom-call(f32[32,128]{1,0:T(8,128)S(1)} %bitcast.7, f32[8,16,128]{2,1,0:T(8,128)S(1)} %get-tuple-element.39.basis_ref, f32[8,16,128]{2,1,0:T(8,128)S(1)} %get-tuple-element.40.side_ref, f32[8,16,128]{2,1,0:T(8,128)S(1)} %get-tuple-element.41.rhs_ref, f32[8,16,128]{2,1,0:T(8,128)S(1)} %get-tuple-element.42.store_ref, ...), custom_call_target="tpu_custom_call" | custom-call | tf_op jit(solution)/shard_map/pressure/pallas_call | solution.py:733
  (7 shorter events, 0.1 us)
Async XLA Ops:
  0.0 3.8 %copy-start.6 = (s32[8,16,128]{2,1,0:T(8,128)S(1)}, s32[8,16,128]{2,1,0:T(8,128)}, u32[]{:S(2)}) copy-start(s32[8,16,128]{2,1,0:T(8,128)} %param.7) | copy-start | bytes 196612
  0.8 4.9 %collective-permute-start.3 = (s32[4,16,128]{2,1,0:T(8,128)S(1)}, s32[4,16,128]{2,1,0:T(8,128)S(1)}, u32[]{:S(2)}, u32[]{:S(2)}) collective-permute-start(s32[4,16,128]{2,1,0:T(8,128)S(1)} %slice_select_fusion.1), channel_id=1, source_target_pairs={{0,4},{1,5},{2,6},{3,7},{4,0},{5,1},{6,2},{7,3},{8,12},{9,13},{10,... | collective-permute-start | bytes 98312 | tf_op jit(solution)/shard_map/ppermute | solution.py:306
  3.8 4.3 %collective-permute-start.1 = (s32[8,16,128]{2,1,0:T(8,128)S(1)}, s32[8,16,128]{2,1,0:T(8,128)S(1)}, u32[]{:S(2)}, u32[]{:S(2)}) collective-permute-start(s32[8,16,128]{2,1,0:T(8,128)S(1)} %copy-done.6), channel_id=1, source_target_pairs={{0,4},{1,2},{2,1},{3,7},{4,0},{5,6},{6,5},{7,3},{8,12},{9,10},{10,... | collective-permute-start | bytes 196616 | tf_op jit(solution)/shard_map/ppermute | solution.py:306
  3.9 4.2 %collective-permute-start = (s32[8,16,128]{2,1,0:T(8,128)S(1)}, s32[8,16,128]{2,1,0:T(8,128)S(1)}, u32[]{:S(2)}, u32[]{:S(2)}) collective-permute-start(s32[8,16,128]{2,1,0:T(8,128)S(1)} %copy-done.6), channel_id=1, source_target_pairs={{0,1},{1,0},{2,3},{3,2},{4,5},{5,4},{6,7},{7,6},{8,9},{9,8},{10,11... | collective-permute-start | bytes 196616 | tf_op jit(solution)/shard_map/ppermute | solution.py:306
  8.1 0.8 %copy-start = (f32[8,16,128]{2,1,0:T(8,128)S(1)}, f32[8,16,128]{2,1,0:T(8,128)}, u32[]{:S(2)}) copy-start(f32[8,16,128]{2,1,0:T(8,128)} %source_ref.1) | copy-start | bytes 196612
  8.2 3.8 %collective-permute-start.4 = (s32[4,8,128]{2,1,0:T(8,128)S(1)}, s32[4,8,128]{2,1,0:T(8,128)S(1)}, u32[]{:S(2)}, u32[]{:S(2)}) collective-permute-start(s32[4,8,128]{2,1,0:T(8,128)S(1)} %fusion.1), channel_id=1, source_target_pairs={{0,4},{1,5},{2,6},{3,7},{4,0},{5,1},{6,2},{7,3},{8,12},{9,13},{10,... | collective-permute-start | bytes 49160 | tf_op jit(solution)/shard_map/ppermute | solution.py:306
  8.6 0.7 %copy-start.4 = (s32[64]{0:T(128)S(1)}, s32[64]{0:T(128)}, u32[]{:S(2)}) copy-start(s32[64]{0:T(128)} %param.12) | copy-start | bytes 772
  8.6 0.7 %copy-start.5 = (f32[64]{0:T(128)S(1)}, f32[64]{0:T(128)}, u32[]{:S(2)}) copy-start(f32[64]{0:T(128)} %param.13) | copy-start | bytes 772
  8.6 3.4 %collective-permute-start.2 = (s32[4,24,128]{2,1,0:T(8,128)S(1)}, s32[4,24,128]{2,1,0:T(8,128)S(1)}, u32[]{:S(2)}, u32[]{:S(2)}) collective-permute-start(s32[4,24,128]{2,1,0:T(8,128)S(1)} %slice_select_fusion), channel_id=1, source_target_pairs={{0,1},{1,0},{2,3},{3,2},{4,8},{5,9},{6,10},{7,11},{8,4},{9,5},{10,... | collective-permute-start | bytes 147464 | tf_op jit(solution)/shard_map/ppermute | solution.py:306
  8.7 0.7 %copy-start.1 = (f32[8]{0:T(128)S(1)}, f32[8]{0:T(128)}, u32[]{:S(2)}) copy-start(f32[8]{0:T(128)} %perm_ref.1) | copy-start | bytes 100
  8.7 0.7 %copy-start.2 = (f32[8]{0:T(128)S(1)}, f32[8]{0:T(128)}, u32[]{:S(2)}) copy-start(f32[8]{0:T(128)} %store_ref.1) | copy-start | bytes 100
  8.7 0.7 %copy-start.3 = (s32[64]{0:T(128)S(1)}, s32[64]{0:T(128)}, u32[]{:S(2)}) copy-start(s32[64]{0:T(128)} %param.11) | copy-start | bytes 772

commit v7 on v6

--- a/solution.py
+++ b/solution.py
@@ -598,13 +598,13 @@
     sums_ref[2:3] = mass_01 - energy + (low_high - low_2) + down(low_high - high_2, 1)
     sums_ref[3:4] = -low_high
     sums_ref[6:8] = jnp.zeros((2, layers), jnp.float32)
-    window = pltpu.roll(sums_ref[...], 0, 1, stride=1, stride_axis=0)
-    width = 1
-    while width < BLOCK_Z:
-        window = window + pltpu.roll(window, width, 1)
-        width *= 2
+    line = lax.broadcasted_iota(jnp.int32, (layers, layers), 0)
+    lane = lane_iota((layers, layers))
+    segment = lambda at: lax.rem(at + BLOCK_Z // 2, layers) // BLOCK_Z
+    same = jnp.where(segment(line) == segment(lane), 1.0, 0.0)
+    window = jnp.dot(sums_ref[...], same, precision=HIGHEST, preferred_element_type=jnp.float32)
     row = lax.broadcasted_iota(jnp.int32, window.shape, 0)
-    keep = lax.rem(lane_iota(window.shape) + layers - BLOCK_Z // 2 + 1 - row, BLOCK_Z) == 0
+    keep = lax.rem(lane_iota(window.shape), BLOCK_Z) == row
     packed = jnp.sum(jnp.where(keep, window, 0.0), axis=0, keepdims=True)
     packed_ref[...] = jnp.broadcast_to(packed, packed_ref.shape)
 
@@ -653,7 +653,7 @@
     packed = jnp.sum(rows_ref[...], axis=0, keepdims=True)
 
     def held(segment, kind):
-        return layer == lax.rem(segment * BLOCK_Z + half - 1 + kind, layers)
+        return layer == lax.rem(segment * BLOCK_Z + kind, layers)
 
     parity = lax.rem(node, 2)
     own = held(node, parity) | held(node + 1, parity)

time: 27.3 us -> 27.1 us (level)
  no operation moved by 1% of the time
where the time goes in v7:
time: 27.1 us; the launch traced here: 26.9 us
  blocking collectives  13.2 us (49%)
  starting transfers between devices  5.09 us (19%)
  waiting for transfers between devices  4.07 us (15%)
  Pallas kernels  2.91 us (11%)
  other arithmetic  0.9 us (3%)
  local copies, waits for them, and re-layouts  0.69 us (3%)
    all_to_all x1, blocking collectives, column_step(): everyone = lax.all_to_all(copies, AXES, 0, 0, tiled=True)  13.2 us
    ppermute x5, starting transfers between devices, swap_along(): return lax.ppermute(value, AXES, pairs)  5.09 us
    ppermute x5, waiting for transfers between devices, swap_along(): return lax.ppermute(value, AXES, pairs)  4.07 us
    pallas_call x1, Pallas kernels, column_step(): pl.pallas_call(tile_kernel, out_shape=(jax.ShapeDtypeStruct((2 * facies_p...  1.16 us
    pallas_call x1, Pallas kernels, column_step(): pl.pallas_call(pressure_kernel, out_shape=tile, in_specs=[vmem] * 7, out_...  0.89 us
    pallas_call x1, Pallas kernels, column_step(): pl.pallas_call(basis_kernel, out_shape=(jax.ShapeDtypeStruct((size, layer...  0.86 us
    select_n x3, other arithmetic, end_planes(): return jnp.where(at_first, value[:MARGIN], value[count - MARGIN:])  0.86 us
    unnamed x15, local copies, waits for them, and re-layouts  0.69 us
  transfers between devices with their start and end apart: 5, of which 3 were waited for; matrix products, arithmetic and copies ran while one was open for 0% of the time, Pallas kernels for 4%

profile of v7, /device:TPU:0, one launch (start us, length us, event | category | flops | bytes accessed | tf_op | source)
XLA Modules:
  0.0 26.9 jit_solution(6949601859447132433)
XLA Ops:
  0.0 0.0 copy-start.6
  0.0 0.8 %slice_select_fusion.1 = s32[4,16,128]{2,1,0:T(8,128)S(1)} fusion(s32[8,16,128]{2,1,0:T(8,128)} %param.7, pred[]{:T(512)S(6)} %not.4), kind=kLoop, calls=%fused_computation.4 | loop fusion | flops 8192 | bytes 98305 | tf_op jit(solution)/shard_map/jit(_where)/select_n | solution.py:314
  0.8 3.0 %collective-permute-start.3 = (s32[4,16,128]{2,1,0:T(8,128)S(1)}, s32[4,16,128]{2,1,0:T(8,128)S(1)}, u32[]{:S(2)}, u32[]{:S(2)}) collective-permute-start(s32[4,16,128]{2,1,0:T(8,128)S(1)} %slice_select_fusion.1), channel_id=1, source_target_pairs={{0,4},{1,5},{2,6},{3,7},{4,0},{5,1},{6,2},{7,3},{8,12},{9,13},{10,... | collective-permute-start | bytes 98312 | tf_op jit(solution)/shard_map/ppermute | solution.py:306
  3.8 0.0 copy-done.6
  3.8 0.1 collective-permute-start.1
  3.9 1.6 %collective-permute-start = (s32[8,16,128]{2,1,0:T(8,128)S(1)}, s32[8,16,128]{2,1,0:T(8,128)S(1)}, u32[]{:S(2)}, u32[]{:S(2)}) collective-permute-start(s32[8,16,128]{2,1,0:T(8,128)S(1)} %copy-done.6), channel_id=1, source_target_pairs={{0,1},{1,0},{2,3},{3,2},{4,5},{5,4},{6,7},{7,6},{8,9},{9,8},{10,11... | collective-permute-start | bytes 196616 | tf_op jit(solution)/shard_map/ppermute | solution.py:306
  5.4 0.3 collective-permute-done.3
  5.7 2.4 %collective-permute-done.1 = s32[8,16,128]{2,1,0:T(8,128)S(1)} collective-permute-done((s32[8,16,128]{2,1,0:T(8,128)S(1)}, s32[8,16,128]{2,1,0:T(8,128)S(1)}, u32[]{:S(2)}, u32[]{:S(2)}) %collective-permute-start.1) | collective-permute-done | bytes 65568 | tf_op jit(solution)/shard_map/ppermute | solution.py:306
  8.1 0.0 collective-permute-done
  8.1 0.0 copy-start
  8.2 0.4 %collective-permute-start.4 = (s32[4,8,128]{2,1,0:T(8,128)S(1)}, s32[4,8,128]{2,1,0:T(8,128)S(1)}, u32[]{:S(2)}, u32[]{:S(2)}) collective-permute-start(s32[4,8,128]{2,1,0:T(8,128)S(1)} %fusion.1), channel_id=1, source_target_pairs={{0,4},{1,5},{2,6},{3,7},{4,0},{5,1},{6,2},{7,3},{8,12},{9,13},{10,... | collective-permute-start | bytes 49160 | tf_op jit(solution)/shard_map/ppermute | solution.py:306
  8.6 0.0 copy-start.4
  8.6 0.0 copy-start.5
  8.6 0.1 collective-permute-start.2
  8.7 0.0 copy-start.1
  8.7 0.0 copy-start.2
  8.7 0.0 copy-start.3
  8.7 0.3 %copy-done = f32[8,16,128]{2,1,0:T(8,128)S(1)} copy-done((f32[8,16,128]{2,1,0:T(8,128)S(1)}, f32[8,16,128]{2,1,0:T(8,128)}, u32[]{:S(2)}) %copy-start) | copy-done | bytes 65560
  9.0 0.2 copy-done.4
  9.2 0.0 copy-done.5
  9.2 0.1 copy-done.1
  9.3 0.0 copy-done.2
  9.3 0.0 copy-done.3
  9.4 1.2 %tile.1 = (f32[16,128]{1,0:T(8,128)S(1)}, f32[8,24,128]{2,1,0:T(8,128)S(1)}, f32[8,24,128]{2,1,0:T(8,128)S(1)}, f32[8,24,128]{2,1,0:T(8,128)S(1)}, f32[8,24,128]...) custom-call(s32[8,24,128]{2,1,0:T(8,128)S(1)} %pad_add_fusion.rows_r, ...), custom_call_target="tpu_custom_call" | custom-call | flops 3000000 | bytes 1000000 | tf_op jit(solution)/shard_map/tile/pallas_call | solution.py:701
  10.5 1.4 %collective-permute-done.4 = s32[4,8,128]{2,1,0:T(8,128)S(1)} collective-permute-done((s32[4,8,128]{2,1,0:T(8,128)S(1)}, s32[4,8,128]{2,1,0:T(8,128)S(1)}, u32[]{:S(2)}, u32[]{:S(2)}) %collective-permute-start.4) | collective-permute-done | bytes 16416 | tf_op jit(solution)/shard_map/ppermute | solution.py:306
  12.0 0.0 collective-permute-done.2
  12.0 0.9 %basis.1 = (f32[32,128]{1,0:T(8,128)S(1)}, f32[8,16,128]{2,1,0:T(8,128)S(1)}, f32[8,16,128]{2,1,0:T(8,128)S(1)}, f32[8,16,128]{2,1,0:T(8,128)S(1)}, f32[8,16,128...) custom-call(s32[4,24,128]{2,1,0:T(8,128)S(1)} %get-tuple-element.48.refs_0_, ...), custom_call_target="tpu_custom_call" | custom-call | tf_op jit(solution)/shard_map/basis/pallas_call | solution.py:721
  12.8 13.2 %all_to_all.11 = f32[32,1,128]{2,1,0:T(1,128)S(1)} all-to-all(f32[32,1,128]{2,1,0:T(1,128)S(1)} %bitcast.8), channel_id=1, replica_groups=mesh['gx'=8,'gy'=4] {'gx','gy'}, dimensions={0} | all-to-all | bytes 32768 | tf_op jit(solution)/shard_map/all_to_all | solution.py:732
  26.0 0.9 %pressure.1 = f32[8,16,128]{2,1,0:T(8,128)} custom-call(f32[32,128]{1,0:T(8,128)S(1)} %bitcast.7, f32[8,16,128]{2,1,0:T(8,128)S(1)} %get-tuple-element.39.basis_ref, f32[8,16,128]{2,1,0:T(8,128)S(1)} %get-tuple-element.40.side_ref, f32[8,16,128]{2,1,0:T(8,128)S(1)} %get-tuple-element.41.rhs_ref, f32[8,16,128]{2,1,0:T(8,128)S(1)} %get-tuple-element.42.store_ref, ...), custom_call_target="tpu_custom_call" | custom-call | tf_op jit(solution)/shard_map/pressure/pallas_call | solution.py:733
  (7 shorter events, 0.1 us)
Async XLA Ops:
  0.0 3.8 %copy-start.6 = (s32[8,16,128]{2,1,0:T(8,128)S(1)}, s32[8,16,128]{2,1,0:T(8,128)}, u32[]{:S(2)}) copy-start(s32[8,16,128]{2,1,0:T(8,128)} %param.7) | copy-start | bytes 196612
  0.8 4.9 %collective-permute-start.3 = (s32[4,16,128]{2,1,0:T(8,128)S(1)}, s32[4,16,128]{2,1,0:T(8,128)S(1)}, u32[]{:S(2)}, u32[]{:S(2)}) collective-permute-start(s32[4,16,128]{2,1,0:T(8,128)S(1)} %slice_select_fusion.1), channel_id=1, source_target_pairs={{0,4},{1,5},{2,6},{3,7},{4,0},{5,1},{6,2},{7,3},{8,12},{9,13},{10,... | collective-permute-start | bytes 98312 | tf_op jit(solution)/shard_map/ppermute | solution.py:306
  3.8 4.3 %collective-permute-start.1 = (s32[8,16,128]{2,1,0:T(8,128)S(1)}, s32[8,16,128]{2,1,0:T(8,128)S(1)}, u32[]{:S(2)}, u32[]{:S(2)}) collective-permute-start(s32[8,16,128]{2,1,0:T(8,128)S(1)} %copy-done.6), channel_id=1, source_target_pairs={{0,4},{1,2},{2,1},{3,7},{4,0},{5,6},{6,5},{7,3},{8,12},{9,10},{10,... | collective-permute-start | bytes 196616 | tf_op jit(solution)/shard_map/ppermute | solution.py:306
  3.9 4.2 %collective-permute-start = (s32[8,16,128]{2,1,0:T(8,128)S(1)}, s32[8,16,128]{2,1,0:T(8,128)S(1)}, u32[]{:S(2)}, u32[]{:S(2)}) collective-permute-start(s32[8,16,128]{2,1,0:T(8,128)S(1)} %copy-done.6), channel_id=1, source_target_pairs={{0,1},{1,0},{2,3},{3,2},{4,5},{5,4},{6,7},{7,6},{8,9},{9,8},{10,11... | collective-permute-start | bytes 196616 | tf_op jit(solution)/shard_map/ppermute | solution.py:306
  8.1 0.8 %copy-start = (f32[8,16,128]{2,1,0:T(8,128)S(1)}, f32[8,16,128]{2,1,0:T(8,128)}, u32[]{:S(2)}) copy-start(f32[8,16,128]{2,1,0:T(8,128)} %source_ref.1) | copy-start | bytes 196612
  8.2 3.8 %collective-permute-start.4 = (s32[4,8,128]{2,1,0:T(8,128)S(1)}, s32[4,8,128]{2,1,0:T(8,128)S(1)}, u32[]{:S(2)}, u32[]{:S(2)}) collective-permute-start(s32[4,8,128]{2,1,0:T(8,128)S(1)} %fusion.1), channel_id=1, source_target_pairs={{0,4},{1,5},{2,6},{3,7},{4,0},{5,1},{6,2},{7,3},{8,12},{9,13},{10,... | collective-permute-start | bytes 49160 | tf_op jit(solution)/shard_map/ppermute | solution.py:306
  8.6 0.7 %copy-start.4 = (s32[64]{0:T(128)S(1)}, s32[64]{0:T(128)}, u32[]{:S(2)}) copy-start(s32[64]{0:T(128)} %param.12) | copy-start | bytes 772
  8.6 0.7 %copy-start.5 = (f32[64]{0:T(128)S(1)}, f32[64]{0:T(128)}, u32[]{:S(2)}) copy-start(f32[64]{0:T(128)} %param.13) | copy-start | bytes 772
  8.6 3.4 %collective-permute-start.2 = (s32[4,24,128]{2,1,0:T(8,128)S(1)}, s32[4,24,128]{2,1,0:T(8,128)S(1)}, u32[]{:S(2)}, u32[]{:S(2)}) collective-permute-start(s32[4,24,128]{2,1,0:T(8,128)S(1)} %slice_select_fusion), channel_id=1, source_target_pairs={{0,1},{1,0},{2,3},{3,2},{4,8},{5,9},{6,10},{7,11},{8,4},{9,5},{10,... | collective-permute-start | bytes 147464 | tf_op jit(solution)/shard_map/ppermute | solution.py:306
  8.7 0.7 %copy-start.1 = (f32[8]{0:T(128)S(1)}, f32[8]{0:T(128)}, u32[]{:S(2)}) copy-start(f32[8]{0:T(128)} %perm_ref.1) | copy-start | bytes 100
  8.7 0.7 %copy-start.2 = (f32[8]{0:T(128)S(1)}, f32[8]{0:T(128)}, u32[]{:S(2)}) copy-start(f32[8]{0:T(128)} %store_ref.1) | copy-start | bytes 100
  8.7 0.7 %copy-start.3 = (s32[64]{0:T(128)S(1)}, s32[64]{0:T(128)}, u32[]{:S(2)}) copy-start(s32[64]{0:T(128)} %param.11) | copy-start | bytes 772

commit v8 on v7

--- a/solution.py
+++ b/solution.py
@@ -284,6 +284,7 @@
 
 
 MARGIN = SWEEPS + 1
+FACES = 6
 AXES = ("gx", "gy")
 VMEM_BYTES = 16 * 2**20
 
@@ -359,9 +360,11 @@
     layer = lane_iota(resist.shape)
     y_face = jnp.where(face_y, 2.0 / (resist + up(resist, 0)), 0.0)
     z_face = jnp.where(layer == resist.shape[1] - 1, 0.0, 2.0 / (resist + up(resist, 1)))
-    part = store + y_face + down(y_face, 0) + z_face + down(z_face, 1)
     z_faces = [jnp.where(face_ends(layer, parity), 0.0, z_face) for parity in (0, 1)]
-    return y_face, z_faces[0], z_faces[1], part
+    faces = (y_face, *z_faces)
+    before = (down(y_face, 0), *(down(value, 1) for value in z_faces))
+    part = store + y_face + before[0] + z_face + jnp.maximum(before[1], before[2])
+    return faces + before, part
 
 
 def y_face_mask(shape, tile_y):
@@ -371,7 +374,7 @@
     return inside & (row != tile_y + MARGIN - 1)
 
 
-def sweep_planes(low, high, read, write, face_x, face_y, face_z, scale):
+def sweep_planes(low, high, read, write, face_x, faces_of, scale):
     if low >= high:
         return
     here = read(low)
@@ -379,13 +382,13 @@
     for plane in range(low, high):
         beyond = read(plane + 1)
         flux = face_x(plane) * (beyond - here)
-        flux_y = face_y(plane) * (up(here, 0) - here)
-        above = up(here, 1)
-        gain = above * (1.0 - here)
-        loss = here * (1.0 - above)
-        z0, z1 = face_z(plane)
-        total = (flux - flux_before) + (flux_y - down(flux_y, 0))
-        total = total + (z0 * gain - z1 * loss) + down(z0 * loss - z1 * gain, 1)
+        y_after, z0_after, z1_after, y_before, z0_before, z1_before = faces_of(plane)
+        above, below = (up(here, 1), down(here, 1))
+        other = 1.0 - here
+        total = flux - flux_before
+        total = total + (y_after * (up(here, 0) - here) + y_before * (down(here, 0) - here))
+        total = total + (z0_after * (above * other) - z1_after * (here * (1.0 - above)))
+        total = total + (z0_before * (below * other) - z1_before * (here * (1.0 - below)))
         write(plane, here + scale(plane) * total)
         here, flux_before = (beyond, flux)
 
@@ -396,8 +399,7 @@
 
 def tile_kernel(
     rows_ref, source_ref, perm_ref, store_ref, well_x_ref, well_y_ref, well_rate_ref,
-    table_ref, resist_ref, storage_ref, x_ref, y_ref, z0_ref, z1_ref, part_ref, scale_ref, rhs_ref,
-    *field_refs,
+    table_ref, rhs_ref, resist_ref, storage_ref, x_ref, part_ref, scale_ref, *more_refs,
 ):
     tile_x, rows, layers = rows_ref.shape
     tile_y = source_ref.shape[1]
@@ -411,6 +413,7 @@
     for code in range(codes):
         table_ref[code : code + 1] = resists[code]
         table_ref[codes + code : codes + code + 1] = stores[code]
+    face_refs, field_refs = (more_refs[:FACES], more_refs[FACES:])
     face_y = y_face_mask((rows, layers), tile_y)
     hit_y = (
         lax.broadcasted_iota(jnp.int32, (tile_y, well_y_ref.shape[1]), 0) + anchor_y
@@ -420,12 +423,11 @@
     for plane in range(tile_x):
         resist = code_select(resists, rows_ref[plane])
         store = code_select(stores, rows_ref[plane])
-        y_face, z0, z1, part = plane_faces(resist, store, face_y)
+        faces, part = plane_faces(resist, store, face_y)
         resist_ref[plane] = resist
         storage_ref[plane] = store
-        y_ref[plane] = y_face
-        z0_ref[plane] = z0
-        z1_ref[plane] = z1
+        for ref, face in zip(face_refs, faces):
+            ref[plane] = face
         part_ref[plane] = part
         if plane:
             x_face = 2.0 / (before + resist)
@@ -446,21 +448,19 @@
             read,
             field.__setitem__,
             x_ref.__getitem__,
-            y_ref.__getitem__,
-            lambda plane: (z0_ref[plane], z1_ref[plane]),
+            lambda plane: [ref[plane] for ref in face_refs],
             scale_ref.__getitem__,
         )
         read = field.__getitem__
 
 
 def basis_kernel(*refs):
-    before_ref, after_ref, table_ref, resist_ref, storage_ref, x_ref, y_ref, z0_ref, z1_ref = refs[:9]
-    part_ref, scale_ref, rhs_ref = refs[9:12]
-    near_fields = refs[12 : 12 + SWEEPS]
-    refs = refs[12 + SWEEPS :]
-    packed_ref, basis_ref, side_ref, rhs_out_ref, store_out_ref, up_ref, down_ref = refs[:7]
-    scale_far, x_far, y_far, z0_far, z1_far, sums_ref = refs[7:13]
-    far_fields = refs[13:]
+    before_ref, after_ref, table_ref, rhs_ref, resist_ref, storage_ref, x_ref, part_ref, scale_ref = refs[:9]
+    refs = refs[9:]
+    near_faces, near_fields, refs = (refs[:FACES], refs[FACES : FACES + SWEEPS], refs[FACES + SWEEPS :])
+    packed_ref, basis_ref, side_ref, rhs_out_ref, store_out_ref, up_ref, down_ref, sums_ref = refs[:8]
+    scale_far, x_far = refs[8:10]
+    far_faces, far_fields = (refs[10 : 10 + FACES], refs[10 + FACES :])
     tile_x, tile_y, layers = rhs_ref.shape
     rows = resist_ref.shape[1]
     planes = tile_x + 2 * MARGIN
@@ -481,9 +481,9 @@
     def near_or_far(near, far, depth=0):
         return lambda plane: near[plane - MARGIN] if own(plane, depth) else far[plane]
 
-    face_y = near_or_far(y_ref, y_far)
-    face_z0 = near_or_far(z0_ref, z0_far)
-    face_z1 = near_or_far(z1_ref, z1_far)
+    def faces_of(plane):
+        return [near_or_far(near, far)(plane) for near, far in zip(near_faces, far_faces)]
+
     scale = near_or_far(scale_ref, scale_far, 1)
     resist_last, x_last, part_last = (None, None, None)
     for plane in range(planes):
@@ -497,9 +497,9 @@
             resist = code_select(table[:codes], facies)
             if 0 < plane < planes - 1:
                 store = code_select(table[codes:], facies)
-                y_far[plane], z0_far[plane], z1_far[plane], part = plane_faces(
-                    resist, store, face_mask_y
-                )
+                faces, part = plane_faces(resist, store, face_mask_y)
+                for ref, face in zip(far_faces, faces):
+                    ref[plane] = face
         if plane:
             if own(plane - 1) and own(plane):
                 x_face = face_x(plane - 1)
@@ -526,8 +526,7 @@
                 read,
                 far_fields[sweep_id].__setitem__,
                 face_x,
-                face_y,
-                lambda plane: (face_z0(plane), face_z1(plane)),
+                faces_of,
                 scale,
             )
         read = near_or_far(near_fields[sweep_id], far_fields[sweep_id], depth)
@@ -545,12 +544,13 @@
         here_all = read(at)
         here = inner(here_all)
         step_y_all = up(here_all, 0) - here_all
-        flux_y_all = y_ref[plane] * step_y_all
-        flux_y = inner(flux_y_all)
+        y_after, z0_after, z1_after, y_before, z0_before, z1_before = faces_of(at)
+        flux_y = inner(y_after * step_y_all)
+        flux_y_before = inner(y_before * (here_all - down(here_all, 0)))
         step_x = inner(read(at + 1)) - here
         flux_x = inner(face_x(at)) * step_x
         flux_before = inner(face_x(at - 1)) * (here - inner(read(at - 1)))
-        z_face = jnp.maximum(inner(z0_ref[plane]), inner(z1_ref[plane]))
+        z_face = inner(jnp.maximum(z0_after, z1_after))
         above = up(here, 1)
         step_z = above - here
         energy_z = z_face * step_z * step_z
@@ -563,12 +563,12 @@
         z_cut = jnp.where(cut_any, z_face, 0.0)
         basis_ref[plane] = here
         side_ref[plane] = factor * (
-            (flux_before - flux_x) + (inner(down(flux_y_all, 0)) - flux_y)
+            (flux_before - flux_x) + (flux_y_before - flux_y)
         )
         rhs_out_ref[plane] = factor * rhs
         store_out_ref[plane] = factor * store
         up_ref[plane] = factor * z_face
-        down_ref[plane] = factor * down(z_face, 1)
+        down_ref[plane] = factor * inner(jnp.maximum(z0_before, z1_before))
         terms = (
             store * here * here,
             store * here * other,
@@ -701,11 +701,10 @@
     near = pl.pallas_call(
         tile_kernel,
         out_shape=(jax.ShapeDtypeStruct((2 * facies_perm.shape[0], layers), f32),)
-        + (wide,) * 8
         + (tile,)
-        + (wide,) * SWEEPS,
+        + (wide,) * (5 + FACES + SWEEPS),
         in_specs=[vmem, vmem, smem, smem, vmem, vmem, vmem],
-        out_specs=(vmem,) * (10 + SWEEPS),
+        out_specs=(vmem,) * (7 + FACES + SWEEPS),
         compiler_params=params,
         cost_estimate=pl.CostEstimate(flops=3000000, bytes_accessed=1000000, transcendentals=0),
         name="tile",
@@ -721,11 +720,10 @@
     copies, *fields = pl.pallas_call(
         basis_kernel,
         out_shape=(jax.ShapeDtypeStruct((size, layers), f32),) + (tile,) * 6,
-        in_specs=[vmem] * (12 + SWEEPS),
+        in_specs=[vmem] * (9 + FACES + SWEEPS),
         out_specs=(vmem,) * 7,
-        scratch_shapes=[pltpu.VMEM((planes, rows, layers), f32)] * 5
-        + [pltpu.VMEM((8, layers), f32)]
-        + [pltpu.VMEM((planes, rows, layers), f32)] * SWEEPS,
+        scratch_shapes=[pltpu.VMEM((8, layers), f32)]
+        + [pltpu.VMEM((planes, rows, layers), f32)] * (2 + FACES + SWEEPS),
         compiler_params=params,
         name="basis",
     )(before, after, *near)

time: 27.1 us -> 27 us (level)
  Pallas kernels: 2.91 us -> 2.62 us
where the time goes in v8:
time: 27 us; the launch traced here: 26.8 us
  blocking collectives  13.2 us (49%)
  starting transfers between devices  5.09 us (19%)
  waiting for transfers between devices  4.23 us (16%)
  Pallas kernels  2.62 us (10%)
  other arithmetic  0.9 us (3%)
  local copies, waits for them, and re-layouts  0.69 us (3%)
    all_to_all x1, blocking collectives, column_step(): everyone = lax.all_to_all(copies, AXES, 0, 0, tiled=True)  13.2 us
    ppermute x5, starting transfers between devices, swap_along(): return lax.ppermute(value, AXES, pairs)  5.09 us
    ppermute x5, waiting for transfers between devices, swap_along(): return lax.ppermute(value, AXES, pairs)  4.23 us
    pallas_call x1, Pallas kernels, column_step(): pl.pallas_call(tile_kernel, out_shape=(jax.ShapeDtypeStruct((2 * facies_p...  1 us
    pallas_call x1, Pallas kernels, column_step(): pl.pallas_call(pressure_kernel, out_shape=tile, in_specs=[vmem] * 7, out_...  0.89 us
    select_n x3, other arithmetic, end_planes(): return jnp.where(at_first, value[:MARGIN], value[count - MARGIN:])  0.86 us
    pallas_call x1, Pallas kernels, column_step(): pl.pallas_call(basis_kernel, out_shape=(jax.ShapeDtypeStruct((size, layer...  0.74 us
    unnamed x15, local copies, waits for them, and re-layouts  0.69 us
  transfers between devices with their start and end apart: 5, of which 3 were waited for; matrix products, arithmetic and copies ran while one was open for 0% of the time, Pallas kernels for 4%

profile of v8, /device:TPU:0, one launch (start us, length us, event | category | flops | bytes accessed | tf_op | source)
XLA Modules:
  0.0 26.8 jit_solution(5120943444348490007)
XLA Ops:
  0.0 0.0 copy-start.6
  0.0 0.8 %slice_select_fusion.1 = s32[4,16,128]{2,1,0:T(8,128)S(1)} fusion(s32[8,16,128]{2,1,0:T(8,128)} %param.7, pred[]{:T(512)S(6)} %not.4), kind=kLoop, calls=%fused_computation.4 | loop fusion | flops 8192 | bytes 98305 | tf_op jit(solution)/shard_map/jit(_where)/select_n | solution.py:315
  0.8 3.0 %collective-permute-start.3 = (s32[4,16,128]{2,1,0:T(8,128)S(1)}, s32[4,16,128]{2,1,0:T(8,128)S(1)}, u32[]{:S(2)}, u32[]{:S(2)}) collective-permute-start(s32[4,16,128]{2,1,0:T(8,128)S(1)} %slice_select_fusion.1), channel_id=1, source_target_pairs={{0,4},{1,5},{2,6},{3,7},{4,0},{5,1},{6,2},{7,3},{8,12},{9,13},{10,... | collective-permute-start | bytes 98312 | tf_op jit(solution)/shard_map/ppermute | solution.py:307
  3.8 0.0 copy-done.6
  3.8 0.1 collective-permute-start.1
  3.9 1.6 %collective-permute-start = (s32[8,16,128]{2,1,0:T(8,128)S(1)}, s32[8,16,128]{2,1,0:T(8,128)S(1)}, u32[]{:S(2)}, u32[]{:S(2)}) collective-permute-start(s32[8,16,128]{2,1,0:T(8,128)S(1)} %copy-done.6), channel_id=1, source_target_pairs={{0,1},{1,0},{2,3},{3,2},{4,5},{5,4},{6,7},{7,6},{8,9},{9,8},{10,11... | collective-permute-start | bytes 196616 | tf_op jit(solution)/shard_map/ppermute | solution.py:307
  5.4 0.3 collective-permute-done.3
  5.7 2.4 %collective-permute-done.1 = s32[8,16,128]{2,1,0:T(8,128)S(1)} collective-permute-done((s32[8,16,128]{2,1,0:T(8,128)S(1)}, s32[8,16,128]{2,1,0:T(8,128)S(1)}, u32[]{:S(2)}, u32[]{:S(2)}) %collective-permute-start.1) | collective-permute-done | bytes 65568 | tf_op jit(solution)/shard_map/ppermute | solution.py:307
  8.1 0.0 collective-permute-done
  8.1 0.0 copy-start
  8.2 0.4 %collective-permute-start.4 = (s32[4,8,128]{2,1,0:T(8,128)S(1)}, s32[4,8,128]{2,1,0:T(8,128)S(1)}, u32[]{:S(2)}, u32[]{:S(2)}) collective-permute-start(s32[4,8,128]{2,1,0:T(8,128)S(1)} %fusion.1), channel_id=1, source_target_pairs={{0,4},{1,5},{2,6},{3,7},{4,0},{5,1},{6,2},{7,3},{8,12},{9,13},{10,... | collective-permute-start | bytes 49160 | tf_op jit(solution)/shard_map/ppermute | solution.py:307
  8.6 0.0 copy-start.4
  8.6 0.0 copy-start.5
  8.6 0.1 collective-permute-start.2
  8.7 0.0 copy-start.1
  8.7 0.0 copy-start.2
  8.7 0.0 copy-start.3
  8.7 0.3 %copy-done = f32[8,16,128]{2,1,0:T(8,128)S(1)} copy-done((f32[8,16,128]{2,1,0:T(8,128)S(1)}, f32[8,16,128]{2,1,0:T(8,128)}, u32[]{:S(2)}) %copy-start) | copy-done | bytes 65560
  9.0 0.2 copy-done.4
  9.2 0.0 copy-done.5
  9.2 0.1 copy-done.1
  9.3 0.0 copy-done.2
  9.3 0.0 copy-done.3
  9.4 1.0 %tile.1 = (f32[16,128]{1,0:T(8,128)S(1)}, f32[8,16,128]{2,1,0:T(8,128)S(1)}, f32[8,24,128]{2,1,0:T(8,128)S(1)}, f32[8,24,128]{2,1,0:T(8,128)S(1)}, f32[8,24,128]...) custom-call(s32[8,24,128]{2,1,0:T(8,128)S(1)} %pad_add_fusion.rows_r, ...), custom_call_target="tpu_custom_call" | custom-call | flops 3000000 | bytes 1000000 | tf_op jit(solution)/shard_map/tile/pallas_call | solution.py:701
  10.4 1.6 %collective-permute-done.4 = s32[4,8,128]{2,1,0:T(8,128)S(1)} collective-permute-done((s32[4,8,128]{2,1,0:T(8,128)S(1)}, s32[4,8,128]{2,1,0:T(8,128)S(1)}, u32[]{:S(2)}, u32[]{:S(2)}) %collective-permute-start.4) | collective-permute-done | bytes 16416 | tf_op jit(solution)/shard_map/ppermute | solution.py:307
  12.0 0.0 collective-permute-done.2
  12.0 0.7 %basis.1 = (f32[32,128]{1,0:T(8,128)S(1)}, f32[8,16,128]{2,1,0:T(8,128)S(1)}, f32[8,16,128]{2,1,0:T(8,128)S(1)}, f32[8,16,128]{2,1,0:T(8,128)S(1)}, f32[8,16,128...) custom-call(s32[4,24,128]{2,1,0:T(8,128)S(1)} %get-tuple-element.54.refs_0_, ...), custom_call_target="tpu_custom_call" | custom-call | tf_op jit(solution)/shard_map/basis/pallas_call | solution.py:720
  12.7 13.2 %all_to_all.11 = f32[32,1,128]{2,1,0:T(1,128)S(1)} all-to-all(f32[32,1,128]{2,1,0:T(1,128)S(1)} %bitcast.8), channel_id=1, replica_groups=mesh['gx'=8,'gy'=4] {'gx','gy'}, dimensions={0} | all-to-all | bytes 32768 | tf_op jit(solution)/shard_map/all_to_all | solution.py:730
  25.9 0.9 %pressure.1 = f32[8,16,128]{2,1,0:T(8,128)} custom-call(f32[32,128]{1,0:T(8,128)S(1)} %bitcast.7, f32[8,16,128]{2,1,0:T(8,128)S(1)} %get-tuple-element.45.basis_ref, f32[8,16,128]{2,1,0:T(8,128)S(1)} %get-tuple-element.46.side_ref, f32[8,16,128]{2,1,0:T(8,128)S(1)} %get-tuple-element.47.rhs_ref, f32[8,16,128]{2,1,0:T(8,128)S(1)} %get-tuple-element.48.store_ref, ...), custom_call_target="tpu_custom_call" | custom-call | tf_op jit(solution)/shard_map/pressure/pallas_call | solution.py:731
  (7 shorter events, 0.1 us)
Async XLA Ops:
  0.0 3.8 %copy-start.6 = (s32[8,16,128]{2,1,0:T(8,128)S(1)}, s32[8,16,128]{2,1,0:T(8,128)}, u32[]{:S(2)}) copy-start(s32[8,16,128]{2,1,0:T(8,128)} %param.7) | copy-start | bytes 196612
  0.8 4.9 %collective-permute-start.3 = (s32[4,16,128]{2,1,0:T(8,128)S(1)}, s32[4,16,128]{2,1,0:T(8,128)S(1)}, u32[]{:S(2)}, u32[]{:S(2)}) collective-permute-start(s32[4,16,128]{2,1,0:T(8,128)S(1)} %slice_select_fusion.1), channel_id=1, source_target_pairs={{0,4},{1,5},{2,6},{3,7},{4,0},{5,1},{6,2},{7,3},{8,12},{9,13},{10,... | collective-permute-start | bytes 98312 | tf_op jit(solution)/shard_map/ppermute | solution.py:307
  3.8 4.3 %collective-permute-start.1 = (s32[8,16,128]{2,1,0:T(8,128)S(1)}, s32[8,16,128]{2,1,0:T(8,128)S(1)}, u32[]{:S(2)}, u32[]{:S(2)}) collective-permute-start(s32[8,16,128]{2,1,0:T(8,128)S(1)} %copy-done.6), channel_id=1, source_target_pairs={{0,4},{1,2},{2,1},{3,7},{4,0},{5,6},{6,5},{7,3},{8,12},{9,10},{10,... | collective-permute-start | bytes 196616 | tf_op jit(solution)/shard_map/ppermute | solution.py:307
  3.9 4.2 %collective-permute-start = (s32[8,16,128]{2,1,0:T(8,128)S(1)}, s32[8,16,128]{2,1,0:T(8,128)S(1)}, u32[]{:S(2)}, u32[]{:S(2)}) collective-permute-start(s32[8,16,128]{2,1,0:T(8,128)S(1)} %copy-done.6), channel_id=1, source_target_pairs={{0,1},{1,0},{2,3},{3,2},{4,5},{5,4},{6,7},{7,6},{8,9},{9,8},{10,11... | collective-permute-start | bytes 196616 | tf_op jit(solution)/shard_map/ppermute | solution.py:307
  8.1 0.8 %copy-start = (f32[8,16,128]{2,1,0:T(8,128)S(1)}, f32[8,16,128]{2,1,0:T(8,128)}, u32[]{:S(2)}) copy-start(f32[8,16,128]{2,1,0:T(8,128)} %source_ref.1) | copy-start | bytes 196612
  8.2 3.8 %collective-permute-start.4 = (s32[4,8,128]{2,1,0:T(8,128)S(1)}, s32[4,8,128]{2,1,0:T(8,128)S(1)}, u32[]{:S(2)}, u32[]{:S(2)}) collective-permute-start(s32[4,8,128]{2,1,0:T(8,128)S(1)} %fusion.1), channel_id=1, source_target_pairs={{0,4},{1,5},{2,6},{3,7},{4,0},{5,1},{6,2},{7,3},{8,12},{9,13},{10,... | collective-permute-start | bytes 49160 | tf_op jit(solution)/shard_map/ppermute | solution.py:307
  8.6 0.7 %copy-start.4 = (s32[64]{0:T(128)S(1)}, s32[64]{0:T(128)}, u32[]{:S(2)}) copy-start(s32[64]{0:T(128)} %param.12) | copy-start | bytes 772
  8.6 0.7 %copy-start.5 = (f32[64]{0:T(128)S(1)}, f32[64]{0:T(128)}, u32[]{:S(2)}) copy-start(f32[64]{0:T(128)} %param.13) | copy-start | bytes 772
  8.6 3.4 %collective-permute-start.2 = (s32[4,24,128]{2,1,0:T(8,128)S(1)}, s32[4,24,128]{2,1,0:T(8,128)S(1)}, u32[]{:S(2)}, u32[]{:S(2)}) collective-permute-start(s32[4,24,128]{2,1,0:T(8,128)S(1)} %slice_select_fusion), channel_id=1, source_target_pairs={{0,1},{1,0},{2,3},{3,2},{4,8},{5,9},{6,10},{7,11},{8,4},{9,5},{10,... | collective-permute-start | bytes 147464 | tf_op jit(solution)/shard_map/ppermute | solution.py:307
  8.7 0.7 %copy-start.1 = (f32[8]{0:T(128)S(1)}, f32[8]{0:T(128)}, u32[]{:S(2)}) copy-start(f32[8]{0:T(128)} %perm_ref.1) | copy-start | bytes 100
  8.7 0.7 %copy-start.2 = (f32[8]{0:T(128)S(1)}, f32[8]{0:T(128)}, u32[]{:S(2)}) copy-start(f32[8]{0:T(128)} %store_ref.1) | copy-start | bytes 100
  8.7 0.7 %copy-start.3 = (s32[64]{0:T(128)S(1)}, s32[64]{0:T(128)}, u32[]{:S(2)}) copy-start(s32[64]{0:T(128)} %param.11) | copy-start | bytes 772

commit v9 on v8

--- a/solution.py
+++ b/solution.py
@@ -289,42 +289,50 @@
 VMEM_BYTES = 16 * 2**20
 
 
-def swap_along(value, axis, first):
-    sizes = {name_: lax.axis_size(name_) for name_ in AXES}
-    other = AXES[1 - AXES.index(axis)]
+def neighbour(index, size, first):
+    partner = first + ((index - first) ^ 1) if index >= first else -1
+    return partner if 0 <= partner < size else None
+
+
+def swap(value, first_x, first_y):
+    size_x, size_y = (lax.axis_size(axis) for axis in AXES)
     pairs = []
-    for gx in range(sizes[AXES[0]]):
-        for gy in range(sizes[AXES[1]]):
-            place = {AXES[0]: gx, AXES[1]: gy}
-            partner = dict(place)
-            along = first + ((place[axis] - first) ^ 1) if place[axis] >= first else -1
-            if 0 <= along < sizes[axis]:
-                partner[axis] = along
-            else:
-                partner[other] = place[other] ^ 1
-            if partner[other] < sizes[other]:
-                pairs.append(tuple(p[AXES[0]] * sizes[AXES[1]] + p[AXES[1]] for p in (place, partner)))
+    for x in range(size_x):
+        for y in range(size_y):
+            to_x = x if first_x is None else neighbour(x, size_x, first_x)
+            to_y = y if first_y is None else neighbour(y, size_y, first_y)
+            if to_x is None:
+                to_x, to_y = (x, neighbour(y, size_y, 0))
+            elif to_y is None:
+                to_x, to_y = (neighbour(x, size_x, 0), y)
+            if to_x is not None and to_y is not None:
+                pairs.append((x * size_y + y, to_x * size_y + to_y))
     return lax.ppermute(value, AXES, pairs)
 
 
 def wide_tile(facies):
-    count = facies.shape[0]
     even_x, even_y = (lax.axis_index(axis) % 2 == 0 for axis in AXES)
 
-    def end_planes(value, at_first):
-        return jnp.where(at_first, value[:MARGIN], value[count - MARGIN :])
-
-    far = swap_along(facies, "gy", 1)
-    near = swap_along(facies, "gy", 0)
-    beside = swap_along(end_planes(facies, ~even_x), "gx", 0)
-    before = jnp.where(even_y, far[:, -MARGIN:], near[:, -MARGIN:])
-    after = jnp.where(even_y, near[:, :MARGIN], far[:, :MARGIN])
-    rest = jnp.concatenate([after, before], axis=1)
-    own = jnp.concatenate([facies, rest], axis=1)
-    far = swap_along(end_planes(own, even_x), "gx", 1)
-    corners = swap_along(end_planes(rest, ~even_x), "gx", 0)
-    near = jnp.concatenate([beside, corners], axis=1)
-    return own, jnp.where(even_x, far, near), jnp.where(even_x, near, far)
+    def planes(value, at_first):
+        return jnp.where(at_first, value[:MARGIN], value[-MARGIN:])
+
+    def rows(value, at_first):
+        return jnp.where(at_first, value[:, :MARGIN], value[:, -MARGIN:])
+
+    def sides(far, near):
+        return jnp.concatenate([jnp.where(even_y, near, far), jnp.where(even_y, far, near)], axis=1)
+
+    near_end = planes(facies, ~even_x)
+    far_y = swap(facies, None, 1)
+    near_y = swap(facies, None, 0)
+    near_x = swap(near_end, 0, None)
+    own = jnp.concatenate([facies, sides(rows(far_y, ~even_y), rows(near_y, even_y))], axis=1)
+    far_x = swap(planes(own, even_x), 1, None)
+    beside = (rows(near_x, even_y), rows(near_x, ~even_y))
+    corner_far = swap(beside[0], None, 1)
+    corner_near = swap(beside[1], None, 0)
+    near_x = jnp.concatenate([near_x, sides(corner_far, corner_near)], axis=1)
+    return own, jnp.where(even_x, far_x, near_x), jnp.where(even_x, near_x, far_x)
 
 
 def lane_iota(shape):
@@ -419,6 +427,7 @@
         lax.broadcasted_iota(jnp.int32, (tile_y, well_y_ref.shape[1]), 0) + anchor_y
         == well_y_ref[...]
     )
+    ones = jnp.ones((well_rate_ref.shape[1], layers), jnp.float32)
     before, x_before, part_before = (None, None, None)
     for plane in range(tile_x):
         resist = code_select(resists, rows_ref[plane])
@@ -437,7 +446,8 @@
             x_before = x_face
         before, part_before = (resist, part)
         hit = hit_y & (well_x_ref[...] == anchor_x + plane)
-        column = jnp.sum(jnp.where(hit, well_rate_ref[...], 0.0), axis=1, keepdims=True)
+        rates = jnp.where(hit, well_rate_ref[...], 0.0)
+        column = jnp.dot(rates, ones, precision=HIGHEST, preferred_element_type=jnp.float32)
         rhs_ref[plane] = source_ref[plane] + column / layers
     start = start_field((rows, layers))
     read = lambda plane: start

time: 27 us -> 26.4 us (0.978)
  waiting for transfers between devices: 4.23 us -> 1.61 us
  starting transfers between devices: 5.09 us -> 6.9 us
    ppermute x5 -> x6, waiting for transfers between devices: 4.23 us -> 1.61 us  [swap(): return lax.ppermute(value, AXES, pairs)]
    ppermute x5 -> x6, starting transfers between devices: 5.09 us -> 6.9 us  [swap(): return lax.ppermute(value, AXES, pairs)]
    select_n x5 -> x6, other arithmetic: 0.88 us -> 0.88 us  [the longest x2 0.84 us: planes(): return jnp.where(at_first, value[:MARGIN], value[-MARGIN:])]
    unnamed x15 -> x14, local copies, waits for them, and re-layouts: 0.69 us -> 0.69 us
  transfers between devices with their start and end apart: 5 -> 6, of which waited for: 3 -> 3; matrix products, arithmetic and copies ran while one was open for 0% -> 0% of each run, Pallas kernels for 4% -> 4%
where the time goes in v9:
time: 26.4 us; the launch traced here: 26.2 us
  blocking collectives  13.4 us (51%)
  starting transfers between devices  6.9 us (26%)
  Pallas kernels  2.58 us (10%)
  waiting for transfers between devices  1.61 us (6%)
  other arithmetic  0.9 us (3%)
  local copies, waits for them, and re-layouts  0.69 us (3%)
    all_to_all x1, blocking collectives, column_step(): everyone = lax.all_to_all(copies, AXES, 0, 0, tiled=True)  13.4 us
    ppermute x6, starting transfers between devices, swap(): return lax.ppermute(value, AXES, pairs)  6.9 us
    ppermute x6, waiting for transfers between devices, swap(): return lax.ppermute(value, AXES, pairs)  1.61 us
    pallas_call x1, Pallas kernels, column_step(): pl.pallas_call(tile_kernel, out_shape=(jax.ShapeDtypeStruct((2 * facies_p...  0.96 us
    pallas_call x1, Pallas kernels, column_step(): pl.pallas_call(pressure_kernel, out_shape=tile, in_specs=[vmem] * 7, out_...  0.89 us
    select_n x2, other arithmetic, planes(): return jnp.where(at_first, value[:MARGIN], value[-MARGIN:])  0.84 us
    pallas_call x1, Pallas kernels, column_step(): pl.pallas_call(basis_kernel, out_shape=(jax.ShapeDtypeStruct((size, layer...  0.74 us
    unnamed x14, local copies, waits for them, and re-layouts  0.69 us
  transfers between devices with their start and end apart: 6, of which 3 were waited for; matrix products, arithmetic and copies ran while one was open for 0% of the time, Pallas kernels for 4%

profile of v9, /device:TPU:0, one launch (start us, length us, event | category | flops | bytes accessed | tf_op | source)
XLA Modules:
  0.0 26.2 jit_solution(11619688604561198591)
XLA Ops:
  0.0 0.0 copy-start.6
  0.0 0.8 %slice_select_fusion.1 = s32[4,16,128]{2,1,0:T(8,128)S(1)} fusion(s32[8,16,128]{2,1,0:T(8,128)} %param.7, pred[]{:T(512)S(6)} %not.8), kind=kLoop, calls=%fused_computation.5 | loop fusion | flops 8192 | bytes 98305 | tf_op jit(solution)/shard_map/jit(_where)/select_n | solution.py:317
  0.8 3.0 %collective-permute-start.3 = (s32[4,16,128]{2,1,0:T(8,128)S(1)}, s32[4,16,128]{2,1,0:T(8,128)S(1)}, u32[]{:S(2)}, u32[]{:S(2)}) collective-permute-start(s32[4,16,128]{2,1,0:T(8,128)S(1)} %slice_select_fusion.1), channel_id=1, source_target_pairs={{0,4},{1,5},{2,6},{3,7},{4,0},{5,1},{6,2},{7,3},{8,12},{9,13},{10,... | collective-permute-start | bytes 98312 | tf_op jit(solution)/shard_map/ppermute | solution.py:310
  3.8 0.0 copy-done.6
  3.8 0.1 collective-permute-start.1
  3.9 1.6 %collective-permute-start = (s32[8,16,128]{2,1,0:T(8,128)S(1)}, s32[8,16,128]{2,1,0:T(8,128)S(1)}, u32[]{:S(2)}, u32[]{:S(2)}) collective-permute-start(s32[8,16,128]{2,1,0:T(8,128)S(1)} %copy-done.6), channel_id=1, source_target_pairs={{0,1},{1,0},{2,3},{3,2},{4,5},{5,4},{6,7},{7,6},{8,9},{9,8},{10,11... | collective-permute-start | bytes 196616 | tf_op jit(solution)/shard_map/ppermute | solution.py:310
  5.4 0.3 collective-permute-done.3
  5.7 0.0 collective-permute-start.4
  5.7 2.1 %collective-permute-start.5 = (s32[4,4,128]{2,1,0:T(4,128)S(1)}, s32[4,4,128]{2,1,0:T(4,128)S(1)}, u32[]{:S(2)}, u32[]{:S(2)}) collective-permute-start(s32[4,4,128]{2,1,0:T(4,128)S(1)} %get-tuple-element.56), channel_id=1, source_target_pairs={{0,4},{1,2},{2,1},{3,7},{4,0},{5,6},{6,5},{7,3},{8,12},{9,10},{10,... | collective-permute-start | bytes 24584 | tf_op jit(solution)/shard_map/ppermute | solution.py:310
  7.8 0.3 %collective-permute-done.1 = s32[8,16,128]{2,1,0:T(8,128)S(1)} collective-permute-done((s32[8,16,128]{2,1,0:T(8,128)S(1)}, s32[8,16,128]{2,1,0:T(8,128)S(1)}, u32[]{:S(2)}, u32[]{:S(2)}) %collective-permute-start.1) | collective-permute-done | bytes 65568 | tf_op jit(solution)/shard_map/ppermute | solution.py:310
  8.1 0.0 collective-permute-done
  8.1 0.0 copy-start
  8.1 0.2 collective-permute-start.2
  8.4 0.0 collective-permute-done.4
  8.4 1.1 %collective-permute-done.5 = s32[4,4,128]{2,1,0:T(4,128)S(1)} collective-permute-done((s32[4,4,128]{2,1,0:T(4,128)S(1)}, s32[4,4,128]{2,1,0:T(4,128)S(1)}, u32[]{:S(2)}, u32[]{:S(2)}) %collective-permute-start.5) | collective-permute-done | bytes 8224 | tf_op jit(solution)/shard_map/ppermute | solution.py:310
  9.4 0.0 copy-start.4
  9.4 0.0 copy-start.5
  9.4 0.0 copy-start.1
  9.5 0.0 copy-start.2
  9.5 0.0 copy-start.3
  9.5 0.0 copy-done
  9.5 0.6 %copy-done.4 = s32[64]{0:T(128)S(1)} copy-done((s32[64]{0:T(128)S(1)}, s32[64]{0:T(128)}, u32[]{:S(2)}) %copy-start.4) | copy-done | bytes 280
  10.1 0.0 copy-done.5
  10.1 0.0 copy-done.1
  10.1 0.0 copy-done.2
  10.1 0.0 copy-done.3
  10.2 1.0 %tile.1 = (f32[16,128]{1,0:T(8,128)S(1)}, f32[8,16,128]{2,1,0:T(8,128)S(1)}, f32[8,24,128]{2,1,0:T(8,128)S(1)}, f32[8,24,128]{2,1,0:T(8,128)S(1)}, f32[8,24,128]...) custom-call(s32[8,24,128]{2,1,0:T(8,128)S(1)} %pad_add_fusion.rows_r, ...), custom_call_target="tpu_custom_call" | custom-call | flops 3000000 | bytes 1000000 | tf_op jit(solution)/shard_map/tile/pallas_call | solution.py:711
  11.1 0.0 collective-permute-done.2
  11.1 0.7 %basis.1 = (f32[32,128]{1,0:T(8,128)S(1)}, f32[8,16,128]{2,1,0:T(8,128)S(1)}, f32[8,16,128]{2,1,0:T(8,128)S(1)}, f32[8,16,128]{2,1,0:T(8,128)S(1)}, f32[8,16,128...) custom-call(s32[4,24,128]{2,1,0:T(8,128)S(1)} %get-tuple-element.54.refs_0_, ...), custom_call_target="tpu_custom_call" | custom-call | tf_op jit(solution)/shard_map/basis/pallas_call | solution.py:730
  11.9 13.4 %all_to_all.11 = f32[32,1,128]{2,1,0:T(1,128)S(1)} all-to-all(f32[32,1,128]{2,1,0:T(1,128)S(1)} %bitcast.12), channel_id=1, replica_groups=mesh['gx'=8,'gy'=4] {'gx','gy'}, dimensions={0} | all-to-all | bytes 32768 | tf_op jit(solution)/shard_map/all_to_all | solution.py:740
  25.3 0.9 %pressure.1 = f32[8,16,128]{2,1,0:T(8,128)} custom-call(f32[32,128]{1,0:T(8,128)S(1)} %bitcast.11, f32[8,16,128]{2,1,0:T(8,128)S(1)} %get-tuple-element.45.basis_ref, f32[8,16,128]{2,1,0:T(8,128)S(1)} %get-tuple-element.46.side_ref, f32[8,16,128]{2,1,0:T(8,128)S(1)} %get-tuple-element.47.rhs_ref, f32[8,16,128]{2,1,0:T(8,128)S(1)} %get-tuple-element.48.store_ref, ...), custom_call_target="tpu_custom_call" | custom-call | tf_op jit(solution)/shard_map/pressure/pallas_call | solution.py:741
  (6 shorter events, 0.1 us)
Async XLA Ops:
  0.0 3.8 %copy-start.6 = (s32[8,16,128]{2,1,0:T(8,128)S(1)}, s32[8,16,128]{2,1,0:T(8,128)}, u32[]{:S(2)}) copy-start(s32[8,16,128]{2,1,0:T(8,128)} %param.7) | copy-start | bytes 196612
  0.8 4.9 %collective-permute-start.3 = (s32[4,16,128]{2,1,0:T(8,128)S(1)}, s32[4,16,128]{2,1,0:T(8,128)S(1)}, u32[]{:S(2)}, u32[]{:S(2)}) collective-permute-start(s32[4,16,128]{2,1,0:T(8,128)S(1)} %slice_select_fusion.1), channel_id=1, source_target_pairs={{0,4},{1,5},{2,6},{3,7},{4,0},{5,1},{6,2},{7,3},{8,12},{9,13},{10,... | collective-permute-start | bytes 98312 | tf_op jit(solution)/shard_map/ppermute | solution.py:310
  3.8 4.3 %collective-permute-start.1 = (s32[8,16,128]{2,1,0:T(8,128)S(1)}, s32[8,16,128]{2,1,0:T(8,128)S(1)}, u32[]{:S(2)}, u32[]{:S(2)}) collective-permute-start(s32[8,16,128]{2,1,0:T(8,128)S(1)} %copy-done.6), channel_id=1, source_target_pairs={{0,4},{1,2},{2,1},{3,7},{4,0},{5,6},{6,5},{7,3},{8,12},{9,10},{10,... | collective-permute-start | bytes 196616 | tf_op jit(solution)/shard_map/ppermute | solution.py:310
  3.9 4.2 %collective-permute-start = (s32[8,16,128]{2,1,0:T(8,128)S(1)}, s32[8,16,128]{2,1,0:T(8,128)S(1)}, u32[]{:S(2)}, u32[]{:S(2)}) collective-permute-start(s32[8,16,128]{2,1,0:T(8,128)S(1)} %copy-done.6), channel_id=1, source_target_pairs={{0,1},{1,0},{2,3},{3,2},{4,5},{5,4},{6,7},{7,6},{8,9},{9,8},{10,11... | collective-permute-start | bytes 196616 | tf_op jit(solution)/shard_map/ppermute | solution.py:310
  5.7 2.7 %collective-permute-start.4 = (s32[4,4,128]{2,1,0:T(4,128)S(1)}, s32[4,4,128]{2,1,0:T(4,128)S(1)}, u32[]{:S(2)}, u32[]{:S(2)}) collective-permute-start(s32[4,4,128]{2,1,0:T(4,128)S(1)} %get-tuple-element.55), channel_id=1, source_target_pairs={{0,1},{1,0},{2,3},{3,2},{4,5},{5,4},{6,7},{7,6},{8,9},{9,8},{10,11... | collective-permute-start | bytes 24584 | tf_op jit(solution)/shard_map/ppermute | solution.py:310
  5.7 3.7 %collective-permute-start.5 = (s32[4,4,128]{2,1,0:T(4,128)S(1)}, s32[4,4,128]{2,1,0:T(4,128)S(1)}, u32[]{:S(2)}, u32[]{:S(2)}) collective-permute-start(s32[4,4,128]{2,1,0:T(4,128)S(1)} %get-tuple-element.56), channel_id=1, source_target_pairs={{0,4},{1,2},{2,1},{3,7},{4,0},{5,6},{6,5},{7,3},{8,12},{9,10},{10,... | collective-permute-start | bytes 24584 | tf_op jit(solution)/shard_map/ppermute | solution.py:310
  8.1 1.4 %copy-start = (f32[8,16,128]{2,1,0:T(8,128)S(1)}, f32[8,16,128]{2,1,0:T(8,128)}, u32[]{:S(2)}) copy-start(f32[8,16,128]{2,1,0:T(8,128)} %source_ref.1) | copy-start | bytes 196612
  8.1 3.0 %collective-permute-start.2 = (s32[4,24,128]{2,1,0:T(8,128)S(1)}, s32[4,24,128]{2,1,0:T(8,128)S(1)}, u32[]{:S(2)}, u32[]{:S(2)}) collective-permute-start(s32[4,24,128]{2,1,0:T(8,128)S(1)} %slice_select_fusion), channel_id=1, source_target_pairs={{0,1},{1,0},{2,3},{3,2},{4,8},{5,9},{6,10},{7,11},{8,4},{9,5},{10,... | collective-permute-start | bytes 147464 | tf_op jit(solution)/shard_map/ppermute | solution.py:310
  9.4 0.7 %copy-start.4 = (s32[64]{0:T(128)S(1)}, s32[64]{0:T(128)}, u32[]{:S(2)}) copy-start(s32[64]{0:T(128)} %param.12) | copy-start | bytes 772
  9.4 0.7 %copy-start.5 = (f32[64]{0:T(128)S(1)}, f32[64]{0:T(128)}, u32[]{:S(2)}) copy-start(f32[64]{0:T(128)} %param.13) | copy-start | bytes 772
  9.4 0.7 %copy-start.1 = (f32[8]{0:T(128)S(1)}, f32[8]{0:T(128)}, u32[]{:S(2)}) copy-start(f32[8]{0:T(128)} %perm_ref.1) | copy-start | bytes 100
  9.5 0.7 %copy-start.2 = (f32[8]{0:T(128)S(1)}, f32[8]{0:T(128)}, u32[]{:S(2)}) copy-start(f32[8]{0:T(128)} %store_ref.1) | copy-start | bytes 100
  9.5 0.7 %copy-start.3 = (s32[64]{0:T(128)S(1)}, s32[64]{0:T(128)}, u32[]{:S(2)}) copy-start(s32[64]{0:T(128)} %param.11) | copy-start | bytes 772
